TPU v7x, 32 devices: a whole 2x2x4 slice. The times are simulated.
32 devices in a mesh: dp: 16 (over z, y, x), tensor: 2 (over core).
Axes of the slice: x: 2, y: 2, z: 4, core: 2. Of those that a mesh axis runs over, the one named last changes fastest.
Arguments:
- tokens: bfloat16 [8192, 1536], P('dp'), may hold values from -6 to 6
- cotangent: bfloat16 [48, 256, 1536], P('dp'), may hold values from -6 to 6
- lengths: int32 [16, 3], replicated, may hold values from 1 to 256, 512 in all within a row
- dealing: int32 [48], replicated, may hold values from 0 to 47, as said below
- attn_gain: float32 [1536], replicated, may hold values from 0.1 to 1.9
- w_query: bfloat16 [1536, 1536], P(None, 'tensor'), may hold values from -0.15625 to 0.15625
- w_key: bfloat16 [1536, 1536], P(None, 'tensor'), may hold values from -0.15625 to 0.15625
- w_value: bfloat16 [1536, 1536], P(None, 'tensor'), may hold values from -0.15625 to 0.15625
- w_house: bfloat16 [1536, 1536], P(None, 'tensor'), may hold values from -0.15625 to 0.15625
- w_beta: bfloat16 [1536, 12], P(None, 'tensor'), may hold values from -0.15625 to 0.15625
- conv_taps: float32 [4, 1536], P(None, 'tensor'), may hold values from -4 to 4
- w_out: bfloat16 [1536, 1536], P('tensor'), may hold values from -0.625 to 0.625
- ffn_gain: float32 [1536], replicated, may hold values from 0.1 to 1.9
- w_gate: bfloat16 [1536, 4096], P(None, 'tensor'), may hold values from -0.15625 to 0.15625
- w_up: bfloat16 [1536, 4096], P(None, 'tensor'), may hold values from -0.15625 to 0.15625
- w_down: bfloat16 [4096, 1536], P('tensor'), may hold values from -0.09375 to 0.09375
Outputs:
- output: bfloat16 [48, 256, 1536], P('dp')
- input_grad: bfloat16 [8192, 1536], P('dp')
- attn_gain_grad: float32 [1536], P('dp')
- query_grad: float32 [1536, 1536], P('dp', 'tensor')
- key_grad: float32 [1536, 1536], P('dp', 'tensor')
- value_grad: float32 [1536, 1536], P('dp', 'tensor')
- house_grad: float32 [1536, 1536], P('dp', 'tensor')
- beta_grad: float32 [1536, 12], P('dp', 'tensor')
- taps_grad: float32 [4, 1536], P(None, 'tensor')
- out_grad: float32 [1536, 1536], P('tensor', 'dp')
- ffn_gain_grad: float32 [1536], P('dp')
- gate_grad: float32 [1536, 4096], P('dp', 'tensor')
- up_grad: float32 [1536, 4096], P('dp', 'tensor')
- down_grad: float32 [4096, 1536], P('tensor', 'dp')
Inputs may be any that keep to these rules, and one draw needn't show every extreme that they name: Each row of lengths sums to exactly 512, and its largest entry is exactly 256. dealing is a permutation of the sequences; dealing[d * 3 + k] is the sequence in slot k of index d of dp. Each index d takes one sequence of group d + 1 if that exists, one of group d - 1 if that exists, and the rest of its own group d.
All inputs are finite; a program needn't handle non-finite values.
Results may differ from a plain program's by a relative error of at most 0.012.
The roundings to bfloat16 on the way count: a program that leaves them out, or rounds other values in their place, can miss the bound.
Values may be sent and summed in bfloat16 or wider, within the bound.
No kernel may reach another device: no remote copies, remote signals or barrier semaphores. Data moves between devices by JAX's collectives and lax.ppermute only.
A program may use at most 320 MiB of HBM per device.

v0:
```python
import jax
import jax.numpy as jnp
from jax import lax
from jax.sharding import PartitionSpec as P

EPSILON = 1e-06
HIGHEST = lax.Precision.HIGHEST


def with_halo(block, sides, width):
    for axis, dim in sides:
        count = lax.axis_size(axis)
        forward = [(i, i + 1) for i in range(count - 1)]
        backward = [(target, source) for source, target in forward]
        low = lax.ppermute(
            lax.slice_in_dim(block, block.shape[dim] - width, None, axis=dim), axis, forward
        )
        high = lax.ppermute(lax.slice_in_dim(block, 0, width, axis=dim), axis, backward)
        block = jnp.concatenate([low, block, high], axis=dim)
    return block


def from_behind(x, axis, by):
    devices = lax.axis_size(axis)
    pairs = [(i, i + by) for i in range(devices) if 0 <= i + by < devices]
    return lax.ppermute(x, axis, pairs)


def pair_product(form, left, right):
    return jnp.einsum(form, left, right, precision=HIGHEST)


def rounded(source):
    lowered = lax.optimization_barrier(source.astype(jnp.bfloat16)).astype(jnp.float32)
    return source + lax.stop_gradient(lowered - source)


def contract_rows(first_op, second_op):
    return lax.dot_general(
        first_op, second_op, (((0,), (0,)), ((), ())), preferred_element_type=jnp.float32
    )


def contract_cols(first_op, second_op):
    return lax.dot_general(
        first_op, second_op, (((1,), (1,)), ((), ())), preferred_element_type=jnp.float32
    )


def norm_back(d_normed, source, inverse, gain_vec):
    scaled = d_normed * gain_vec
    return inverse * scaled - source * (inverse * inverse * inverse) * jnp.mean(
        scaled * source, axis=1, keepdims=True
    )


def path_mixer(queries, keys_in, values_in, house_in, beta_logit, conv_taps):
    slot_count, length, channels = queries.shape
    head_count = beta_logit.shape[2]
    conv_out = conv_taps[0] * house_in
    for shift_by in range(1, conv_taps.shape[0]):
        shifted = jnp.pad(house_in, ((0, 0), (shift_by, 0), (0, 0)))[:, :length]
        conv_out = conv_out + conv_taps[shift_by] * shifted

    def heads_first(tensor_in):
        return tensor_in.reshape(slot_count, length, head_count, -1).transpose(0, 2, 1, 3)

    query_heads = heads_first(queries)
    key_heads = heads_first(keys_in)
    value_heads = heads_first(values_in)
    conv_heads = heads_first(conv_out)
    scaling = query_heads.shape[-1] ** (-0.5)
    house_dir = rounded(
        conv_heads * lax.rsqrt(jnp.sum(conv_heads * conv_heads, axis=-1, keepdims=True) + EPSILON)
    )
    beta_gate = 2.0 * jax.nn.sigmoid(beta_logit.transpose(0, 2, 1))
    row_index = jnp.arange(length)[:, None]
    col_index = jnp.arange(length)[None, :]
    lower_incl = col_index <= row_index
    strict = col_index < row_index
    gram_matrix = pair_product("bhsd,bhrd->bhsr", house_dir, house_dir)
    coupling = jnp.where(strict, gram_matrix * beta_gate[:, :, None, :], 0.0)
    query_house = jnp.where(
        lower_incl, pair_product("bhid,bhsd->bhis", query_heads, house_dir), 0.0
    )
    house_key = jnp.where(strict, pair_product("bhrd,bhjd->bhrj", house_dir, key_heads), 0.0)
    identity = jnp.eye(length, dtype=jnp.float32)
    solved = lax.linalg.triangular_solve(identity + coupling, house_key, left_side=True, lower=True)
    scores = pair_product("bhid,bhjd->bhij", query_heads, key_heads)
    scores = scores - jnp.einsum(
        "bhis,bhsj->bhij", query_house * beta_gate[:, :, None, :], solved, precision=HIGHEST
    )
    scores = jnp.where(lower_incl, scores * scaling, -1e30)
    row_max = jnp.max(scores, axis=-1, keepdims=True)
    raw_weights = jnp.exp(scores - row_max)
    weights = rounded(raw_weights / jnp.sum(raw_weights, axis=-1, keepdims=True))
    mixed = pair_product("bhij,bhjd->bhid", weights, value_heads)
    return mixed.transpose(0, 2, 1, 3).reshape(slot_count, length, channels)


def on_device(
    tokens,
    cotangent,
    lengths,
    dealing,
    attn_gain,
    w_query,
    w_key,
    w_value,
    w_house,
    w_beta,
    conv_taps,
    w_out,
    ffn_gain,
    w_gate,
    w_up,
    w_down,
):
    tok_rows, width = tokens.shape
    slot_count = cotangent.shape[0]
    seq_span = cotangent.shape[1]
    device = lax.axis_index("dp")
    window = with_halo(tokens, (("dp", 0),), tok_rows)
    seq_ends = jnp.cumsum(lengths, axis=1, dtype=jnp.int32)
    starts = (seq_ends - lengths).reshape(-1)
    taken_ids = lax.dynamic_slice_in_dim(dealing, device * slot_count, slot_count)
    seq_sizes = lengths.reshape(-1)[taken_ids]
    anchor = (taken_ids // slot_count - device + 1) * tok_rows + starts[taken_ids]
    places = jnp.arange(seq_span, dtype=jnp.int32)
    live_mask = places[None, :] < seq_sizes[:, None]
    flat_index = jnp.where(live_mask, anchor[:, None] + places[None, :], 3 * tok_rows).reshape(-1)
    live_rows = live_mask.reshape(-1, 1)
    row_data = jnp.take(window, flat_index, axis=0, mode="fill", fill_value=0).astype(jnp.float32)
    grad_rows = jnp.where(live_rows, cotangent.reshape(-1, width), 0)

    def as_slots(matrix):
        return matrix.reshape(slot_count, seq_span, -1)

    inverse1 = lax.rsqrt(jnp.mean(row_data * row_data, axis=1, keepdims=True) + EPSILON)
    normed1 = (row_data * inverse1 * attn_gain).astype(jnp.bfloat16)
    query_b = jnp.dot(normed1, w_query, preferred_element_type=jnp.float32).astype(jnp.bfloat16)
    key_b = jnp.dot(normed1, w_key, preferred_element_type=jnp.float32).astype(jnp.bfloat16)
    value_b = jnp.dot(normed1, w_value, preferred_element_type=jnp.float32).astype(jnp.bfloat16)
    house_val = jnp.dot(normed1, w_house, preferred_element_type=jnp.float32)
    logit_val = jnp.dot(normed1, w_beta, preferred_element_type=jnp.float32)
    mixer_in = (
        as_slots(query_b).astype(jnp.float32),
        as_slots(key_b).astype(jnp.float32),
        as_slots(value_b).astype(jnp.float32),
        as_slots(house_val),
        as_slots(logit_val),
        conv_taps,
    )
    mixed_slots = path_mixer(*mixer_in)
    mixed_b = mixed_slots.reshape(-1, mixed_slots.shape[2]).astype(jnp.bfloat16)
    attn_part = jnp.dot(mixed_b, w_out, preferred_element_type=jnp.float32)
    hidden = row_data + lax.psum(attn_part, "tensor")
    inverse2 = lax.rsqrt(jnp.mean(hidden * hidden, axis=1, keepdims=True) + EPSILON)
    normed2 = (hidden * inverse2 * ffn_gain).astype(jnp.bfloat16)
    gate_val = jnp.dot(normed2, w_gate, preferred_element_type=jnp.float32)
    up_val = jnp.dot(normed2, w_up, preferred_element_type=jnp.float32)
    gate_sig = jax.nn.sigmoid(gate_val)
    gate_silu = gate_val * gate_sig
    inner_act = (gate_silu * up_val).astype(jnp.bfloat16)
    down_part = jnp.dot(inner_act, w_down, preferred_element_type=jnp.float32)
    final = hidden + lax.psum(down_part.astype(jnp.bfloat16), "tensor").astype(jnp.float32)
    output = (
        jnp.where(live_rows, final, 0.0).astype(jnp.bfloat16).reshape(slot_count, seq_span, width)
    )
    d_inner = contract_cols(grad_rows, w_down)
    d_gate = (d_inner * up_val * gate_sig * (1.0 + gate_val * (1.0 - gate_sig))).astype(
        jnp.bfloat16
    )
    d_up = (d_inner * gate_silu).astype(jnp.bfloat16)
    d_norm2_part = contract_cols(d_gate, w_gate) + contract_cols(d_up, w_up)
    g_gate = contract_rows(normed2, d_gate)
    g_up = contract_rows(normed2, d_up)
    g_down = contract_rows(inner_act, grad_rows)
    d_norm2 = lax.psum(d_norm2_part, "tensor")
    g_ffn_gain = jnp.sum(d_norm2 * hidden * inverse2, axis=0)
    d_hidden = grad_rows.astype(jnp.float32) + norm_back(d_norm2, hidden, inverse2, ffn_gain)
    ffn_parts = (
        lax.psum_scatter(g_ffn_gain, "dp", scatter_dimension=0, tiled=True),
        lax.psum_scatter(g_gate, "dp", scatter_dimension=0, tiled=True),
        lax.psum_scatter(g_up, "dp", scatter_dimension=0, tiled=True),
        lax.psum_scatter(g_down, "dp", scatter_dimension=1, tiled=True),
    )
    d_branch = d_hidden.astype(jnp.bfloat16)
    d_mixed = contract_cols(d_branch, w_out)
    g_out = contract_rows(mixed_b, d_branch)
    mixer_grads = jax.vjp(path_mixer, *mixer_in)[1](as_slots(d_mixed))
    d_query = mixer_grads[0].reshape(-1, w_query.shape[1]).astype(jnp.bfloat16)
    d_key = mixer_grads[1].reshape(-1, w_key.shape[1]).astype(jnp.bfloat16)
    d_value = mixer_grads[2].reshape(-1, w_value.shape[1]).astype(jnp.bfloat16)
    d_house = mixer_grads[3].reshape(-1, w_house.shape[1]).astype(jnp.bfloat16)
    d_logit = mixer_grads[4].reshape(-1, w_beta.shape[1]).astype(jnp.bfloat16)
    g_taps = mixer_grads[5]
    d_norm1_part = (
        contract_cols(d_query, w_query)
        + contract_cols(d_key, w_key)
        + contract_cols(d_value, w_value)
        + contract_cols(d_house, w_house)
        + contract_cols(d_logit, w_beta)
    )
    g_query = contract_rows(normed1, d_query)
    g_key = contract_rows(normed1, d_key)
    g_value = contract_rows(normed1, d_value)
    g_house = contract_rows(normed1, d_house)
    g_beta = contract_rows(normed1, d_logit)
    d_norm1 = lax.psum(d_norm1_part, "tensor")
    g_attn_gain = jnp.sum(d_norm1 * row_data * inverse1, axis=0)
    d_rows = d_hidden + norm_back(d_norm1, row_data, inverse1, attn_gain)
    taps_total = lax.psum(g_taps, "dp")
    back_rows = (
        jnp.zeros((3 * tok_rows, width), jnp.bfloat16)
        .at[flat_index]
        .set(d_rows.astype(jnp.bfloat16), mode="drop")
    )
    from_upper = from_behind(back_rows[:tok_rows], "dp", -1)
    from_lower = from_behind(back_rows[2 * tok_rows :], "dp", 1)
    input_grad = back_rows[tok_rows : 2 * tok_rows] + from_upper + from_lower
    attn_parts = (
        lax.psum_scatter(g_attn_gain, "dp", scatter_dimension=0, tiled=True),
        lax.psum_scatter(g_query, "dp", scatter_dimension=0, tiled=True),
        lax.psum_scatter(g_key, "dp", scatter_dimension=0, tiled=True),
        lax.psum_scatter(g_value, "dp", scatter_dimension=0, tiled=True),
        lax.psum_scatter(g_house, "dp", scatter_dimension=0, tiled=True),
        lax.psum_scatter(g_beta, "dp", scatter_dimension=0, tiled=True),
        lax.psum_scatter(g_out, "dp", scatter_dimension=1, tiled=True),
    )
    every = attn_parts + ffn_parts
    return (
        output,
        input_grad,
        every[0],
        every[1],
        every[2],
        every[3],
        every[4],
        every[5],
        taps_total,
        every[6],
        every[7],
        every[8],
        every[9],
        every[10],
    )


def solution(mesh):
    in_specs = (
        P("dp", None),
        P("dp", None, None),
        P(),
        P(),
        P(),
        P(None, "tensor"),
        P(None, "tensor"),
        P(None, "tensor"),
        P(None, "tensor"),
        P(None, "tensor"),
        P(None, "tensor"),
        P("tensor", None),
        P(),
        P(None, "tensor"),
        P(None, "tensor"),
        P("tensor", None),
    )
    out_specs = (
        P("dp", None, None),
        P("dp", None),
        P("dp"),
        P("dp", "tensor"),
        P("dp", "tensor"),
        P("dp", "tensor"),
        P("dp", "tensor"),
        P("dp", "tensor"),
        P(None, "tensor"),
        P("tensor", "dp"),
        P("dp"),
        P("dp", "tensor"),
        P("dp", "tensor"),
        P("tensor", "dp"),
    )
    return jax.shard_map(
        on_device, mesh=mesh, in_specs=in_specs, out_specs=out_specs, check_vma=False
    )
```

profile of v0, /device:TPU:0, one launch (start us, length us, event | category | flops | bytes accessed | tf_op | source)
XLA Modules:
  0.0 2435.1 jit_solution(5778942652675962632)
XLA Ops:
  7.2 6.1 collective-permute-start
  23.6 56.3 %collective-permute-done = bf16[512,1536]{1,0:T(8,128)(2,1)} collective-permute-done((bf16[512,1536]{1,0:T(8,128)(2,1)}, bf16[512,1536]{1,0:T(8,128)(2,1)}, u32[]{:S(2)}, u32[]{:S(2)}) %collective-permute-start) | collective-permute-done | bytes 1572896 | tf_op jit(solution)/shard_map/ppermute | solution.py:15
  85.8 8.9 gather_fusion.2
  105.5 4.4 convolution_convert_fusion.2
  114.8 4.4 convolution_convert_fusion.3
  123.7 4.8 fusion.150
  138.7 4.6 fusion.151
  143.4 4.5 broadcast_select_fusion
  147.8 7.7 add_select_fusion
  155.6 15.1 while.6
  156.2 4.4 constant_dynamic-slice_fusion.5
  170.7 355.3 %custom-call.7 = f32[3,6,2,128,128]{3,4,2,1,0:T(8,128)} custom-call(f32[3,6,2,128,128]{4,3,2,1,0:T(8,128)} %bitcast.239), custom_call_target="InvertDiagBlocksLowerTriangular" | custom-call | tf_op jit(solution)/shard_map/triangular_solve/custom-call.1 | solution.py:88
  526.1 4.4 fusion.48
  530.5 6.4 fusion.110
  539.5 9.4 fusion.22
  554.5 4.6 fusion.79
  561.1 4.2 fusion.98
  569.3 25.6 %all-reduce.18.cloned.1.call-done = f32[768,1536]{1,0:T(8,128)} async-done(((f32[768,1536]{1,0:T(8,128)}), f32[768,1536]{1,0:T(8,128)}) %all-reduce.18.cloned.1.call-update) | async-done | bytes 4718608 | tf_op jit(solution)/shard_map/psum | solution.py:157
  601.3 11.7 fusion.153
  613.1 7.0 fusion.152
  620.1 13.6 multiply_convert_fusion
  633.6 5.1 fusion.154
  638.7 10.0 convolution_add_fusion
  648.8 9.1 convolution_convert_fusion
  658.0 4.2 reshape.299
  665.5 13.7 all-reduce.22.cloned.1.call-done
  679.2 5.6 multiply_reduce_fusion
  684.8 20.2 all-reduce.20.cloned.1.call-done
  705.0 7.3 subtract_add_fusion.1
  724.4 10.1 fusion.78
  739.4 8.0 fusion.17
  747.4 8.6 multiply_reduce_fusion.2
  756.0 9.8 fusion.32
  772.2 5.0 fusion.106
  781.0 7.0 fusion.108
  790.0 7.7 fusion.46
  801.3 5.9 fusion.29
  807.3 4.6 fusion.24
  811.9 10.0 fusion.25
  824.5 6.5 fusion.43
  831.1 5.0 fusion.13
  843.8 5.0 fusion.80
  850.9 6.3 multiply_reduce_fusion.10
  862.0 4.3 fusion.94
  884.0 7.4 fusion.96
  891.7 5.7 fusion.92
  897.5 5.7 fusion.88
  903.3 5.7 fusion.84
  909.1 4.2 fusion.156
  914.9 10.0 fusion.160
  926.6 9.9 fusion.159
  936.6 10.0 fusion.158
  951.8 13.0 scatter_custom_fusion
  969.9 5.7 collective-permute-start.3
  976.9 109.6 %reduce-scatter.28.cloned.1.call-done = f32[96,6]{1,0:T(8,128)} async-done(((f32[1536,6]{1,0:T(8,128)}), f32[96,6]{1,0:T(8,128)}) %reduce-scatter.28.cloned.1.call-update) | async-done | bytes 2320
  1088.0 75.7 %all-reduce.12 = (f32[1536]{0:T(1024)S(1)}, f32[4,768]{1,0:T(4,128)}, f32[1536]{0:T(1024)S(1)}) all-reduce(f32[1536]{0:T(1024)S(1)} %get-tuple-element.91, f32[4,768]{1,0:T(4,128)S(1)} %pad_add_fusion, f32[1536]{0:T(1024)S(1)} %copy-done.91), channel_id=2, replica_groups=mesh['dp'=16,'tensor'=2] {'dp'}, use_global_device_ids=true, to_apply=%region_20.23.clone | all-reduce | flops 6144 | bytes 49152
  1168.9 59.5 %reduce-scatter.20.cloned.1.call-done = f32[768,96]{0,1:T(8,128)} async-done(((f32[768,1536]{0,1:T(8,128)}), f32[768,96]{0,1:T(8,128)}) %reduce-scatter.20.cloned.1.call-update) | async-done | bytes 294928 | tf_op jit(solution)/shard_map/reduce_scatter | solution.py:229
  1228.4 142.6 %reduce-scatter.12.cloned.1.call-done = f32[96,768]{1,0:T(8,128)} async-done(((f32[1536,768]{1,0:T(8,128)}), f32[96,768]{1,0:T(8,128)}) %reduce-scatter.12.cloned.1.call-update) | async-done | bytes 294928 | tf_op jit(solution)/shard_map/reduce_scatter | solution.py:224
  1371.0 141.3 %reduce-scatter.14.cloned.1.call-done = f32[96,768]{1,0:T(8,128)} async-done(((f32[1536,768]{1,0:T(8,128)}), f32[96,768]{1,0:T(8,128)}) %reduce-scatter.14.cloned.1.call-update) | async-done | bytes 294928 | tf_op jit(solution)/shard_map/reduce_scatter | solution.py:225
  1512.3 143.4 %reduce-scatter.16.cloned.1.call-done = f32[96,768]{1,0:T(8,128)} async-done(((f32[1536,768]{1,0:T(8,128)}), f32[96,768]{1,0:T(8,128)}) %reduce-scatter.16.cloned.1.call-update) | async-done | bytes 294928 | tf_op jit(solution)/shard_map/reduce_scatter | solution.py:226
  1655.7 141.5 %reduce-scatter.18.cloned.1.call-done = f32[96,768]{1,0:T(8,128)} async-done(((f32[1536,768]{1,0:T(8,128)}), f32[96,768]{1,0:T(8,128)}) %reduce-scatter.18.cloned.1.call-update) | async-done | bytes 294928 | tf_op jit(solution)/shard_map/reduce_scatter | solution.py:227
  1797.2 210.3 %reduce-scatter.26.cloned.1.call-done = f32[2048,96]{0,1:T(8,128)} async-done(((f32[2048,1536]{0,1:T(8,128)}), f32[2048,96]{0,1:T(8,128)}) %reduce-scatter.26.cloned.1.call-update) | async-done | bytes 786448 | tf_op jit(solution)/shard_map/reduce_scatter | solution.py:186
  2007.5 209.8 %reduce-scatter.24.cloned.1.call-done = f32[96,2048]{1,0:T(8,128)} async-done(((f32[1536,2048]{1,0:T(8,128)}), f32[96,2048]{1,0:T(8,128)}) %reduce-scatter.24.cloned.1.call-update) | async-done | bytes 786448 | tf_op jit(solution)/shard_map/reduce_scatter | solution.py:185
  2217.3 210.8 %reduce-scatter.22.cloned.1.call-done = f32[96,2048]{1,0:T(8,128)} async-done(((f32[1536,2048]{1,0:T(8,128)}), f32[96,2048]{1,0:T(8,128)}) %reduce-scatter.22.cloned.1.call-update) | async-done | bytes 786448 | tf_op jit(solution)/shard_map/reduce_scatter | solution.py:184
  (392 shorter events, 169.5 us)
Async XLA Ops:
  7.2 553.9 %copy-start = (bf16[768,1536]{1,0:T(8,128)(2,1)S(1)}, bf16[768,1536]{1,0:T(8,128)(2,1)}, u32[]{:S(2)}) copy-start(bf16[768,1536]{1,0:T(8,128)(2,1)} %param.31) | copy-start | bytes 7077892
  7.2 587.7 %all-reduce.18.cloned.1.call-start = ((), (), s32[]{:S(2)}) async-start(), calls=%async_computation.9 | async-start | bytes 9437184 | tf_op jit(solution)/shard_map/psum | solution.py:157
  7.2 72.6 %collective-permute-start = (bf16[512,1536]{1,0:T(8,128)(2,1)}, bf16[512,1536]{1,0:T(8,128)(2,1)}, u32[]{:S(2)}, u32[]{:S(2)}) collective-permute-start(bf16[512,1536]{1,0:T(8,128)(2,1)} %param.20), channel_id=1, source_target_pairs={{0,2},{2,4},{4,6},{6,8},{8,10},{10,12},{12,14},{14,16},{16,18},{18... | collective-permute-start | bytes 4718600 | tf_op jit(solution)/shard_map/ppermute | solution.py:15
  13.4 68.5 %collective-permute-start.1 = (bf16[512,1536]{1,0:T(8,128)(2,1)}, bf16[512,1536]{1,0:T(8,128)(2,1)}, u32[]{:S(2)}, u32[]{:S(2)}) collective-permute-start(bf16[512,1536]{1,0:T(8,128)(2,1)} %param.20), channel_id=1, source_target_pairs={{2,0},{4,2},{6,4},{8,6},{10,8},{12,10},{14,12},{16,14},{18,16},{20... | collective-permute-start | bytes 4718600 | tf_op jit(solution)/shard_map/ppermute | solution.py:18
  19.2 66.6 %copy-start.96 = (pred[768]{0:T(1024)(128)(4,1)}, pred[768]{0:T(1024)(128)(4,1)S(1)}, u32[]{:S(2)}) copy-start(pred[768]{0:T(1024)(128)(4,1)S(1)} %lt.89) | copy-start | bytes 2308
  22.1 106.4 %copy-start.80 = (f32[768]{0:T(1024)}, f32[768]{0:T(1024)S(1)}, u32[]{:S(2)}) copy-start(f32[768]{0:T(1024)S(1)} %get-tuple-element.96) | copy-start | bytes 9220
  22.2 106.4 %copy-start.82 = (f32[768]{0:T(1024)}, f32[768]{0:T(1024)S(1)}, u32[]{:S(2)}) copy-start(f32[768]{0:T(1024)S(1)} %get-tuple-element.97) | copy-start | bytes 9220
  22.2 106.4 %copy-start.84 = (f32[768]{0:T(1024)}, f32[768]{0:T(1024)S(1)}, u32[]{:S(2)}) copy-start(f32[768]{0:T(1024)S(1)} %get-tuple-element.98) | copy-start | bytes 9220
  22.2 106.4 %copy-start.86 = (f32[768]{0:T(1024)}, f32[768]{0:T(1024)S(1)}, u32[]{:S(2)}) copy-start(f32[768]{0:T(1024)S(1)} %get-tuple-element.99) | copy-start | bytes 9220
  23.6 74.3 %copy-start.88 = (pred[768]{0:T(1024)(128)(4,1)}, pred[768]{0:T(1024)(128)(4,1)S(1)}, u32[]{:S(2)}) copy-start(pred[768]{0:T(1024)(128)(4,1)S(1)} %compare_and_fusion) | copy-start | bytes 2308
  123.7 15.0 copy-start.19
  138.7 9.1 copy-start.2
  147.8 7.7 copy-start.104
  526.1 10.9 copy-start.30
  526.1 10.9 copy-start.35
  530.5 8.9 copy-start.11
  530.5 8.9 slice-start.4
  539.5 9.4 copy-start.13
  539.5 9.4 copy-start.20
  539.5 9.4 copy-start.23
  565.3 29.6 %copy-start.89 = (pred[768]{0:T(1024)(128)(4,1)S(1)}, pred[768]{0:T(1024)(128)(4,1)}, u32[]{:S(2)}) copy-start(pred[768]{0:T(1024)(128)(4,1)} %copy-done.88) | copy-start | bytes 2308
  565.3 113.9 %all-reduce.22.cloned.1.call-start = ((), (), s32[]{:S(2)}) async-start(), calls=%async_computation.11 | async-start | bytes 9437184 | tf_op jit(solution)/shard_map/psum | solution.py:179
  569.3 29.7 %copy-start.75 = (f32[1536]{0:T(1024)S(1)}, f32[1536]{0:T(1024)}, u32[]{:S(2)}) copy-start(f32[1536]{0:T(1024)} %param.32) | copy-start | bytes 18436
  598.9 14.1 slice-start.14
  601.3 11.7 copy-start.52
  601.3 11.7 slice-start.15
  648.8 56.2 %all-reduce.20.cloned.1.call-start = ((), (), s32[]{:S(2)}) async-start(), calls=%async_computation.10 | async-start | bytes 4718592 | tf_op jit(solution)/shard_map/psum | solution.py:166
  657.9 288.7 %all-reduce.24.cloned.1.call-start = ((), (), s32[]{:S(2)}) async-start(), calls=%async_computation.12 | async-start | bytes 9437184 | tf_op jit(solution)/shard_map/psum | solution.py:210
  721.6 12.9 slice-start
  724.4 10.1 slice-start.1
  724.4 10.1 copy-start.45
  737.7 9.7 slice-start.8
  739.3 8.1 copy-start.5
  739.3 8.1 copy-start.64
  739.4 8.0 slice-start.9
  739.4 8.0 copy-start.12
  739.4 8.0 copy-start.14
  756.0 12.0 copy-start.31
  790.0 7.8 copy-start.24
  790.0 7.8 copy-start.29
  790.0 7.8 copy-start.47
  797.8 9.5 slice-start.10
  824.5 11.6 slice-start.12
  824.5 13.9 slice-start.2
  831.1 7.4 slice-start.3
  843.8 7.1 copy-start.36
  843.8 7.1 copy-start.38
  880.6 206.0 %reduce-scatter.28.cloned.1.call-start = ((), (), s32[]{:S(2)}) async-start(), calls=%async_computation.21 | async-start | bytes 835584
  884.0 344.4 %reduce-scatter.20.cloned.1.call-start = ((), (), s32[]{:S(2)}) async-start(), calls=%async_computation.17 | async-start | bytes 5013504 | tf_op jit(solution)/shard_map/reduce_scatter | solution.py:229
  891.5 479.5 %reduce-scatter.12.cloned.1.call-start = ((), (), s32[]{:S(2)}) async-start(), calls=%async_computation.13 | async-start | bytes 5013504 | tf_op jit(solution)/shard_map/reduce_scatter | solution.py:224
  897.4 614.9 %reduce-scatter.14.cloned.1.call-start = ((), (), s32[]{:S(2)}) async-start(), calls=%async_computation.14 | async-start | bytes 5013504 | tf_op jit(solution)/shard_map/reduce_scatter | solution.py:225
  903.2 752.5 %reduce-scatter.16.cloned.1.call-start = ((), (), s32[]{:S(2)}) async-start(), calls=%async_computation.15 | async-start | bytes 5013504 | tf_op jit(solution)/shard_map/reduce_scatter | solution.py:226
  909.0 888.2 %reduce-scatter.18.cloned.1.call-start = ((), (), s32[]{:S(2)}) async-start(), calls=%async_computation.16 | async-start | bytes 5013504 | tf_op jit(solution)/shard_map/reduce_scatter | solution.py:227
  913.3 1094.3 %reduce-scatter.26.cloned.1.call-start = ((), (), s32[]{:S(2)}) async-start(), calls=%async_computation.20 | async-start | bytes 13369344 | tf_op jit(solution)/shard_map/reduce_scatter | solution.py:186
  924.9 1292.4 %reduce-scatter.24.cloned.1.call-start = ((), (), s32[]{:S(2)}) async-start(), calls=%async_computation.19 | async-start | bytes 13369344 | tf_op jit(solution)/shard_map/reduce_scatter | solution.py:185
  936.5 1491.6 %reduce-scatter.22.cloned.1.call-start = ((), (), s32[]{:S(2)}) async-start(), calls=%async_computation.18 | async-start | bytes 13369344 | tf_op jit(solution)/shard_map/reduce_scatter | solution.py:184
  964.8 10.8 copy-start.103
  964.8 12.1 copy-start.95
  964.8 12.1 copy-start.93
  964.8 12.1 copy-start.92
  964.8 123.2 %copy-start.91 = (f32[1536]{0:T(1024)S(1)}, f32[1536]{0:T(1024)}, u32[]{:S(2)}) copy-start(f32[1536]{0:T(1024)} %get-tuple-element.89) | copy-start | bytes 18436
  968.6 196.3 %collective-permute-start.2 = (bf16[512,1536]{1,0:T(8,128)(2,1)}, bf16[512,1536]{1,0:T(8,128)(2,1)}, u32[]{:S(2)}, u32[]{:S(2)}) collective-permute-start(bf16[512,1536]{1,0:T(8,128)(2,1)} %get-tuple-element.125), channel_id=1, source_target_pairs={{2,0},{4,2},{6,4},{8,6},{10,8},{12,10},{14,12},{16,14},{18,16},{20... | collective-permute-start | bytes 4718600 | tf_op jit(solution)/shard_map/ppermute | solution.py:26
  969.9 195.1 %collective-permute-start.3 = (bf16[512,1536]{1,0:T(8,128)(2,1)}, bf16[512,1536]{1,0:T(8,128)(2,1)}, u32[]{:S(2)}, u32[]{:S(2)}) collective-permute-start(bf16[512,1536]{1,0:T(8,128)(2,1)} %get-tuple-element.126), channel_id=1, source_target_pairs={{0,2},{2,4},{4,6},{6,8},{8,10},{10,12},{12,14},{14,16},{16,18},{18... | collective-permute-start | bytes 4718600 | tf_op jit(solution)/shard_map/ppermute | solution.py:26
  1164.3 1263.8 %copy-start.1 = (bf16[768,1536]{1,0:T(8,128)(2,1)S(1)}, bf16[768,1536]{1,0:T(8,128)(2,1)}, u32[]{:S(2)}) copy-start(bf16[768,1536]{1,0:T(8,128)(2,1)} %param.31) | copy-start | bytes 7077892
  (76 other events, 235.4 us)
Sparse Core Ops, SparseCore 0:
  565.4 29.4 all-reduce.17
  648.9 30.2 all-reduce.21
  682.2 22.7 all-reduce.19
  880.7 30.3 all-reduce.23
  915.6 170.8 reduce-scatter.27
  1092.1 136.1 reduce-scatter.19
  1234.9 136.0 reduce-scatter.11
  1376.7 135.5 reduce-scatter.13
  1518.9 136.7 reduce-scatter.15
  1661.3 135.8 reduce-scatter.17
  1804.4 203.0 reduce-scatter.25
  2013.6 203.6 reduce-scatter.23
  2224.5 203.6 reduce-scatter.21
where the time goes:
time: 2450 us; the launch traced here: 2440 us
  waiting for transfers between devices  1490 us (61%)
  other arithmetic  429 us (18%)
  matrix products  315 us (13%)
  local copies, waits for them, and re-layouts  95.5 us (4%)
  blocking collectives  75.7 us (3%)
    another operation x4, other arithmetic, path_mixer(): lax.linalg.triangular_solve(identity + coupling, house_key, left_side=Tru...  357 us
    reduce_scatter x1, waiting for transfers between devices, on_device(): lax.psum_scatter(g_gate, 'dp', scatter_dimension=0, tiled=True)  211 us
    reduce_scatter x1, waiting for transfers between devices, on_device(): lax.psum_scatter(g_down, 'dp', scatter_dimension=1, tiled=True)  210 us
    reduce_scatter x1, waiting for transfers between devices, on_device(): lax.psum_scatter(g_up, 'dp', scatter_dimension=0, tiled=True)  210 us
    reduce_scatter x1, waiting for transfers between devices, on_device(): lax.psum_scatter(g_value, 'dp', scatter_dimension=0, tiled=True)  143 us
    reduce_scatter x1, waiting for transfers between devices, on_device(): lax.psum_scatter(g_query, 'dp', scatter_dimension=0, tiled=True)  143 us
    reduce_scatter x1, waiting for transfers between devices, on_device(): lax.psum_scatter(g_house, 'dp', scatter_dimension=0, tiled=True)  142 us
    reduce_scatter x1, waiting for transfers between devices, on_device(): lax.psum_scatter(g_key, 'dp', scatter_dimension=0, tiled=True)  141 us
  transfers between devices with their start and end apart: 17, of which 14 were waited for; matrix products, arithmetic and copies ran while one was open for 5% of the time, Pallas kernels for 0%

commit v1 on v0

v1 whole, which is shorter than its diff:
```python
import functools
import jax
import jax.numpy as jnp
from jax import lax
from jax.experimental import pallas as pl
from jax.experimental.pallas import tpu as pltpu
from jax.sharding import PartitionSpec as P

EPSILON = 1e-06
BF = jnp.bfloat16
F32 = jnp.float32


def dot_nn(a, b):
    return lax.dot_general(a, b, (((1,), (0,)), ((), ())), preferred_element_type=F32)


def dot_nt(a, b):
    return lax.dot_general(a, b, (((1,), (1,)), ((), ())), preferred_element_type=F32)


def dot_tn(a, b):
    return lax.dot_general(a, b, (((0,), (0,)), ((), ())), preferred_element_type=F32)


def halves(x):
    high = x.astype(BF)
    return high, (x - high.astype(F32)).astype(BF)


def dot_split(a, b):
    a_high, a_low = halves(a)
    b_high, b_low = halves(b)
    return dot_nn(a_high, b_high) + (dot_nn(a_high, b_low) + dot_nn(a_low, b_high))


def unit_lower_inverse(strict, base):
    size = strict.shape[0]
    lanes = 128
    tiles = size // lanes
    per_tile = lanes // base
    lane = lax.broadcasted_iota(jnp.int32, (base, lanes), 1)
    row = lax.broadcasted_iota(jnp.int32, (base, lanes), 0)
    owner = lane // base
    within = lane % base
    compact = []
    for tile in range(tiles):
        piece = jnp.zeros((base, lanes), F32)
        for block in range(per_tile):
            top = tile * lanes + block * base
            piece = jnp.where(
                owner == block, strict[top : top + base, tile * lanes : (tile + 1) * lanes], piece
            )
        compact.append(piece)
    solved = [jnp.where(row == within, 1.0, 0.0).astype(F32) for _ in range(tiles)]
    for step in range(base - 1):
        index = owner * base + step
        for tile in range(tiles):
            weight = jnp.take_along_axis(compact[tile], index, axis=1)
            solved[tile] = solved[tile] - weight * solved[tile][step : step + 1, :]
    rows = []
    for tile in range(tiles):
        for block in range(per_tile):
            piece = jnp.where(owner == block, solved[tile], 0.0)
            parts = [jnp.zeros((base, lanes), F32)] * tiles
            parts[tile] = piece
            rows.append(jnp.concatenate(parts, axis=1))
    inverse = jnp.concatenate(rows, axis=0)
    grown = base * 2
    row_big = lax.broadcasted_iota(jnp.int32, (size, size), 0)
    col_big = lax.broadcasted_iota(jnp.int32, (size, size), 1)
    while grown < size:
        joined = (row_big // grown == col_big // grown) & (
            row_big // (grown // 2) != col_big // (grown // 2)
        )
        cross = jnp.where(joined, strict, 0.0)
        inverse = inverse - dot_split(dot_split(inverse, cross), inverse)
        grown *= 2
    half = size // 2
    first, second = inverse[:half, :half], inverse[half:, half:]
    corner = -dot_split(dot_split(second, strict[half:, :half]), first)
    top = jnp.concatenate([first, jnp.zeros((half, half), F32)], axis=1)
    bottom = jnp.concatenate([corner, second], axis=1)
    return jnp.concatenate([top, bottom], axis=0)


def shifted_rows(x, amount, place):
    return jnp.where(place >= amount, pltpu.roll(x, amount, 0), 0.0)


def direction(house, taps, place):
    conv = taps[0:1, :] * house
    for shift in range(1, taps.shape[0]):
        conv = conv + taps[shift : shift + 1, :] * shifted_rows(house, shift, place)
    inverse = lax.rsqrt(jnp.sum(conv * conv, axis=1, keepdims=True) + EPSILON)
    return conv, inverse


PAIRS = ((0, 0), (1, 0), (1, 1))


def scores_of(query, key, house_dir, begin, half, a, b):
    rows, cols = slice(a * half, (a + 1) * half), slice(b * half, (b + 1) * half)
    left = jnp.concatenate([query[rows], house_dir[rows]], axis=0)
    right = jnp.concatenate([key[cols], house_dir[cols]], axis=0)
    every = dot_nt(left, right)
    col = lax.broadcasted_iota(jnp.int32, (half, half), 1) + b * half
    row = lax.broadcasted_iota(jnp.int32, (half, half), 0) + a * half
    inside = col >= begin[rows]
    upto = inside & (col <= row)
    before = inside & (col < row)
    return (
        every[:half, :half],
        jnp.where(upto, every[:half, half:], 0.0),
        jnp.where(before, every[half:, :half], 0.0),
        jnp.where(before, every[half:, half:], 0.0),
        upto,
        before,
    )


def forward_head(query, key, value, house, logit, taps, begin, place):
    half = query.shape[0] // 2
    scaling = query.shape[1] ** (-0.5)
    conv, inverse = direction(house, taps, place)
    house_dir = (conv * inverse).astype(BF)
    beta = 2.0 * jax.nn.sigmoid(logit)
    raw, cross, know, gram, upto = {}, {}, {}, {}, {}
    for a, b in PAIRS:
        raw[a, b], x, know[a, b], g, upto[a, b], _ = scores_of(
            query, key, house_dir, begin, half, a, b
        )
        beta_cols = beta[:, b * half : (b + 1) * half]
        cross[a, b] = (x * beta_cols).astype(BF)
        gram[a, b] = g * beta_cols
    eye = (
        lax.broadcasted_iota(jnp.int32, (half, half), 0)
        == lax.broadcasted_iota(jnp.int32, (half, half), 1)
    )
    tail = {}
    for a in (0, 1):
        tail[a] = jnp.where(eye, 0.0, unit_lower_inverse(gram[a, a], 32)).astype(BF)
    z00 = know[0, 0] + dot_nn(tail[0], know[0, 0].astype(BF))
    z00b = z00.astype(BF)
    z11 = know[1, 1] + dot_nn(tail[1], know[1, 1].astype(BF))
    z11b = z11.astype(BF)
    rest = know[1, 0] - dot_nn(gram[1, 0].astype(BF), z00b)
    z10 = rest + dot_nn(tail[1], rest.astype(BF))
    z10b = z10.astype(BF)
    s00 = raw[0, 0] - dot_nn(cross[0, 0], z00b)
    s10 = raw[1, 0] - dot_nn(cross[1, 0], z00b) - dot_nn(cross[1, 1], z10b)
    s11 = raw[1, 1] - dot_nn(cross[1, 1], z11b)
    s00 = jnp.where(upto[0, 0], s00 * scaling, -1e30)
    s10 = jnp.where(upto[1, 0], s10 * scaling, -1e30)
    s11 = jnp.where(upto[1, 1], s11 * scaling, -1e30)
    top0 = jnp.max(s00, axis=1, keepdims=True)
    top1 = jnp.maximum(
        jnp.max(s10, axis=1, keepdims=True), jnp.max(s11, axis=1, keepdims=True)
    )
    e00, e10, e11 = jnp.exp(s00 - top0), jnp.exp(s10 - top1), jnp.exp(s11 - top1)
    sum0 = jnp.sum(e00, axis=1, keepdims=True)
    sum1 = jnp.sum(e10, axis=1, keepdims=True) + jnp.sum(e11, axis=1, keepdims=True)
    inv0, inv1 = 1.0 / sum0, 1.0 / sum1
    p00, p10, p11 = (
        (e00 * inv0).astype(BF),
        (e10 * inv1).astype(BF),
        (e11 * inv1).astype(BF),
    )
    mixed0 = dot_nn(p00, value[:half])
    mixed1 = dot_nn(p10, value[:half]) + dot_nn(p11, value[half:])
    mixed = jnp.concatenate([mixed0, mixed1], axis=0).astype(BF)
    return mixed, (p00, p10, p11, z00b, z10b, z11b, tail[0], tail[1])


def forward_kernel(heads, begin_ref, logit_ref, taps_ref, house_ref, q_ref, k_ref, v_ref, mixed_ref, kept_ref):
    step = pl.program_id(0)
    begin = begin_ref[...]
    rows = begin.shape[0]
    place = lax.broadcasted_iota(jnp.int32, (rows, 1), 0) - begin
    for head in range(heads):
        cols = slice(head * 128, (head + 1) * 128)
        logit = logit_ref[pl.ds(step * heads + head, 1), :]
        mixed, kept = forward_head(
            q_ref[:, cols], k_ref[:, cols], v_ref[:, cols], house_ref[:, cols], logit,
            taps_ref[:, cols], begin, place,
        )
        mixed_ref[:, cols] = mixed
        for slot, item in enumerate(kept):
            kept_ref[head, slot] = item


def mixer_forward(begin, logit, taps, house, query, key, value, heads=2):
    rows, width = query.shape
    count = width // 128
    half = rows // 2
    wide = pl.BlockSpec((rows, heads * 128), lambda i: (0, i))
    return pl.pallas_call(
        functools.partial(forward_kernel, heads),
        grid=(count // heads,),
        in_specs=[
            pl.BlockSpec((rows, 1), lambda i: (0, 0)),
            pl.BlockSpec(logit.shape, lambda i: (0, 0)),
            pl.BlockSpec((taps.shape[0], heads * 128), lambda i: (0, i)),
            wide, wide, wide, wide,
        ],
        out_specs=[wide, pl.BlockSpec((heads, 8, half, half), lambda i: (i, 0, 0, 0))],
        out_shape=[
            jax.ShapeDtypeStruct((rows, width), BF),
            jax.ShapeDtypeStruct((count, 8, half, half), BF),
        ],
        compiler_params=pltpu.CompilerParams(vmem_limit_bytes=56 << 20),
        cost_estimate=pl.CostEstimate(flops=60_000_000_000, bytes_accessed=16_000_000, transcendentals=2_000_000),
        name="mixer_forward",
    )(begin, logit, taps, house, query, key, value)


def backward_head(query, key, value, house, logit, taps, begin, place, d_mixed, kept):
    p00, p10, p11, z00, z10, z11, tail0, tail1 = kept
    rows = query.shape[0]
    half = rows // 2
    scaling = query.shape[1] ** (-0.5)
    conv, inverse = direction(house, taps, place)
    direct = conv * inverse
    house_dir = direct.astype(BF)
    beta = 2.0 * jax.nn.sigmoid(logit)
    cross, cross_b, gram, gram_raw, upto, before, beta_cols = {}, {}, {}, {}, {}, {}, {}
    for a, b in PAIRS:
        _, cross[a, b], _, gram_raw[a, b], upto[a, b], before[a, b] = scores_of(
            query, key, house_dir, begin, half, a, b
        )
        beta_cols[b] = beta[:, b * half : (b + 1) * half]
        cross_b[a, b] = (cross[a, b] * beta_cols[b]).astype(BF)
    gram10 = (gram_raw[1, 0] * beta_cols[0]).astype(BF)
    d0, d1 = d_mixed[:half], d_mixed[half:]
    v0, v1 = value[:half], value[half:]
    dp00, dp10, dp11 = dot_nt(d0, v0), dot_nt(d1, v0), dot_nt(d1, v1)
    dv0 = dot_tn(p00, d0) + dot_tn(p10, d1)
    dv1 = dot_tn(p11, d1)
    f00, f10, f11 = p00.astype(F32), p10.astype(F32), p11.astype(F32)
    mean0 = jnp.sum(f00 * dp00, axis=1, keepdims=True)
    mean1 = jnp.sum(f10 * dp10, axis=1, keepdims=True) + jnp.sum(f11 * dp11, axis=1, keepdims=True)
    ds = {
        (0, 0): (f00 * (dp00 - mean0) * scaling).astype(BF),
        (1, 0): (f10 * (dp10 - mean1) * scaling).astype(BF),
        (1, 1): (f11 * (dp11 - mean1) * scaling).astype(BF),
    }
    dx = {
        (0, 0): dot_nt(ds[0, 0], z00),
        (1, 0): dot_nt(ds[1, 0], z00),
        (1, 1): dot_nt(ds[1, 1], z11) + dot_nt(ds[1, 0], z10),
    }
    dz00 = dot_tn(cross_b[0, 0], ds[0, 0]) + dot_tn(cross_b[1, 0], ds[1, 0])
    dz10 = dot_tn(cross_b[1, 1], ds[1, 0])
    dz11 = dot_tn(cross_b[1, 1], ds[1, 1])
    e11 = dz11 + dot_tn(tail1, dz11.astype(BF))
    e10 = dz10 + dot_tn(tail1, dz10.astype(BF))
    rest = dz00 - dot_tn(gram10, e10.astype(BF))
    e00 = rest + dot_tn(tail0, rest.astype(BF))
    e00b, e10b, e11b = e00.astype(BF), e10.astype(BF), e11.astype(BF)
    dn = {
        (0, 0): dot_nt(e00b, z00),
        (1, 0): dot_nt(e10b, z00),
        (1, 1): dot_nt(e10b, z10) + dot_nt(e11b, z11),
    }
    dy = {(0, 0): e00, (1, 0): e10, (1, 1): e11}
    d_beta = [jnp.zeros((1, half), F32), jnp.zeros((1, half), F32)]
    d_q = [0.0, 0.0]
    d_w = [0.0, 0.0]
    d_k = [0.0, 0.0]
    for a, b in PAIRS:
        part_x = jnp.where(upto[a, b], -dx[a, b], 0.0)
        part_n = jnp.where(before[a, b], dn[a, b], 0.0)
        part_y = jnp.where(before[a, b], -dy[a, b], 0.0)
        d_beta[b] = d_beta[b] + jnp.sum(
            part_x * cross[a, b] + part_n * gram_raw[a, b], axis=0, keepdims=True
        )
        upper = jnp.concatenate([ds[a, b], (part_x * beta_cols[b]).astype(BF)], axis=1)
        lower = jnp.concatenate([part_y.astype(BF), (part_n * beta_cols[b]).astype(BF)], axis=1)
        big = jnp.concatenate([upper, lower], axis=0)
        rows_a, cols_b = slice(a * half, (a + 1) * half), slice(b * half, (b + 1) * half)
        right = jnp.concatenate([key[cols_b], house_dir[cols_b]], axis=0)
        left = jnp.concatenate([query[rows_a], house_dir[rows_a]], axis=0)
        by_row = dot_nn(big, right)
        by_col = dot_tn(big, left)
        d_q[a] = d_q[a] + by_row[:half]
        d_w[a] = d_w[a] + by_row[half:]
        d_k[b] = d_k[b] + by_col[:half]
        d_w[b] = d_w[b] + by_col[half:]
    d_dir = jnp.concatenate(d_w, axis=0)
    d_conv = inverse * d_dir - direct * (
        inverse * jnp.sum(direct * d_dir, axis=1, keepdims=True)
    )
    d_house = taps[0:1, :] * d_conv
    d_taps = [jnp.sum(d_conv * house, axis=0, keepdims=True)]
    for shift in range(1, taps.shape[0]):
        live = jnp.where(place >= shift, d_conv, 0.0)
        d_house = d_house + taps[shift : shift + 1, :] * pltpu.roll(live, rows - shift, 0)
        d_taps.append(jnp.sum(live * pltpu.roll(house, shift, 0), axis=0, keepdims=True))
    d_logit = jnp.concatenate(d_beta, axis=1) * beta * (1.0 - 0.5 * beta)
    return (
        jnp.concatenate(d_q, axis=0).astype(BF),
        jnp.concatenate(d_k, axis=0).astype(BF),
        jnp.concatenate([dv0, dv1], axis=0).astype(BF),
        d_house.astype(BF),
        d_logit,
        d_taps,
    )


def backward_kernel(
    heads, begin_ref, logit_ref, taps_ref, house_ref, q_ref, k_ref, v_ref, dm_ref, kept_ref,
    dq_ref, dk_ref, dv_ref, dh_ref, dl_ref, dt_ref,
):
    step = pl.program_id(0)
    begin = begin_ref[...]
    rows = begin.shape[0]
    place = lax.broadcasted_iota(jnp.int32, (rows, 1), 0) - begin
    for head in range(heads):
        cols = slice(head * 128, (head + 1) * 128)
        logit = logit_ref[pl.ds(step * heads + head, 1), :]
        kept = tuple(kept_ref[head, slot] for slot in range(8))
        d_q, d_k, d_v, d_h, d_l, d_t = backward_head(
            q_ref[:, cols], k_ref[:, cols], v_ref[:, cols], house_ref[:, cols], logit,
            taps_ref[:, cols], begin, place, dm_ref[:, cols], kept,
        )
        dq_ref[:, cols] = d_q
        dk_ref[:, cols] = d_k
        dv_ref[:, cols] = d_v
        dh_ref[:, cols] = d_h
        dl_ref[pl.ds(step * heads + head, 1), :] = d_l
        for tap, item in enumerate(d_t):
            dt_ref[tap : tap + 1, cols] = item


def mixer_backward(begin, logit, taps, house, query, key, value, d_mixed, kept, heads=2):
    rows, width = query.shape
    count = width // 128
    half = rows // 2
    wide = pl.BlockSpec((rows, heads * 128), lambda i: (0, i))
    narrow = pl.BlockSpec((taps.shape[0], heads * 128), lambda i: (0, i))
    whole = pl.BlockSpec(logit.shape, lambda i: (0, 0))
    big = jax.ShapeDtypeStruct((rows, width), BF)
    return pl.pallas_call(
        functools.partial(backward_kernel, heads),
        grid=(count // heads,),
        in_specs=[
            pl.BlockSpec((rows, 1), lambda i: (0, 0)),
            whole, narrow, wide, wide, wide, wide, wide,
            pl.BlockSpec((heads, 8, half, half), lambda i: (i, 0, 0, 0)),
        ],
        out_specs=[wide, wide, wide, wide, whole, narrow],
        out_shape=[big, big, big, big, jax.ShapeDtypeStruct(logit.shape, F32), jax.ShapeDtypeStruct(taps.shape, F32)],
        compiler_params=pltpu.CompilerParams(vmem_limit_bytes=56 << 20),
        cost_estimate=pl.CostEstimate(flops=60_000_000_000, bytes_accessed=20_000_000, transcendentals=2_000_000),
        name="mixer_backward",
    )(begin, logit, taps, house, query, key, value, d_mixed, kept)


def wgrad_kernel(order_ref, left_ref, right_ref, out_ref, packed):
    count = out_ref.shape[0] // left_ref.shape[1]
    block = left_ref.shape[1]

    @pl.when(pl.program_id(0) == 0)
    def _():
        for i in range(count):
            packed[i * block : (i + 1) * block, :] = left_ref[order_ref[i]]

    out_ref[...] = dot_nn(packed[...], right_ref[...]).astype(out_ref.dtype)


def wgrad(order, left, right, dtype, tile=512):
    count = order.shape[0]
    block, tokens = left.shape[1:]
    columns = right.shape[1]
    tile = next(t for t in (tile, 384, 256, 128) if columns % t == 0)
    return pl.pallas_call(
        wgrad_kernel,
        grid_spec=pltpu.PrefetchScalarGridSpec(
            num_scalar_prefetch=1,
            grid=(columns // tile,),
            in_specs=[
                pl.BlockSpec(left.shape, lambda j, order: (0, 0, 0)),
                pl.BlockSpec((tokens, tile), lambda j, order: (0, j)),
            ],
            out_specs=pl.BlockSpec((count * block, tile), lambda j, order: (0, j)),
            scratch_shapes=[pltpu.VMEM((count * block, tokens), BF)],
        ),
        out_shape=jax.ShapeDtypeStruct((count * block, columns), dtype),
        compiler_params=pltpu.CompilerParams(vmem_limit_bytes=32 << 20),
        cost_estimate=pl.CostEstimate(
            flops=2 * count * block * tokens * columns,
            bytes_accessed=2 * (left.size + right.size + count * block * columns),
            transcendentals=0,
        ),
        name="wgrad",
    )(order, left, right)


def swap(x, axis, bit):
    size = lax.axis_size(axis)
    return lax.ppermute(x, axis, [(i, i ^ (1 << bit)) for i in range(size)])


def shard_order(me, size, bits):
    position = size - 1 - jnp.arange(size, dtype=jnp.int32)
    flips = jnp.zeros((size,), jnp.int32)
    for rank, bit in enumerate(bits):
        flips = flips + (((position >> (len(bits) - 1 - rank)) & 1) << bit)
    return me ^ flips


def scatter_sum(leave, stay, bits):
    terms = [stay, swap(leave, "dp", bits[0])]
    for bit in bits[1:]:
        half = terms[0].shape[0] // 2
        out = sum(t[:half].astype(F32) for t in terms).astype(BF)
        terms = [t[half:] for t in terms] + [swap(out, "dp", bit)]
    return sum(t.astype(F32) for t in terms)


def tensor_sum(x):
    if lax.axis_size("tensor") == 2:
        return x.astype(F32) + swap(x, "tensor", 0).astype(F32)
    return lax.psum(x, "tensor").astype(F32)


def contract_cols(a, b):
    return dot_nt(a, b)


def norm_back(d_normed, source, inverse, gain_vec):
    scaled = d_normed * gain_vec
    return inverse * scaled - source * (inverse * inverse * inverse) * jnp.mean(
        scaled * source, axis=1, keepdims=True
    )


def chosen(index, count):
    return (index[:, None] == jnp.arange(count, dtype=jnp.int32)[None, :]).astype(BF)


def on_device(
    tokens,
    cotangent,
    lengths,
    dealing,
    attn_gain,
    w_query,
    w_key,
    w_value,
    w_house,
    w_beta,
    conv_taps,
    w_out,
    ffn_gain,
    w_gate,
    w_up,
    w_down,
):
    rows, width = tokens.shape
    slots, span = cotangent.shape[:2]
    size = lax.axis_size("dp")
    me = lax.axis_index("dp")
    block = width // size
    up = [(i, i + 1) for i in range(size - 1)]
    down = [(i + 1, i) for i in range(size - 1)]

    own = lax.dynamic_index_in_dim(lengths, me, 0, keepdims=False)
    earlier = jnp.arange(slots)[None, :] < jnp.arange(slots)[:, None]
    starts = jnp.sum(jnp.where(earlier, own[None, :], 0), axis=1)
    row = jnp.arange(rows, dtype=jnp.int32)
    segment = jnp.sum((starts[None, :] <= row[:, None]).astype(jnp.int32), axis=1) - 1
    begin = jnp.max(jnp.where(starts[None, :] <= row[:, None], starts[None, :], 0), axis=1)
    ids = me * slots + jnp.arange(slots, dtype=jnp.int32)
    place = jnp.sum(
        jnp.where(
            dealing[None, :] == ids[:, None],
            jnp.arange(dealing.shape[0], dtype=jnp.int32)[None, :],
            0,
        ),
        axis=1,
    )
    holder = place // slots - me
    slot_of = place % slots
    held = lax.dynamic_slice_in_dim(dealing, me * slots, slots)
    held_from = held // slots - me
    slot_index = jnp.arange(slots, dtype=jnp.int32)
    slot_up = jnp.sum(jnp.where(held_from == 1, slot_index, 0))
    slot_down = jnp.sum(jnp.where(held_from == -1, slot_index, 0))

    cot_low = lax.ppermute(
        lax.dynamic_index_in_dim(cotangent, slot_up, 0, keepdims=False), "dp", up
    )
    cot_high = lax.ppermute(
        lax.dynamic_index_in_dim(cotangent, slot_down, 0, keepdims=False), "dp", down
    )
    which = jnp.arange(slots, dtype=jnp.int32)[None, :] == segment[:, None]
    row_holder = jnp.sum(jnp.where(which, holder[None, :], 0), axis=1)
    row_slot = jnp.sum(jnp.where(which, slot_of[None, :], 0), axis=1)
    offset = row - begin
    pick_own = chosen(jnp.where(row_holder == 0, row_slot * span + offset, -1), slots * span)
    pick_low = chosen(jnp.where(row_holder == -1, offset, -1), span)
    pick_high = chosen(jnp.where(row_holder == 1, offset, -1), span)
    d_final = (
        dot_nn(pick_own, cotangent.reshape(-1, width))
        + dot_nn(pick_low, cot_low)
        + dot_nn(pick_high, cot_high)
    ).astype(BF)

    row_data = tokens.astype(F32)
    inverse1 = lax.rsqrt(jnp.mean(row_data * row_data, axis=1, keepdims=True) + EPSILON)
    normed1 = (row_data * inverse1 * attn_gain).astype(BF)
    query = dot_nn(normed1, w_query).astype(BF)
    key = dot_nn(normed1, w_key).astype(BF)
    value = dot_nn(normed1, w_value).astype(BF)
    house = dot_nn(normed1, w_house)
    logit = lax.dot_general(
        w_beta, normed1, (((0,), (1,)), ((), ())), preferred_element_type=F32
    )
    begin_col = begin[:, None]
    mixed, kept = mixer_forward(begin_col, logit, conv_taps, house, query, key, value)
    hidden = row_data + tensor_sum(dot_nn(mixed, w_out))
    inverse2 = lax.rsqrt(jnp.mean(hidden * hidden, axis=1, keepdims=True) + EPSILON)
    normed2 = (hidden * inverse2 * ffn_gain).astype(BF)
    gate = dot_nn(normed2, w_gate)
    lift = dot_nn(normed2, w_up)
    gate_sig = jax.nn.sigmoid(gate)
    gate_silu = gate * gate_sig
    inner = (gate_silu * lift).astype(BF)

    d_inner = dot_nt(d_final, w_down)
    d_gate = (d_inner * lift * gate_sig * (1.0 + gate * (1.0 - gate_sig))).astype(BF)
    d_up = (d_inner * gate_silu).astype(BF)
    bits_a = list(range(size.bit_length() - 1))
    bits_b = [1, 0] + bits_a[2:]
    order_a = shard_order(me, size, bits_a)
    order_b = shard_order(me, size, bits_b)
    first = size // 2

    def sharded(left):
        return left.T.reshape(size, block, left.shape[0])

    def scattered(left, right, order, bits):
        leave = wgrad(order[:first], left, right, BF)
        stay = wgrad(order[first:], left, right, BF)
        return scatter_sum(leave, stay, bits)

    d_final_t = sharded(d_final)
    normed2_t = sharded(normed2)
    middle = inner.shape[1] // 2
    g_gate = scattered(normed2_t, d_gate, order_a, bits_a)
    g_up = scattered(normed2_t, d_up, order_b, bits_b)
    g_down_a = scattered(d_final_t, inner[:, :middle], order_a, bits_a)
    g_down_b = scattered(d_final_t, inner[:, middle:], order_b, bits_b)
    d_norm2 = tensor_sum(dot_nt(d_gate, w_gate) + dot_nt(d_up, w_up))
    g_ffn_gain = jnp.sum(d_norm2 * hidden * inverse2, axis=0)
    d_hidden = d_final.astype(F32) + norm_back(d_norm2, hidden, inverse2, ffn_gain)
    d_branch = d_hidden.astype(BF)
    d_mixed = dot_nt(d_branch, w_out).astype(BF)
    d_branch_t = sharded(d_branch)
    middle = mixed.shape[1] // 2
    g_out_a = scattered(d_branch_t, mixed[:, :middle], order_a, bits_a)
    g_out_b = scattered(d_branch_t, mixed[:, middle:], order_b, bits_b)

    d_query, d_key, d_value, d_house, d_logit, g_taps = mixer_backward(
        begin_col, logit, conv_taps, house, query, key, value, d_mixed, kept
    )
    d_logit_b = d_logit.astype(BF)
    normed1_t = sharded(normed1)
    heads = d_logit.shape[0]
    extra = jnp.pad(d_logit_b.T, ((0, 0), (0, 128 - heads)))
    columns = query.shape[1]
    g_qk = scattered(
        normed1_t, jnp.concatenate([d_query, d_key], axis=1), order_a, bits_a
    )
    g_vhb = scattered(
        normed1_t, jnp.concatenate([d_value, d_house, extra], axis=1), order_b, bits_b
    )
    d_norm1_part = (
        dot_nt(d_query, w_query)
        + dot_nt(d_key, w_key)
        + dot_nt(d_value, w_value)
        + dot_nt(d_house, w_house)
        + lax.dot_general(d_logit_b, w_beta, (((0,), (1,)), ((), ())), preferred_element_type=F32)
    )
    d_norm1 = tensor_sum(d_norm1_part)
    g_attn_gain = jnp.sum(d_norm1 * row_data * inverse1, axis=0)
    input_grad = (d_hidden + norm_back(d_norm1, row_data, inverse1, attn_gain)).astype(BF)

    small = jnp.concatenate([g_taps.reshape(-1), g_attn_gain, g_ffn_gain]).reshape(-1, 128)
    for bit in bits_a:
        small = small + swap(small, "dp", bit)
    small = small.reshape(-1)
    taps_total = small[: g_taps.size].reshape(g_taps.shape)
    gains = small[g_taps.size :].reshape(2, width)
    gains = lax.dynamic_slice_in_dim(gains, me * block, block, axis=1)

    down_part = dot_nn(inner, w_down).astype(BF)
    final = (hidden + tensor_sum(down_part)).astype(BF)
    offsets = jnp.arange(span, dtype=jnp.int32)

    def to_neighbour(by):
        start = jnp.sum(jnp.where(holder == by, starts, 0))
        length = jnp.sum(jnp.where(holder == by, own, 0))
        return dot_nn(chosen(jnp.where(offsets < length, start + offsets, -1), rows), final).astype(BF)

    out_low = lax.ppermute(to_neighbour(1), "dp", up)
    out_high = lax.ppermute(to_neighbour(-1), "dp", down)
    mine = held_from == 0
    inside = jnp.where(mine, held % slots, 0)
    slot_start = jnp.where(mine, starts[inside], 0)
    slot_length = jnp.where(mine, own[inside], 0)
    pick = jnp.where(
        offsets[None, :] < slot_length[:, None], slot_start[:, None] + offsets[None, :], -1
    ).reshape(-1)
    kept_rows = dot_nn(chosen(pick, rows), final).astype(BF).reshape(slots, span, width)
    output = jnp.where(
        (held_from == -1)[:, None, None],
        out_low[None],
        jnp.where((held_from == 1)[:, None, None], out_high[None], kept_rows),
    )
    return (
        output,
        input_grad,
        gains[0],
        g_qk[:, :columns],
        g_qk[:, columns:],
        g_vhb[:, :columns],
        g_vhb[:, columns : 2 * columns],
        g_vhb[:, 2 * columns : 2 * columns + heads],
        taps_total,
        jnp.concatenate([g_out_a, g_out_b], axis=1).T,
        gains[1],
        g_gate,
        g_up,
        jnp.concatenate([g_down_a, g_down_b], axis=1).T,
    )


def solution(mesh):
    in_specs = (
        P("dp", None),
        P("dp", None, None),
        P(),
        P(),
        P(),
        P(None, "tensor"),
        P(None, "tensor"),
        P(None, "tensor"),
        P(None, "tensor"),
        P(None, "tensor"),
        P(None, "tensor"),
        P("tensor", None),
        P(),
        P(None, "tensor"),
        P(None, "tensor"),
        P("tensor", None),
    )
    out_specs = (
        P("dp", None, None),
        P("dp", None),
        P("dp"),
        P("dp", "tensor"),
        P("dp", "tensor"),
        P("dp", "tensor"),
        P("dp", "tensor"),
        P("dp", "tensor"),
        P(None, "tensor"),
        P("tensor", "dp"),
        P("dp"),
        P("dp", "tensor"),
        P("dp", "tensor"),
        P("tensor", "dp"),
    )
    return jax.shard_map(
        on_device, mesh=mesh, in_specs=in_specs, out_specs=out_specs, check_vma=False
    )
```

time: 2450 us -> 571 us (0.23)
  waiting for transfers between devices: 1490 us -> 201 us
  other arithmetic: 429 us -> 84.6 us
  matrix products: 315 us -> 86.8 us
  Pallas kernels: 0 us -> 99.2 us
  blocking collectives: 75.7 us -> 0 us
  local copies, waits for them, and re-layouts: 95.5 us -> 32.9 us
  starting transfers between devices: 15.4 us -> 54.6 us
    reduce_scatter x8 -> x0, waiting for transfers between devices: 1260 us -> none  [the longest x1 211 us: on_device(): lax.psum_scatter(g_gate, 'dp', scatter_dimension=0, tiled=True)]
    another operation x5 -> x0, other arithmetic: 357 us -> none  [the longest x4 357 us: path_mixer(): lax.linalg.triangular_solve(identity + coupling, house_key, left_side=Tru...]
    dot_general x45 -> x24, matrix products: 268 us -> 86.8 us  [the longest x14 49.6 us: dot_nn(): lax.dot_general(a, b, (((1,), (0,)), ((), ())), preferred_element_type=F32)]
    ppermute x4 -> x44, waiting for transfers between devices: 58.2 us -> 201 us  [the longest x40 179 us: swap(): return lax.ppermute(x, axis, [(i, i ^ 1 << bit) for i in range(size)])]
    unnamed x14 -> x0, waiting for transfers between devices: 110 us -> none
    pallas_call x0 -> x18, Pallas kernels: none -> 99.2 us  [the longest x16 46.6 us: wgrad(): pl.pallas_call(wgrad_kernel, grid_spec=pltpu.PrefetchScalarGridSpec(num_s...]
    unnamed x1 -> x0, blocking collectives: 75.7 us -> none
    psum x4 -> x0, waiting for transfers between devices: 59.6 us -> none  [the longest x1 25.6 us: on_device(): hidden = row_data + lax.psum(attn_part, 'tensor')]
  transfers between devices with their start and end apart: 17 -> 44, of which waited for: 14 -> 24; matrix products, arithmetic and copies ran while one was open for 5% -> 25% of each run, Pallas kernels for 0% -> 12%
where the time goes in v1:
time: 571 us; the launch traced here: 565 us
  waiting for transfers between devices  201 us (35%)
  Pallas kernels  99.2 us (17%)
  matrix products  86.8 us (15%)
  other arithmetic  84.6 us (15%)
  starting transfers between devices  54.6 us (10%)
  local copies, waits for them, and re-layouts  32.9 us (6%)
  between operations  5.77 us (1%)
    ppermute x40, waiting for transfers between devices, swap(): return lax.ppermute(x, axis, [(i, i ^ 1 << bit) for i in range(size)])  179 us
    dot_general x14, matrix products, dot_nn(): lax.dot_general(a, b, (((1,), (0,)), ((), ())), preferred_element_type=F32)  49.6 us
    pallas_call x16, Pallas kernels, wgrad(): pl.pallas_call(wgrad_kernel, grid_spec=pltpu.PrefetchScalarGridSpec(num_s...  46.6 us
    ppermute x40, starting transfers between devices, swap(): return lax.ppermute(x, axis, [(i, i ^ 1 << bit) for i in range(size)])  41.1 us
    convert_element_type x24, other arithmetic, scatter_sum(): out = sum((t[:half].astype(F32) for t in terms)).astype(BF)  36.5 us
    dot_general x8, matrix products, dot_nt(): lax.dot_general(a, b, (((1,), (1,)), ((), ())), preferred_element_type=F32)  32.4 us
    pallas_call x1, Pallas kernels, mixer_forward(): pl.pallas_call(functools.partial(forward_kernel, heads), grid=(count // h...  30.4 us
    pallas_call x1, Pallas kernels, mixer_backward(): pl.pallas_call(functools.partial(backward_kernel, heads), grid=(count //...  22.1 us
  transfers between devices with their start and end apart: 44, of which 24 were waited for; matrix products, arithmetic and copies ran while one was open for 25% of the time, Pallas kernels for 12%

profile of v1, /device:TPU:0, one launch (start us, length us, event | category | flops | bytes accessed | tf_op | source)
XLA Modules:
  0.0 565.0 jit_solution(13193861917519433419)
XLA Ops:
  5.3 2.6 convolution_bitcast_fusion.logit_ref
  8.0 2.6 fusion.34.house_ref
  12.9 2.3 convolution_convert_fusion.6.k_ref
  15.2 2.3 convolution_convert_fusion.5.v_ref
  17.5 30.4 %mixer_forward.1 = (bf16[512,768]{1,0:T(8,128)(2,1)}, bf16[6,8,256,256]{3,2,1,0:T(8,128)(2,1)}) custom-call(s32[512,1]{1,0:T(8,128)} %copy.44.begin_ref, f32[6,512]{1,0:T(8,128)} %convolution_bitcast_fusion.logit_ref, f32[4,768]{1,0:T(4,128)} %taps_ref.3, f32[512,768]{1,0:T(8,128)} %fusion.34.house_ref, bf16[512,768]{1,0:T(8,128)(2,1)} %convolution_convert_fusion.7.q_ref, ...), custom_call_target="tpu_custom_call" | custom-call | flops 60000002048 | bytes 16000000 | tf_op jit(solution)/shard_map/mixer_forward/pallas_call | solution.py:197
  48.0 4.2 fusion.46
  57.3 2.7 dynamic-slice_bitcast_fusion
  59.9 5.3 collective-permute-start.4
  74.0 3.1 fusion.14
  77.1 21.9 %collective-permute-done.4 = bf16[256,1536]{1,0:T(8,128)(2,1)} collective-permute-done((bf16[256,1536]{1,0:T(8,128)(2,1)}, bf16[256,1536]{1,0:T(8,128)(2,1)}, u32[]{:S(2)}, u32[]{:S(2)}) %collective-permute-start.4) | collective-permute-done | bytes 786464 | tf_op jit(solution)/shard_map/ppermute | solution.py:491
  100.9 2.9 fusion.12
  103.8 3.1 copy.50
  106.9 8.9 %fusion.48 = f32[512,2048]{1,0:T(8,128)} fusion(bf16[512,1536]{1,0:T(8,128)(2,1)} %fusion.12, bf16[2048,1536]{1,0:T(8,128)(2,1)} %param.31), kind=kOutput, calls=%fused_computation.177 | convolution fusion | flops 3221225472 | bytes 12058624 | tf_op jit(solution)/shard_map/dot_general | solution.py:19
  115.8 3.7 multiply_reduce_fusion.2
  119.5 9.1 %fusion.47 = f32[512,2048]{1,0:T(8,128)} fusion(bf16[1536,2048]{1,0:T(8,128)(2,1)} %param.30, f32[512,1536]{1,0:T(8,128)S(1)} %get-tuple-element.93, f32[1536]{0:T(1024)S(1)} %copy-done.57, f32[512]{0:T(512)S(1)} %get-tuple-element.118), kind=kOutput, calls=%fused_computation.176 | convolution fusion | flops 3223584768 | bytes 13639680 | tf_op jit(solution)/shard_map/dot_general | solution.py:15
  128.6 8.0 %multiply_convert_fusion = (bf16[512,2048]{1,0:T(8,128)(2,1)S(1)}, bf16[512,2048]{1,0:T(8,128)(2,1)S(1)}, bf16[512,2048]{1,0:T(8,128)(2,1)S(1)}) fusion(f32[512,2048]{1,0:T(8,128)} %fusion.48, f32[512,2048]{1,0:T(8,128)} %fusion.47, bf16[1536,2048]{1,0:T(8,128)(2,1)S(1)} %bitcast.95, f32[512,1536]{1,0:T(8,128)S(1)} %get-tuple-element.93, ...), kind=kOutput, calls=%fused_computation.8 | convolution fusion | flops 3239313408 | bytes 24125440 | tf_op jit(solution)/shard_map/dot_general | solution.py:15
  136.6 5.1 fusion.49
  147.1 2.4 collective-permute-start.36
  149.5 8.3 %convolution_add_fusion.6 = f32[512,1536]{1,0:T(8,128)} fusion(f32[512,1536]{1,0:T(8,128)} %fusion.49, bf16[512,2048]{1,0:T(8,128)(2,1)S(1)} %get-tuple-element.94.right_ref, bf16[1536,2048]{1,0:T(8,128)(2,1)} %param.30), kind=kOutput, calls=%fused_computation.22 | convolution fusion | flops 3222011904 | bytes 14680064 | tf_op jit(solution)/shard_map/dot_general | solution.py:19
  161.8 4.6 convolution_convert_fusion.1
  166.4 14.7 %collective-permute-done.40 = bf16[768,1024]{1,0:T(8,128)(2,1)S(1)} collective-permute-done((bf16[768,1024]{1,0:T(8,128)(2,1)S(1)}, bf16[768,1024]{1,0:T(8,128)(2,1)S(1)}, u32[]{:S(2)}, u32[]{:S(2)}) %collective-permute-start.40) | collective-permute-done | bytes 1572896 | tf_op jit(solution)/shard_map/ppermute | solution.py:401
  182.5 2.3 collective-permute-start.41
  188.6 2.7 copy.49
  194.2 4.4 wgrad.25
  200.4 3.3 wgrad.24
  205.3 4.3 wgrad.27
  214.2 3.3 wgrad.26
  217.5 5.4 collective-permute-done.42
  224.1 6.4 %collective-permute-done.38 = bf16[192,1024]{1,0:T(8,128)(2,1)S(1)} collective-permute-done((bf16[192,1024]{1,0:T(8,128)(2,1)S(1)}, bf16[192,1024]{1,0:T(8,128)(2,1)S(1)}, u32[]{:S(2)}, u32[]{:S(2)}) %collective-permute-start.38) | collective-permute-done | bytes 393248 | tf_op jit(solution)/shard_map/ppermute | solution.py:401
  230.5 2.6 collective-permute-start.43
  234.1 7.8 %collective-permute-done.43 = bf16[96,1024]{1,0:T(8,128)(2,1)S(1)} collective-permute-done((bf16[96,1024]{1,0:T(8,128)(2,1)S(1)}, bf16[96,1024]{1,0:T(8,128)(2,1)S(1)}, u32[]{:S(2)}, u32[]{:S(2)}) %collective-permute-start.43) | collective-permute-done | bytes 196640 | tf_op jit(solution)/shard_map/ppermute | solution.py:401
  243.0 9.8 %collective-permute-done.39 = bf16[96,1024]{1,0:T(8,128)(2,1)S(1)} collective-permute-done((bf16[96,1024]{1,0:T(8,128)(2,1)S(1)}, bf16[96,1024]{1,0:T(8,128)(2,1)S(1)}, u32[]{:S(2)}, u32[]{:S(2)}) %collective-permute-start.39) | collective-permute-done | bytes 196640 | tf_op jit(solution)/shard_map/ppermute | solution.py:401
  254.8 4.2 multiply_reduce_fusion
  259.0 5.4 convert_bitcast_fusion
  269.3 5.6 collective-permute-start.2
  274.9 2.4 convolution_convert_fusion.4.dm_ref
  277.3 22.1 %mixer_backward.1 = (bf16[512,768]{1,0:T(8,128)(2,1)}, bf16[512,768]{1,0:T(8,128)(2,1)}, bf16[512,768]{1,0:T(8,128)(2,1)}, bf16[512,768]{1,0:T(8,128)(2,1)}, f32[6,512]{1,0:T(8,128)}, /*index=5*/f32[4,768]{1,0:T(4,128)}) custom-call(s32[512,1]{1,0:T(8,128)} %copy.44.begin_ref, f32[6,512]{1,0:T(8,128)} %convolution_bitcast_fusion.logit_ref, ...), custom_call_target="tpu_custom_call" | custom-call | flops 60000002048 | bytes 20000000 | tf_op jit(solution)/shard_map/mixer_backward/pallas_call | solution.py:343
  300.3 3.5 fusion.50
  317.3 2.8 convolution_convert_fusion
  320.2 3.3 add_convert_fusion.1
  325.7 3.3 add_convert_fusion
  332.8 3.4 collective-permute-done.24
  344.3 3.4 select_select_fusion
  347.7 34.5 %collective-permute-done.25 = bf16[384,384]{1,0:T(8,128)(2,1)S(1)} collective-permute-done((bf16[384,384]{1,0:T(8,128)(2,1)S(1)}, bf16[384,384]{1,0:T(8,128)(2,1)S(1)}, u32[]{:S(2)}, u32[]{:S(2)}) %collective-permute-start.25) | collective-permute-done | bytes 294944 | tf_op jit(solution)/shard_map/ppermute | solution.py:401
  386.2 3.1 collective-permute-done.26
  399.8 3.2 add_convert_fusion.8
  404.7 2.6 add_convert_fusion.7
  409.0 4.0 fusion.11
  413.0 4.8 fusion.30
  420.9 2.6 wgrad.17
  424.3 6.1 %wgrad.19 = bf16[768,1664]{1,0:T(8,128)(2,1)S(1)} custom-call(s32[8]{0:T(128)S(1)} %get-tuple-element.122.order_ref, bf16[16,96,512]{2,1,0:T(8,128)(2,1)S(1)} %bitcast.78, bf16[512,1664]{1,0:T(8,128)(2,1)S(1)} %fusion.13.right_ref), custom_call_target="tpu_custom_call" | custom-call | flops 1308622848 | bytes 5832704 | tf_op jit(solution)/shard_map/wgrad/pallas_call | solution.py:376
  434.9 5.4 collective-permute-done.34
  441.9 2.8 collective-permute-start.8
  444.7 16.2 %collective-permute-done.31 = bf16[96,2048]{1,0:T(8,128)(2,1)S(1)} collective-permute-done((bf16[96,2048]{1,0:T(8,128)(2,1)S(1)}, bf16[96,2048]{1,0:T(8,128)(2,1)S(1)}, u32[]{:S(2)}, u32[]{:S(2)}) %collective-permute-start.31) | collective-permute-done | bytes 393248 | tf_op jit(solution)/shard_map/ppermute | solution.py:401
  461.0 2.4 convert_add_fusion.2
  463.4 10.8 %collective-permute-done.8 = f32[48,128]{1,0:T(8,128)S(1)} collective-permute-done((f32[48,128]{1,0:T(8,128)S(1)}, f32[48,128]{1,0:T(8,128)S(1)}, u32[]{:S(2)}, u32[]{:S(2)}) %collective-permute-start.8) | collective-permute-done | bytes 24608 | tf_op jit(solution)/shard_map/ppermute | solution.py:401
  474.7 6.0 %wgrad.18 = bf16[768,1664]{1,0:T(8,128)(2,1)S(1)} custom-call(s32[8]{0:T(128)S(1)} %get-tuple-element.121.order_ref, bf16[16,96,512]{2,1,0:T(8,128)(2,1)S(1)} %bitcast.79, bf16[512,1664]{1,0:T(8,128)(2,1)S(1)} %fusion.13.right_ref), custom_call_target="tpu_custom_call" | custom-call | flops 1308622848 | bytes 5832704 | tf_op jit(solution)/shard_map/wgrad/pallas_call | solution.py:376
  480.7 3.9 collective-permute-done.9
  485.9 2.8 wgrad.16
  494.2 2.4 convert_add_fusion.1
  497.3 18.6 %collective-permute-done.13 = bf16[384,1536]{1,0:T(8,128)(2,1)} collective-permute-done((bf16[384,1536]{1,0:T(8,128)(2,1)}, bf16[384,1536]{1,0:T(8,128)(2,1)}, u32[]{:S(2)}, u32[]{:S(2)}) %collective-permute-start.13) | collective-permute-done | bytes 1179680 | tf_op jit(solution)/shard_map/ppermute | solution.py:401
  522.1 14.8 %collective-permute-done.14 = bf16[192,1536]{1,0:T(8,128)(2,1)S(1)} collective-permute-done((bf16[192,1536]{1,0:T(8,128)(2,1)S(1)}, bf16[192,1536]{1,0:T(8,128)(2,1)S(1)}, u32[]{:S(2)}, u32[]{:S(2)}) %collective-permute-start.14) | collective-permute-done | bytes 589856 | tf_op jit(solution)/shard_map/ppermute | solution.py:401
  538.3 7.4 %collective-permute-done.18 = bf16[192,1664]{1,0:T(8,128)(2,1)S(1)} collective-permute-done((bf16[192,1664]{1,0:T(8,128)(2,1)S(1)}, bf16[192,1664]{1,0:T(8,128)(2,1)S(1)}, u32[]{:S(2)}, u32[]{:S(2)}) %collective-permute-start.18) | collective-permute-done | bytes 639008 | tf_op jit(solution)/shard_map/ppermute | solution.py:401
  548.8 9.6 %collective-permute-done.15 = bf16[96,1536]{1,0:T(8,128)(2,1)S(1)} collective-permute-done((bf16[96,1536]{1,0:T(8,128)(2,1)S(1)}, bf16[96,1536]{1,0:T(8,128)(2,1)S(1)}, u32[]{:S(2)}, u32[]{:S(2)}) %collective-permute-start.15) | collective-permute-done | bytes 294944 | tf_op jit(solution)/shard_map/ppermute | solution.py:401
  (311 shorter events, 135.4 us)
Async XLA Ops:
  0.6 47.3 %copy-start = (bf16[768,1536]{1,0:T(8,128)(2,1)S(1)}, bf16[768,1536]{1,0:T(8,128)(2,1)}, u32[]{:S(2)}) copy-start(bf16[768,1536]{1,0:T(8,128)(2,1)} %param.27) | copy-start | bytes 7077892
  5.3 9.9 %copy-start.61 = (f32[512]{0:T(512)}, f32[512]{0:T(512)S(1)}, u32[]{:S(2)}) copy-start(f32[512]{0:T(512)S(1)} %get-tuple-element.116) | copy-start | bytes 6148
  52.2 63.6 %collective-permute-start = (f32[512,1536]{1,0:T(8,128)}, f32[512,1536]{1,0:T(8,128)}, u32[]{:S(2)}, u32[]{:S(2)}) collective-permute-start(f32[512,1536]{1,0:T(8,128)} %fusion.46), channel_id=1, source_target_pairs={{0,1},{1,0},{2,3},{3,2},{4,5},{5,4},{6,7},{7,6},{8,9},{9,8},{10,11... | collective-permute-start | bytes 9437192 | tf_op jit(solution)/shard_map/ppermute | solution.py:401
  59.9 39.0 %collective-permute-start.4 = (bf16[256,1536]{1,0:T(8,128)(2,1)}, bf16[256,1536]{1,0:T(8,128)(2,1)}, u32[]{:S(2)}, u32[]{:S(2)}) collective-permute-start(bf16[256,1536]{1,0:T(8,128)(2,1)} %get-tuple-element.99), channel_id=1, source_target_pairs={{0,2},{2,4},{4,6},{6,8},{8,10},{10,12},{12,14},{14,16},{16,18},{18... | collective-permute-start | bytes 2359304 | tf_op jit(solution)/shard_map/ppermute | solution.py:491
  65.2 35.7 %collective-permute-start.5 = (bf16[256,1536]{1,0:T(8,128)(2,1)}, bf16[256,1536]{1,0:T(8,128)(2,1)}, u32[]{:S(2)}, u32[]{:S(2)}) collective-permute-start(bf16[256,1536]{1,0:T(8,128)(2,1)} %get-tuple-element.98), channel_id=1, source_target_pairs={{2,0},{4,2},{6,4},{8,6},{10,8},{12,10},{14,12},{16,14},{18,16},{20... | collective-permute-start | bytes 2359304 | tf_op jit(solution)/shard_map/ppermute | solution.py:494
  115.8 12.8 %slice-start = ((s8[6291456]{0:T(1024)(128)(4,1)}), s8[4194304]{0:T(1024)(128)(4,1)S(1)}, s32[]{:S(2)}) async-start(s8[6291456]{0:T(1024)(128)(4,1)} %bitcast.94), calls=%async_computation | async-start | bytes 8388608
  119.5 67.6 %copy-start.21 = (f32[512,1536]{1,0:T(8,128)}, f32[512,1536]{1,0:T(8,128)S(1)}, u32[]{:S(2)}) copy-start(f32[512,1536]{1,0:T(8,128)S(1)} %get-tuple-element.93) | copy-start | bytes 9437188
  136.6 12.9 %copy-start.13 = (bf16[512,2048]{1,0:T(8,128)(2,1)}, bf16[512,2048]{1,0:T(8,128)(2,1)S(1)}, u32[]{:S(2)}) copy-start(bf16[512,2048]{1,0:T(8,128)(2,1)S(1)} %get-tuple-element.94.right_ref) | copy-start | bytes 6291460
  143.1 18.7 %slice-start.2 = ((s8[6291456]{0:T(1024)(128)(4,1)}), s8[4194304]{0:T(1024)(128)(4,1)S(1)}, s32[]{:S(2)}) async-start(s8[6291456]{0:T(1024)(128)(4,1)} %bitcast.96), calls=%async_computation.2 | async-start | bytes 8388608
  145.1 36.1 %collective-permute-start.40 = (bf16[768,1024]{1,0:T(8,128)(2,1)S(1)}, bf16[768,1024]{1,0:T(8,128)(2,1)S(1)}, u32[]{:S(2)}, u32[]{:S(2)}) collective-permute-start(bf16[768,1024]{1,0:T(8,128)(2,1)S(1)} %wgrad.31), channel_id=1, source_target_pairs={{0,4},{2,6},{4,0},{6,2},{8,12},{10,14},{12,8},{14,10},{16,20},{18,... | collective-permute-start | bytes 4718600 | tf_op jit(solution)/shard_map/ppermute | solution.py:401
  147.1 37.8 %collective-permute-start.36 = (bf16[768,1024]{1,0:T(8,128)(2,1)S(1)}, bf16[768,1024]{1,0:T(8,128)(2,1)S(1)}, u32[]{:S(2)}, u32[]{:S(2)}) collective-permute-start(bf16[768,1024]{1,0:T(8,128)(2,1)S(1)} %wgrad.29), channel_id=1, source_target_pairs={{0,2},{2,0},{4,6},{6,4},{8,10},{10,8},{12,14},{14,12},{16,18},{18,... | collective-permute-start | bytes 4718600 | tf_op jit(solution)/shard_map/ppermute | solution.py:401
  149.5 12.3 %slice-start.3 = ((s8[6291456]{0:T(1024)(128)(4,1)}), s8[2097152]{0:T(1024)(128)(4,1)S(1)}, s32[]{:S(2)}) async-start(s8[6291456]{0:T(1024)(128)(4,1)} %bitcast.96), calls=%async_computation.3 | async-start | bytes 4194304
  157.9 97.0 %collective-permute-start.6 = (f32[512,1536]{1,0:T(8,128)}, f32[512,1536]{1,0:T(8,128)}, u32[]{:S(2)}, u32[]{:S(2)}) collective-permute-start(f32[512,1536]{1,0:T(8,128)} %convolution_add_fusion.6), channel_id=1, source_target_pairs={{0,1},{1,0},{2,3},{3,2},{4,5},{5,4},{6,7},{7,6},{8,9},{9,8},{10,11... | collective-permute-start | bytes 9437192 | tf_op jit(solution)/shard_map/ppermute | solution.py:401
  159.8 21.3 %copy-start.19 = (bf16[768,1024]{1,0:T(8,128)(2,1)}, bf16[768,1024]{1,0:T(8,128)(2,1)S(1)}, u32[]{:S(2)}) copy-start(bf16[768,1024]{1,0:T(8,128)(2,1)S(1)} %wgrad.30) | copy-start | bytes 4718596
  161.8 23.1 %copy-start.17 = (bf16[768,1024]{1,0:T(8,128)(2,1)}, bf16[768,1024]{1,0:T(8,128)(2,1)S(1)}, u32[]{:S(2)}) copy-start(bf16[768,1024]{1,0:T(8,128)(2,1)S(1)} %wgrad.28) | copy-start | bytes 4718596
  182.5 27.1 %collective-permute-start.41 = (bf16[384,1024]{1,0:T(8,128)(2,1)}, bf16[384,1024]{1,0:T(8,128)(2,1)}, u32[]{:S(2)}, u32[]{:S(2)}) collective-permute-start(bf16[384,1024]{1,0:T(8,128)(2,1)} %add_convert_fusion.5), channel_id=1, source_target_pairs={{0,2},{2,0},{4,6},{6,4},{8,10},{10,8},{12,14},{14,12},{16,18},{18,... | collective-permute-start | bytes 2359304 | tf_op jit(solution)/shard_map/ppermute | solution.py:401
  186.3 26.1 %collective-permute-start.37 = (bf16[384,1024]{1,0:T(8,128)(2,1)}, bf16[384,1024]{1,0:T(8,128)(2,1)}, u32[]{:S(2)}, u32[]{:S(2)}) collective-permute-start(bf16[384,1024]{1,0:T(8,128)(2,1)} %add_convert_fusion.6), channel_id=1, source_target_pairs={{0,4},{2,6},{4,0},{6,2},{8,12},{10,14},{12,8},{14,10},{16,20},{18,... | collective-permute-start | bytes 2359304 | tf_op jit(solution)/shard_map/ppermute | solution.py:401
  188.6 70.5 %collective-permute-start.1 = (bf16[512,1536]{1,0:T(8,128)(2,1)}, bf16[512,1536]{1,0:T(8,128)(2,1)}, u32[]{:S(2)}, u32[]{:S(2)}) collective-permute-start(bf16[512,1536]{1,0:T(8,128)(2,1)} %convolution_convert_fusion.1), channel_id=1, source_target_pairs={{0,1},{1,0},{2,3},{3,2},{4,5},{5,4},{6,7},{7,6},{8,9},{9,8},{10,11... | collective-permute-start | bytes 4718600 | tf_op jit(solution)/shard_map/ppermute | solution.py:401
  198.6 121.5 %collective-permute-start.28 = (bf16[768,2048]{1,0:T(8,128)(2,1)}, bf16[768,2048]{1,0:T(8,128)(2,1)}, u32[]{:S(2)}, u32[]{:S(2)}) collective-permute-start(bf16[768,2048]{1,0:T(8,128)(2,1)} %wgrad.25), channel_id=1, source_target_pairs={{0,2},{2,0},{4,6},{6,4},{8,10},{10,8},{12,14},{14,12},{16,18},{18,... | collective-permute-start | bytes 9437192 | tf_op jit(solution)/shard_map/ppermute | solution.py:401
  210.8 12.0 %collective-permute-start.42 = (bf16[192,1024]{1,0:T(8,128)(2,1)S(1)}, bf16[192,1024]{1,0:T(8,128)(2,1)S(1)}, u32[]{:S(2)}, u32[]{:S(2)}) collective-permute-start(bf16[192,1024]{1,0:T(8,128)(2,1)S(1)} %add_convert_fusion.11), channel_id=1, source_target_pairs={{0,8},{2,10},{4,12},{6,14},{8,0},{10,2},{12,4},{14,6},{16,24},{18,... | collective-permute-start | bytes 1179656 | tf_op jit(solution)/shard_map/ppermute | solution.py:401
  213.6 16.9 %collective-permute-start.38 = (bf16[192,1024]{1,0:T(8,128)(2,1)S(1)}, bf16[192,1024]{1,0:T(8,128)(2,1)S(1)}, u32[]{:S(2)}, u32[]{:S(2)}) collective-permute-start(bf16[192,1024]{1,0:T(8,128)(2,1)S(1)} %add_convert_fusion.12), channel_id=1, source_target_pairs={{0,8},{2,10},{4,12},{6,14},{8,0},{10,2},{12,4},{14,6},{16,24},{18,... | collective-permute-start | bytes 1179656 | tf_op jit(solution)/shard_map/ppermute | solution.py:401
  217.5 37.3 %copy-start.4 = (bf16[768,2048]{1,0:T(8,128)(2,1)}, bf16[768,2048]{1,0:T(8,128)(2,1)S(1)}, u32[]{:S(2)}) copy-start(bf16[768,2048]{1,0:T(8,128)(2,1)S(1)} %wgrad.26) | copy-start | bytes 9437188
  222.8 100.6 %collective-permute-start.32 = (bf16[768,2048]{1,0:T(8,128)(2,1)}, bf16[768,2048]{1,0:T(8,128)(2,1)}, u32[]{:S(2)}, u32[]{:S(2)}) collective-permute-start(bf16[768,2048]{1,0:T(8,128)(2,1)} %wgrad.27), channel_id=1, source_target_pairs={{0,4},{2,6},{4,0},{6,2},{8,12},{10,14},{12,8},{14,10},{16,20},{18,... | collective-permute-start | bytes 9437192 | tf_op jit(solution)/shard_map/ppermute | solution.py:401
  230.5 11.4 %collective-permute-start.43 = (bf16[96,1024]{1,0:T(8,128)(2,1)S(1)}, bf16[96,1024]{1,0:T(8,128)(2,1)S(1)}, u32[]{:S(2)}, u32[]{:S(2)}) collective-permute-start(bf16[96,1024]{1,0:T(8,128)(2,1)S(1)} %add_convert_fusion.19), channel_id=1, source_target_pairs={{0,16},{2,18},{4,20},{6,22},{8,24},{10,26},{12,28},{14,30},{16,0},... | collective-permute-start | bytes 589832 | tf_op jit(solution)/shard_map/ppermute | solution.py:401
  234.1 20.7 %copy-start.22 = (f32[512,1536]{1,0:T(8,128)S(1)}, f32[512,1536]{1,0:T(8,128)}, u32[]{:S(2)}) copy-start(f32[512,1536]{1,0:T(8,128)} %copy-done.21) | copy-start | bytes 9437188
  241.9 10.9 %collective-permute-start.39 = (bf16[96,1024]{1,0:T(8,128)(2,1)S(1)}, bf16[96,1024]{1,0:T(8,128)(2,1)S(1)}, u32[]{:S(2)}, u32[]{:S(2)}) collective-permute-start(bf16[96,1024]{1,0:T(8,128)(2,1)S(1)} %add_convert_fusion.20), channel_id=1, source_target_pairs={{0,16},{2,18},{4,20},{6,22},{8,24},{10,26},{12,28},{14,30},{16,0},... | collective-permute-start | bytes 589832 | tf_op jit(solution)/shard_map/ppermute | solution.py:401
  264.4 10.5 %copy-start.29 = (f32[512,1536]{1,0:T(8,128)}, f32[512,1536]{1,0:T(8,128)S(1)}, u32[]{:S(2)}) copy-start(f32[512,1536]{1,0:T(8,128)S(1)} %get-tuple-element.89) | copy-start | bytes 9437188
  266.4 76.1 %collective-permute-start.3 = (bf16[256,1536]{1,0:T(8,128)(2,1)}, bf16[256,1536]{1,0:T(8,128)(2,1)}, u32[]{:S(2)}, u32[]{:S(2)}) collective-permute-start(bf16[256,1536]{1,0:T(8,128)(2,1)} %convolution_convert_fusion.2), channel_id=1, source_target_pairs={{2,0},{4,2},{6,4},{8,6},{10,8},{12,10},{14,12},{16,14},{18,16},{20... | collective-permute-start | bytes 2359304 | tf_op jit(solution)/shard_map/ppermute | solution.py:608
  269.3 73.7 %collective-permute-start.2 = (bf16[256,1536]{1,0:T(8,128)(2,1)}, bf16[256,1536]{1,0:T(8,128)(2,1)}, u32[]{:S(2)}, u32[]{:S(2)}) collective-permute-start(bf16[256,1536]{1,0:T(8,128)(2,1)} %convolution_convert_fusion.3), channel_id=1, source_target_pairs={{0,2},{2,4},{4,6},{6,8},{8,10},{10,12},{12,14},{14,16},{16,18},{18... | collective-permute-start | bytes 2359304 | tf_op jit(solution)/shard_map/ppermute | solution.py:607
  311.3 97.7 %collective-permute-start.7 = (f32[512,1536]{1,0:T(8,128)}, f32[512,1536]{1,0:T(8,128)}, u32[]{:S(2)}, u32[]{:S(2)}) collective-permute-start(f32[512,1536]{1,0:T(8,128)} %convolution_add_fusion), channel_id=1, source_target_pairs={{0,1},{1,0},{2,3},{3,2},{4,5},{5,4},{6,7},{7,6},{8,9},{9,8},{10,11... | collective-permute-start | bytes 9437192 | tf_op jit(solution)/shard_map/ppermute | solution.py:401
  320.2 16.1 %collective-permute-start.24 = (bf16[768,384]{1,0:T(8,128)(2,1)}, bf16[768,384]{1,0:T(8,128)(2,1)}, u32[]{:S(2)}, u32[]{:S(2)}) collective-permute-start(bf16[768,384]{1,0:T(8,128)(2,1)} %wgrad.23), channel_id=1, source_target_pairs={{0,4},{2,6},{4,0},{6,2},{8,12},{10,14},{12,8},{14,10},{16,20},{18,... | collective-permute-start | bytes 1769480 | tf_op jit(solution)/shard_map/ppermute | solution.py:401
  323.5 16.3 %collective-permute-start.20 = (bf16[768,384]{1,0:T(8,128)(2,1)}, bf16[768,384]{1,0:T(8,128)(2,1)}, u32[]{:S(2)}, u32[]{:S(2)}) collective-permute-start(bf16[768,384]{1,0:T(8,128)(2,1)} %wgrad.21), channel_id=1, source_target_pairs={{0,2},{2,0},{4,6},{6,4},{8,10},{10,8},{12,14},{14,12},{16,18},{18,... | collective-permute-start | bytes 1769480 | tf_op jit(solution)/shard_map/ppermute | solution.py:401
  332.6 11.7 %copy-start.38 = (bf16[768,1536]{1,0:T(8,128)(2,1)S(1)}, bf16[768,1536]{1,0:T(8,128)(2,1)}, u32[]{:S(2)}) copy-start(bf16[768,1536]{1,0:T(8,128)(2,1)} %convolution_convert_fusion) | copy-start | bytes 7077892
  332.6 11.7 %copy-start.67 = (pred[3]{0:T(512)(128)(4,1)S(1)}, pred[3]{0:T(512)(128)(4,1)}, u32[]{:S(2)}) copy-start(pred[3]{0:T(512)(128)(4,1)} %get-tuple-element.126) | copy-start | bytes 13
  332.6 11.7 %copy-start.68 = (pred[3]{0:T(512)(128)(4,1)S(1)}, pred[3]{0:T(512)(128)(4,1)}, u32[]{:S(2)}) copy-start(pred[3]{0:T(512)(128)(4,1)} %get-tuple-element.127) | copy-start | bytes 13
  336.2 63.6 %collective-permute-start.29 = (bf16[384,2048]{1,0:T(8,128)(2,1)S(1)}, bf16[384,2048]{1,0:T(8,128)(2,1)S(1)}, u32[]{:S(2)}, u32[]{:S(2)}) collective-permute-start(bf16[384,2048]{1,0:T(8,128)(2,1)S(1)} %copy-done.45), channel_id=1, source_target_pairs={{0,4},{2,6},{4,0},{6,2},{8,12},{10,14},{12,8},{14,10},{16,20},{18,... | collective-permute-start | bytes 4718600 | tf_op jit(solution)/shard_map/ppermute | solution.py:401
  339.8 63.8 %collective-permute-start.33 = (bf16[384,2048]{1,0:T(8,128)(2,1)S(1)}, bf16[384,2048]{1,0:T(8,128)(2,1)S(1)}, u32[]{:S(2)}, u32[]{:S(2)}) collective-permute-start(bf16[384,2048]{1,0:T(8,128)(2,1)S(1)} %copy-done.46), channel_id=1, source_target_pairs={{0,2},{2,0},{4,6},{6,4},{8,10},{10,8},{12,14},{14,12},{16,18},{18,... | collective-permute-start | bytes 4718600 | tf_op jit(solution)/shard_map/ppermute | solution.py:401
  342.6 39.5 %collective-permute-start.25 = (bf16[384,384]{1,0:T(8,128)(2,1)S(1)}, bf16[384,384]{1,0:T(8,128)(2,1)S(1)}, u32[]{:S(2)}, u32[]{:S(2)}) collective-permute-start(bf16[384,384]{1,0:T(8,128)(2,1)S(1)} %add_convert_fusion.16), channel_id=1, source_target_pairs={{0,2},{2,0},{4,6},{6,4},{8,10},{10,8},{12,14},{14,12},{16,18},{18,... | collective-permute-start | bytes 884744 | tf_op jit(solution)/shard_map/ppermute | solution.py:401
  342.9 40.3 %collective-permute-start.21 = (bf16[384,384]{1,0:T(8,128)(2,1)S(1)}, bf16[384,384]{1,0:T(8,128)(2,1)S(1)}, u32[]{:S(2)}, u32[]{:S(2)}) collective-permute-start(bf16[384,384]{1,0:T(8,128)(2,1)S(1)} %add_convert_fusion.17), channel_id=1, source_target_pairs={{0,4},{2,6},{4,0},{6,2},{8,12},{10,14},{12,8},{14,10},{16,20},{18,... | collective-permute-start | bytes 884744 | tf_op jit(solution)/shard_map/ppermute | solution.py:401
  383.1 6.2 %collective-permute-start.26 = (bf16[192,384]{1,0:T(8,128)(2,1)S(1)}, bf16[192,384]{1,0:T(8,128)(2,1)S(1)}, u32[]{:S(2)}, u32[]{:S(2)}) collective-permute-start(bf16[192,384]{1,0:T(8,128)(2,1)S(1)} %add_convert_fusion.21), channel_id=1, source_target_pairs={{0,8},{2,10},{4,12},{6,14},{8,0},{10,2},{12,4},{14,6},{16,24},{18,... | collective-permute-start | bytes 442376 | tf_op jit(solution)/shard_map/ppermute | solution.py:401
  384.2 6.9 %collective-permute-start.22 = (bf16[192,384]{1,0:T(8,128)(2,1)S(1)}, bf16[192,384]{1,0:T(8,128)(2,1)S(1)}, u32[]{:S(2)}, u32[]{:S(2)}) collective-permute-start(bf16[192,384]{1,0:T(8,128)(2,1)S(1)} %add_convert_fusion.22), channel_id=1, source_target_pairs={{0,8},{2,10},{4,12},{6,14},{8,0},{10,2},{12,4},{14,6},{16,24},{18,... | collective-permute-start | bytes 442376 | tf_op jit(solution)/shard_map/ppermute | solution.py:401
  390.3 6.2 %collective-permute-start.27 = (bf16[96,384]{1,0:T(8,128)(2,1)S(1)}, bf16[96,384]{1,0:T(8,128)(2,1)S(1)}, u32[]{:S(2)}, u32[]{:S(2)}) collective-permute-start(bf16[96,384]{1,0:T(8,128)(2,1)S(1)} %add_convert_fusion.23), channel_id=1, source_target_pairs={{0,16},{2,18},{4,20},{6,22},{8,24},{10,26},{12,28},{14,30},{16,0},... | collective-permute-start | bytes 221192 | tf_op jit(solution)/shard_map/ppermute | solution.py:401
  392.0 6.1 %collective-permute-start.23 = (bf16[96,384]{1,0:T(8,128)(2,1)S(1)}, bf16[96,384]{1,0:T(8,128)(2,1)S(1)}, u32[]{:S(2)}, u32[]{:S(2)}) collective-permute-start(bf16[96,384]{1,0:T(8,128)(2,1)S(1)} %add_convert_fusion.24), channel_id=1, source_target_pairs={{0,16},{2,18},{4,20},{6,22},{8,24},{10,26},{12,28},{14,30},{16,0},... | collective-permute-start | bytes 221192 | tf_op jit(solution)/shard_map/ppermute | solution.py:401
  399.8 9.2 %copy-start.62 = (f32[512]{0:T(512)S(1)}, f32[512]{0:T(512)}, u32[]{:S(2)}) copy-start(f32[512]{0:T(512)} %copy-done.61) | copy-start | bytes 6148
  403.1 28.8 %collective-permute-start.30 = (bf16[192,2048]{1,0:T(8,128)(2,1)}, bf16[192,2048]{1,0:T(8,128)(2,1)}, u32[]{:S(2)}, u32[]{:S(2)}) collective-permute-start(bf16[192,2048]{1,0:T(8,128)(2,1)} %add_convert_fusion.8), channel_id=1, source_target_pairs={{0,8},{2,10},{4,12},{6,14},{8,0},{10,2},{12,4},{14,6},{16,24},{18,... | collective-permute-start | bytes 2359304 | tf_op jit(solution)/shard_map/ppermute | solution.py:401
  407.4 33.0 %collective-permute-start.34 = (bf16[192,2048]{1,0:T(8,128)(2,1)}, bf16[192,2048]{1,0:T(8,128)(2,1)}, u32[]{:S(2)}, u32[]{:S(2)}) collective-permute-start(bf16[192,2048]{1,0:T(8,128)(2,1)} %add_convert_fusion.7), channel_id=1, source_target_pairs={{0,8},{2,10},{4,12},{6,14},{8,0},{10,2},{12,4},{14,6},{16,24},{18,... | collective-permute-start | bytes 2359304 | tf_op jit(solution)/shard_map/ppermute | solution.py:401
  423.6 16.8 %copy-start.52 = (bf16[384,2048]{1,0:T(8,128)(2,1)S(1)}, bf16[384,2048]{1,0:T(8,128)(2,1)}, u32[]{:S(2)}) copy-start(bf16[384,2048]{1,0:T(8,128)(2,1)} %copy-done.51) | copy-start | bytes 4718596
  423.6 67.2 %collective-permute-start.12 = (bf16[768,1536]{1,0:T(8,128)(2,1)S(1)}, bf16[768,1536]{1,0:T(8,128)(2,1)S(1)}, u32[]{:S(2)}, u32[]{:S(2)}) collective-permute-start(bf16[768,1536]{1,0:T(8,128)(2,1)S(1)} %wgrad.17), channel_id=1, source_target_pairs={{0,2},{2,0},{4,6},{6,4},{8,10},{10,8},{12,14},{14,12},{16,18},{18,... | collective-permute-start | bytes 7077896 | tf_op jit(solution)/shard_map/ppermute | solution.py:401
  430.4 62.2 %collective-permute-start.16 = (bf16[768,1664]{1,0:T(8,128)(2,1)S(1)}, bf16[768,1664]{1,0:T(8,128)(2,1)S(1)}, u32[]{:S(2)}, u32[]{:S(2)}) collective-permute-start(bf16[768,1664]{1,0:T(8,128)(2,1)S(1)} %wgrad.19), channel_id=1, source_target_pairs={{0,4},{2,6},{4,0},{6,2},{8,12},{10,14},{12,8},{14,10},{16,20},{18,... | collective-permute-start | bytes 7667720 | tf_op jit(solution)/shard_map/ppermute | solution.py:401
  433.3 27.6 %collective-permute-start.31 = (bf16[96,2048]{1,0:T(8,128)(2,1)S(1)}, bf16[96,2048]{1,0:T(8,128)(2,1)S(1)}, u32[]{:S(2)}, u32[]{:S(2)}) collective-permute-start(bf16[96,2048]{1,0:T(8,128)(2,1)S(1)} %add_convert_fusion.14), channel_id=1, source_target_pairs={{0,16},{2,18},{4,20},{6,22},{8,24},{10,26},{12,28},{14,30},{16,0},... | collective-permute-start | bytes 1179656 | tf_op jit(solution)/shard_map/ppermute | solution.py:401
  441.9 52.3 %collective-permute-start.35 = (bf16[96,2048]{1,0:T(8,128)(2,1)S(1)}, bf16[96,2048]{1,0:T(8,128)(2,1)S(1)}, u32[]{:S(2)}, u32[]{:S(2)}) collective-permute-start(bf16[96,2048]{1,0:T(8,128)(2,1)S(1)} %add_convert_fusion.13), channel_id=1, source_target_pairs={{0,16},{2,18},{4,20},{6,22},{8,24},{10,26},{12,28},{14,30},{16,0},... | collective-permute-start | bytes 1179656 | tf_op jit(solution)/shard_map/ppermute | solution.py:401
  441.9 32.2 %collective-permute-start.8 = (f32[48,128]{1,0:T(8,128)S(1)}, f32[48,128]{1,0:T(8,128)S(1)}, u32[]{:S(2)}, u32[]{:S(2)}) collective-permute-start(f32[48,128]{1,0:T(8,128)S(1)} %maximum_bitcast_fusion.2), channel_id=1, source_target_pairs={{0,2},{2,0},{4,6},{6,4},{8,10},{10,8},{12,14},{14,12},{16,18},{18,... | collective-permute-start | bytes 73736 | tf_op jit(solution)/shard_map/ppermute | solution.py:401
  474.2 11.8 %copy-start.11 = (bf16[512,1536]{1,0:T(8,128)(2,1)S(1)}, bf16[512,1536]{1,0:T(8,128)(2,1)}, u32[]{:S(2)}) copy-start(bf16[512,1536]{1,0:T(8,128)(2,1)} %copy-done.9) | copy-start | bytes 4718596
  474.2 10.5 %collective-permute-start.9 = (f32[48,128]{1,0:T(8,128)S(1)}, f32[48,128]{1,0:T(8,128)S(1)}, u32[]{:S(2)}, u32[]{:S(2)}) collective-permute-start(f32[48,128]{1,0:T(8,128)S(1)} %fusion.88), channel_id=1, source_target_pairs={{0,4},{2,6},{4,0},{6,2},{8,12},{10,14},{12,8},{14,10},{16,20},{18,... | collective-permute-start | bytes 73736 | tf_op jit(solution)/shard_map/ppermute | solution.py:401
  480.7 11.9 %copy-start.8 = (bf16[768,1664]{1,0:T(8,128)(2,1)}, bf16[768,1664]{1,0:T(8,128)(2,1)S(1)}, u32[]{:S(2)}) copy-start(bf16[768,1664]{1,0:T(8,128)(2,1)S(1)} %wgrad.18) | copy-start | bytes 7667716
  484.6 4.1 collective-permute-start.10
  488.7 7.8 %collective-permute-start.11 = (f32[48,128]{1,0:T(8,128)S(1)}, f32[48,128]{1,0:T(8,128)S(1)}, u32[]{:S(2)}, u32[]{:S(2)}) collective-permute-start(f32[48,128]{1,0:T(8,128)S(1)} %add.485), channel_id=1, source_target_pairs={{0,16},{2,18},{4,20},{6,22},{8,24},{10,26},{12,28},{14,30},{16,0},... | collective-permute-start | bytes 73736 | tf_op jit(solution)/shard_map/ppermute | solution.py:401
  492.3 23.5 %collective-permute-start.13 = (bf16[384,1536]{1,0:T(8,128)(2,1)}, bf16[384,1536]{1,0:T(8,128)(2,1)}, u32[]{:S(2)}, u32[]{:S(2)}) collective-permute-start(bf16[384,1536]{1,0:T(8,128)(2,1)} %add_convert_fusion.4), channel_id=1, source_target_pairs={{0,4},{2,6},{4,0},{6,2},{8,12},{10,14},{12,8},{14,10},{16,20},{18,... | collective-permute-start | bytes 3538952 | tf_op jit(solution)/shard_map/ppermute | solution.py:401
  492.9 25.1 %collective-permute-start.17 = (bf16[384,1664]{1,0:T(8,128)(2,1)S(1)}, bf16[384,1664]{1,0:T(8,128)(2,1)S(1)}, u32[]{:S(2)}, u32[]{:S(2)}) collective-permute-start(bf16[384,1664]{1,0:T(8,128)(2,1)S(1)} %add_convert_fusion.3), channel_id=1, source_target_pairs={{0,2},{2,0},{4,6},{6,4},{8,10},{10,8},{12,14},{14,12},{16,18},{18,... | collective-permute-start | bytes 3833864 | tf_op jit(solution)/shard_map/ppermute | solution.py:401
  517.5 19.5 %collective-permute-start.14 = (bf16[192,1536]{1,0:T(8,128)(2,1)S(1)}, bf16[192,1536]{1,0:T(8,128)(2,1)S(1)}, u32[]{:S(2)}, u32[]{:S(2)}) collective-permute-start(bf16[192,1536]{1,0:T(8,128)(2,1)S(1)} %add_convert_fusion.10), channel_id=1, source_target_pairs={{0,8},{2,10},{4,12},{6,14},{8,0},{10,2},{12,4},{14,6},{16,24},{18,... | collective-permute-start | bytes 1769480 | tf_op jit(solution)/shard_map/ppermute | solution.py:401
  518.1 28.9 %copy-start.55 = (bf16[384,1664]{1,0:T(8,128)(2,1)}, bf16[384,1664]{1,0:T(8,128)(2,1)S(1)}, u32[]{:S(2)}) copy-start(bf16[384,1664]{1,0:T(8,128)(2,1)S(1)} %collective-permute-done.17) | copy-start | bytes 3833860
  520.0 25.7 %collective-permute-start.18 = (bf16[192,1664]{1,0:T(8,128)(2,1)S(1)}, bf16[192,1664]{1,0:T(8,128)(2,1)S(1)}, u32[]{:S(2)}, u32[]{:S(2)}) collective-permute-start(bf16[192,1664]{1,0:T(8,128)(2,1)S(1)} %add_convert_fusion.9), channel_id=1, source_target_pairs={{0,8},{2,10},{4,12},{6,14},{8,0},{10,2},{12,4},{14,6},{16,24},{18,... | collective-permute-start | bytes 1916936 | tf_op jit(solution)/shard_map/ppermute | solution.py:401
  538.3 20.2 %collective-permute-start.15 = (bf16[96,1536]{1,0:T(8,128)(2,1)S(1)}, bf16[96,1536]{1,0:T(8,128)(2,1)S(1)}, u32[]{:S(2)}, u32[]{:S(2)}) collective-permute-start(bf16[96,1536]{1,0:T(8,128)(2,1)S(1)} %add_convert_fusion.18), channel_id=1, source_target_pairs={{0,16},{2,18},{4,20},{6,22},{8,24},{10,26},{12,28},{14,30},{16,0},... | collective-permute-start | bytes 884744 | tf_op jit(solution)/shard_map/ppermute | solution.py:401
  547.0 14.9 %collective-permute-start.19 = (bf16[96,1664]{1,0:T(8,128)(2,1)S(1)}, bf16[96,1664]{1,0:T(8,128)(2,1)S(1)}, u32[]{:S(2)}, u32[]{:S(2)}) collective-permute-start(bf16[96,1664]{1,0:T(8,128)(2,1)S(1)} %add_convert_fusion.15), channel_id=1, source_target_pairs={{0,16},{2,18},{4,20},{6,22},{8,24},{10,26},{12,28},{14,30},{16,0},... | collective-permute-start | bytes 958472 | tf_op jit(solution)/shard_map/ppermute | solution.py:401
  (54 other events, 231.4 us)

commit v2 on v1

v2 whole, which is shorter than its diff:
```python
import functools
import jax
import jax.numpy as jnp
from jax import lax
from jax.experimental import pallas as pl
from jax.experimental.pallas import tpu as pltpu
from jax.sharding import PartitionSpec as P

EPSILON = 1e-06
BF = jnp.bfloat16
F32 = jnp.float32

VMEM = 60 << 20
COST = pl.CostEstimate(flops=0, bytes_accessed=0, transcendentals=0)


def dot_nn(a, b):
    return lax.dot_general(a, b, (((1,), (0,)), ((), ())), preferred_element_type=F32)


def dot_nt(a, b):
    return lax.dot_general(a, b, (((1,), (1,)), ((), ())), preferred_element_type=F32)


def dot_tn(a, b):
    return lax.dot_general(a, b, (((0,), (0,)), ((), ())), preferred_element_type=F32)


def halves(x):
    high = x.astype(BF)
    return high, (x - high.astype(F32)).astype(BF)


def dot_split(a, b):
    a_high, a_low = halves(a)
    b_high, b_low = halves(b)
    return dot_nn(a_high, b_high) + (dot_nn(a_high, b_low) + dot_nn(a_low, b_high))


def unit_lower_inverse(strict, base):
    size = strict.shape[0]
    lanes = 128
    tiles = size // lanes
    per_tile = lanes // base
    lane = lax.broadcasted_iota(jnp.int32, (base, lanes), 1)
    row = lax.broadcasted_iota(jnp.int32, (base, lanes), 0)
    owner = lane // base
    within = lane % base
    compact = []
    for tile in range(tiles):
        piece = jnp.zeros((base, lanes), F32)
        for block in range(per_tile):
            top = tile * lanes + block * base
            piece = jnp.where(
                owner == block, strict[top : top + base, tile * lanes : (tile + 1) * lanes], piece
            )
        compact.append(piece)
    solved = [jnp.where(row == within, 1.0, 0.0).astype(F32) for _ in range(tiles)]
    for step in range(base - 1):
        index = owner * base + step
        for tile in range(tiles):
            weight = jnp.take_along_axis(compact[tile], index, axis=1)
            solved[tile] = solved[tile] - weight * solved[tile][step : step + 1, :]
    rows = []
    for tile in range(tiles):
        for block in range(per_tile):
            piece = jnp.where(owner == block, solved[tile], 0.0)
            parts = [jnp.zeros((base, lanes), F32)] * tiles
            parts[tile] = piece
            rows.append(jnp.concatenate(parts, axis=1))
    inverse = jnp.concatenate(rows, axis=0)
    grown = base * 2
    row_big = lax.broadcasted_iota(jnp.int32, (size, size), 0)
    col_big = lax.broadcasted_iota(jnp.int32, (size, size), 1)
    while grown < size:
        joined = (row_big // grown == col_big // grown) & (
            row_big // (grown // 2) != col_big // (grown // 2)
        )
        cross = jnp.where(joined, strict, 0.0)
        inverse = inverse - dot_split(dot_split(inverse, cross), inverse)
        grown *= 2
    half = size // 2
    first, second = inverse[:half, :half], inverse[half:, half:]
    corner = -dot_split(dot_split(second, strict[half:, :half]), first)
    top = jnp.concatenate([first, jnp.zeros((half, half), F32)], axis=1)
    bottom = jnp.concatenate([corner, second], axis=1)
    return jnp.concatenate([top, bottom], axis=0)


def shifted_rows(x, amount, place):
    return jnp.where(place >= amount, pltpu.roll(x, amount, 0), 0.0)


def direction(house, taps, place):
    conv = taps[0:1, :] * house
    for shift in range(1, taps.shape[0]):
        conv = conv + taps[shift : shift + 1, :] * shifted_rows(house, shift, place)
    inverse = lax.rsqrt(jnp.sum(conv * conv, axis=1, keepdims=True) + EPSILON)
    return conv, inverse


PAIRS = ((0, 0), (1, 0), (1, 1))


def scores_of(query, key, house_dir, begin, half, a, b):
    rows, cols = slice(a * half, (a + 1) * half), slice(b * half, (b + 1) * half)
    left = jnp.concatenate([query[rows], house_dir[rows]], axis=0)
    right = jnp.concatenate([key[cols], house_dir[cols]], axis=0)
    every = dot_nt(left, right)
    col = lax.broadcasted_iota(jnp.int32, (half, half), 1) + b * half
    row = lax.broadcasted_iota(jnp.int32, (half, half), 0) + a * half
    inside = col >= begin[rows]
    upto = inside & (col <= row)
    before = inside & (col < row)
    return (
        every[:half, :half],
        jnp.where(upto, every[:half, half:], 0.0),
        jnp.where(before, every[half:, :half], 0.0),
        jnp.where(before, every[half:, half:], 0.0),
        upto,
        before,
    )


def forward_head(query, key, value, house, logit, taps, begin, place):
    half = query.shape[0] // 2
    scaling = query.shape[1] ** (-0.5)
    conv, inverse = direction(house, taps, place)
    house_dir = (conv * inverse).astype(BF)
    beta = 2.0 * jax.nn.sigmoid(logit)
    raw, cross, know, gram, upto = {}, {}, {}, {}, {}
    for a, b in PAIRS:
        raw[a, b], x, know[a, b], g, upto[a, b], _ = scores_of(
            query, key, house_dir, begin, half, a, b
        )
        beta_cols = beta[:, b * half : (b + 1) * half]
        cross[a, b] = (x * beta_cols).astype(BF)
        gram[a, b] = g * beta_cols
    eye = (
        lax.broadcasted_iota(jnp.int32, (half, half), 0)
        == lax.broadcasted_iota(jnp.int32, (half, half), 1)
    )
    tail = {}
    for a in (0, 1):
        tail[a] = jnp.where(eye, 0.0, unit_lower_inverse(gram[a, a], 32)).astype(BF)
    z00 = know[0, 0] + dot_nn(tail[0], know[0, 0].astype(BF))
    z00b = z00.astype(BF)
    z11 = know[1, 1] + dot_nn(tail[1], know[1, 1].astype(BF))
    z11b = z11.astype(BF)
    rest = know[1, 0] - dot_nn(gram[1, 0].astype(BF), z00b)
    z10 = rest + dot_nn(tail[1], rest.astype(BF))
    z10b = z10.astype(BF)
    s00 = raw[0, 0] - dot_nn(cross[0, 0], z00b)
    s10 = raw[1, 0] - dot_nn(cross[1, 0], z00b) - dot_nn(cross[1, 1], z10b)
    s11 = raw[1, 1] - dot_nn(cross[1, 1], z11b)
    s00 = jnp.where(upto[0, 0], s00 * scaling, -1e30)
    s10 = jnp.where(upto[1, 0], s10 * scaling, -1e30)
    s11 = jnp.where(upto[1, 1], s11 * scaling, -1e30)
    top0 = jnp.max(s00, axis=1, keepdims=True)
    top1 = jnp.maximum(
        jnp.max(s10, axis=1, keepdims=True), jnp.max(s11, axis=1, keepdims=True)
    )
    e00, e10, e11 = jnp.exp(s00 - top0), jnp.exp(s10 - top1), jnp.exp(s11 - top1)
    sum0 = jnp.sum(e00, axis=1, keepdims=True)
    sum1 = jnp.sum(e10, axis=1, keepdims=True) + jnp.sum(e11, axis=1, keepdims=True)
    inv0, inv1 = 1.0 / sum0, 1.0 / sum1
    p00, p10, p11 = (
        (e00 * inv0).astype(BF),
        (e10 * inv1).astype(BF),
        (e11 * inv1).astype(BF),
    )
    mixed0 = dot_nn(p00, value[:half])
    mixed1 = dot_nn(p10, value[:half]) + dot_nn(p11, value[half:])
    mixed = jnp.concatenate([mixed0, mixed1], axis=0).astype(BF)
    return mixed, (p00, p10, p11, z00b, z10b, z11b, tail[0], tail[1])


def forward_kernel(heads, slots, lengths_ref, me_ref, logit_ref, taps_ref, house_ref, q_ref, k_ref, v_ref, mixed_ref, kept_ref):
    step = pl.program_id(0)
    rows = q_ref.shape[0]
    row = lax.broadcasted_iota(jnp.int32, (rows, 1), 0)
    begin = begins(starts_of(lengths_ref, me_ref[0], slots), row)
    place = row - begin
    for head in range(heads):
        cols = slice(head * 128, (head + 1) * 128)
        logit = logit_ref[pl.ds(step * heads + head, 1), :]
        mixed, kept = forward_head(
            q_ref[:, cols], k_ref[:, cols], v_ref[:, cols], house_ref[:, cols], logit,
            taps_ref[:, cols], begin, place,
        )
        mixed_ref[:, cols] = mixed
        for slot, item in enumerate(kept):
            kept_ref[head, slot] = item


def mixer_forward(lengths, me, logit, taps, house, query, key, value, heads=2):
    rows, width = query.shape
    count = width // 128
    half = rows // 2
    wide = pl.BlockSpec((rows, heads * 128), lambda i: (0, i))
    return pl.pallas_call(
        functools.partial(forward_kernel, heads, lengths.shape[1]),
        grid=(count // heads,),
        in_specs=[
            pl.BlockSpec(memory_space=pltpu.SMEM),
            pl.BlockSpec(memory_space=pltpu.SMEM),
            pl.BlockSpec(logit.shape, lambda i: (0, 0)),
            pl.BlockSpec((taps.shape[0], heads * 128), lambda i: (0, i)),
            wide, wide, wide, wide,
        ],
        out_specs=[wide, pl.BlockSpec((heads, 8, half, half), lambda i: (i, 0, 0, 0))],
        out_shape=[
            jax.ShapeDtypeStruct((rows, width), BF),
            jax.ShapeDtypeStruct((count, 8, half, half), BF),
        ],
        compiler_params=pltpu.CompilerParams(vmem_limit_bytes=VMEM),
        cost_estimate=COST,
        name="mixer_forward",
    )(lengths, me, logit, taps, house, query, key, value)


def backward_head(query, key, value, house, logit, taps, begin, place, d_mixed, kept):
    p00, p10, p11, z00, z10, z11, tail0, tail1 = kept
    rows = query.shape[0]
    half = rows // 2
    scaling = query.shape[1] ** (-0.5)
    conv, inverse = direction(house, taps, place)
    direct = conv * inverse
    house_dir = direct.astype(BF)
    beta = 2.0 * jax.nn.sigmoid(logit)
    cross, cross_b, gram, gram_raw, upto, before, beta_cols = {}, {}, {}, {}, {}, {}, {}
    for a, b in PAIRS:
        _, cross[a, b], _, gram_raw[a, b], upto[a, b], before[a, b] = scores_of(
            query, key, house_dir, begin, half, a, b
        )
        beta_cols[b] = beta[:, b * half : (b + 1) * half]
        cross_b[a, b] = (cross[a, b] * beta_cols[b]).astype(BF)
    gram10 = (gram_raw[1, 0] * beta_cols[0]).astype(BF)
    d0, d1 = d_mixed[:half], d_mixed[half:]
    v0, v1 = value[:half], value[half:]
    dp00, dp10, dp11 = dot_nt(d0, v0), dot_nt(d1, v0), dot_nt(d1, v1)
    dv0 = dot_tn(p00, d0) + dot_tn(p10, d1)
    dv1 = dot_tn(p11, d1)
    f00, f10, f11 = p00.astype(F32), p10.astype(F32), p11.astype(F32)
    mean0 = jnp.sum(f00 * dp00, axis=1, keepdims=True)
    mean1 = jnp.sum(f10 * dp10, axis=1, keepdims=True) + jnp.sum(f11 * dp11, axis=1, keepdims=True)
    ds = {
        (0, 0): (f00 * (dp00 - mean0) * scaling).astype(BF),
        (1, 0): (f10 * (dp10 - mean1) * scaling).astype(BF),
        (1, 1): (f11 * (dp11 - mean1) * scaling).astype(BF),
    }
    dx = {
        (0, 0): dot_nt(ds[0, 0], z00),
        (1, 0): dot_nt(ds[1, 0], z00),
        (1, 1): dot_nt(ds[1, 1], z11) + dot_nt(ds[1, 0], z10),
    }
    dz00 = dot_tn(cross_b[0, 0], ds[0, 0]) + dot_tn(cross_b[1, 0], ds[1, 0])
    dz10 = dot_tn(cross_b[1, 1], ds[1, 0])
    dz11 = dot_tn(cross_b[1, 1], ds[1, 1])
    e11 = dz11 + dot_tn(tail1, dz11.astype(BF))
    e10 = dz10 + dot_tn(tail1, dz10.astype(BF))
    rest = dz00 - dot_tn(gram10, e10.astype(BF))
    e00 = rest + dot_tn(tail0, rest.astype(BF))
    e00b, e10b, e11b = e00.astype(BF), e10.astype(BF), e11.astype(BF)
    dn = {
        (0, 0): dot_nt(e00b, z00),
        (1, 0): dot_nt(e10b, z00),
        (1, 1): dot_nt(e10b, z10) + dot_nt(e11b, z11),
    }
    dy = {(0, 0): e00, (1, 0): e10, (1, 1): e11}
    d_beta = [jnp.zeros((1, half), F32), jnp.zeros((1, half), F32)]
    d_q = [0.0, 0.0]
    d_w = [0.0, 0.0]
    d_k = [0.0, 0.0]
    for a, b in PAIRS:
        part_x = jnp.where(upto[a, b], -dx[a, b], 0.0)
        part_n = jnp.where(before[a, b], dn[a, b], 0.0)
        part_y = jnp.where(before[a, b], -dy[a, b], 0.0)
        d_beta[b] = d_beta[b] + jnp.sum(
            part_x * cross[a, b] + part_n * gram_raw[a, b], axis=0, keepdims=True
        )
        upper = jnp.concatenate([ds[a, b], (part_x * beta_cols[b]).astype(BF)], axis=1)
        lower = jnp.concatenate([part_y.astype(BF), (part_n * beta_cols[b]).astype(BF)], axis=1)
        big = jnp.concatenate([upper, lower], axis=0)
        rows_a, cols_b = slice(a * half, (a + 1) * half), slice(b * half, (b + 1) * half)
        right = jnp.concatenate([key[cols_b], house_dir[cols_b]], axis=0)
        left = jnp.concatenate([query[rows_a], house_dir[rows_a]], axis=0)
        by_row = dot_nn(big, right)
        by_col = dot_tn(big, left)
        d_q[a] = d_q[a] + by_row[:half]
        d_w[a] = d_w[a] + by_row[half:]
        d_k[b] = d_k[b] + by_col[:half]
        d_w[b] = d_w[b] + by_col[half:]
    d_dir = jnp.concatenate(d_w, axis=0)
    d_conv = inverse * d_dir - direct * (
        inverse * jnp.sum(direct * d_dir, axis=1, keepdims=True)
    )
    d_house = taps[0:1, :] * d_conv
    d_taps = [jnp.sum(d_conv * house, axis=0, keepdims=True)]
    for shift in range(1, taps.shape[0]):
        live = jnp.where(place >= shift, d_conv, 0.0)
        d_house = d_house + taps[shift : shift + 1, :] * pltpu.roll(live, rows - shift, 0)
        d_taps.append(jnp.sum(live * pltpu.roll(house, shift, 0), axis=0, keepdims=True))
    d_logit = jnp.concatenate(d_beta, axis=1) * beta * (1.0 - 0.5 * beta)
    return (
        jnp.concatenate(d_q, axis=0).astype(BF),
        jnp.concatenate(d_k, axis=0).astype(BF),
        jnp.concatenate([dv0, dv1], axis=0).astype(BF),
        d_house.astype(BF),
        d_logit,
        d_taps,
    )


def backward_kernel(
    heads, slots, lengths_ref, me_ref, logit_ref, taps_ref, house_ref, q_ref, k_ref, v_ref, dm_ref, kept_ref,
    four_ref, dl_ref, dt_ref,
):
    step = pl.program_id(0)
    rows = q_ref.shape[0]
    row = lax.broadcasted_iota(jnp.int32, (rows, 1), 0)
    begin = begins(starts_of(lengths_ref, me_ref[0], slots), row)
    place = row - begin
    for head in range(heads):
        cols = slice(head * 128, (head + 1) * 128)
        logit = logit_ref[pl.ds(step * heads + head, 1), :]
        kept = tuple(kept_ref[head, slot] for slot in range(8))
        d_q, d_k, d_v, d_h, d_l, d_t = backward_head(
            q_ref[:, cols], k_ref[:, cols], v_ref[:, cols], house_ref[:, cols], logit,
            taps_ref[:, cols], begin, place, dm_ref[:, cols], kept,
        )
        for slot, item in enumerate((d_q, d_k, d_v, d_h)):
            four_ref[slot, :, cols] = item
        dl_ref[pl.ds(step * heads + head, 1), :] = d_l
        for tap, item in enumerate(d_t):
            dt_ref[tap : tap + 1, cols] = item


def mixer_backward(lengths, me, logit, taps, house, query, key, value, d_mixed, kept, heads=2):
    rows, width = query.shape
    count = width // 128
    half = rows // 2
    wide = pl.BlockSpec((rows, heads * 128), lambda i: (0, i))
    narrow = pl.BlockSpec((taps.shape[0], heads * 128), lambda i: (0, i))
    whole = pl.BlockSpec(logit.shape, lambda i: (0, 0))
    return pl.pallas_call(
        functools.partial(backward_kernel, heads, lengths.shape[1]),
        grid=(count // heads,),
        in_specs=[
            pl.BlockSpec(memory_space=pltpu.SMEM),
            pl.BlockSpec(memory_space=pltpu.SMEM),
            whole, narrow, wide, wide, wide, wide, wide,
            pl.BlockSpec((heads, 8, half, half), lambda i: (i, 0, 0, 0)),
        ],
        out_specs=[pl.BlockSpec((4, rows, heads * 128), lambda i: (0, 0, i)), whole, narrow],
        out_shape=[
            jax.ShapeDtypeStruct((4, rows, width), BF),
            jax.ShapeDtypeStruct(logit.shape, F32),
            jax.ShapeDtypeStruct(taps.shape, F32),
        ],
        compiler_params=pltpu.CompilerParams(vmem_limit_bytes=VMEM),
        cost_estimate=COST,
        name="mixer_backward",
    )(lengths, me, logit, taps, house, query, key, value, d_mixed, kept)


def starts_of(lengths_ref, me, slots):
    starts, sum_so_far = [], 0
    for j in range(slots):
        starts.append(sum_so_far)
        sum_so_far = sum_so_far + lengths_ref[me, j]
    return starts


def begins(starts, row):
    begin = jnp.zeros_like(row)
    for start in starts[1:]:
        begin = jnp.where(row >= start, start, begin)
    return begin


def group_of(sequence, slots):
    return lax.div(sequence, jnp.int32(slots))


def slot_taken(dealing_ref, me, slots, group):
    found = jnp.int32(0)
    for k in range(slots):
        found = jnp.where(group_of(dealing_ref[me * slots + k], slots) == group, k, found)
    return found


def holder_of(dealing_ref, me, slots, count, sequence):
    far, slot = jnp.int32(0), jnp.int32(0)
    for by in (-1, 0, 1):
        for k in range(slots):
            position = (me + by) * slots + k
            inside = (position >= 0) & (position < count)
            hit = inside & (dealing_ref[jnp.clip(position, 0, count - 1)] == sequence)
            far = jnp.where(hit, by, far)
            slot = jnp.where(hit, k, slot)
    return far, slot


def part_kernel(dealing_ref, me_ref, up_in, down_in, up_out, down_out):
    up_out[...] = up_in[0]
    down_out[...] = down_in[0]


def slots_to_send(dealing, me, cotangent):
    slots, span, width = cotangent.shape
    tile = 512
    out = pl.BlockSpec((span, tile), lambda j, dealing, me: (0, j))

    def source(by):
        return pl.BlockSpec(
            (1, span, tile),
            lambda j, dealing, me: (slot_taken(dealing, me[0], slots, me[0] + by), 0, j),
        )

    shape = jax.ShapeDtypeStruct((span, width), BF)
    return pl.pallas_call(
        part_kernel,
        grid_spec=pltpu.PrefetchScalarGridSpec(
            num_scalar_prefetch=2,
            grid=(width // tile,),
            in_specs=[source(1), source(-1)],
            out_specs=[out, out],
        ),
        out_shape=[shape, shape],
        compiler_params=pltpu.CompilerParams(vmem_limit_bytes=VMEM),
        cost_estimate=COST,
        name="slots_to_send",
    )(dealing, me, cotangent, cotangent)


def arrive_kernel(slots, count, lengths_ref, dealing_ref, me_ref, own_ref, low_ref, high_ref, out_ref, turned_ref, picks):
    span = low_ref.shape[0]

    @pl.when(pl.program_id(0) == 0)
    def _():
        me = me_ref[0]
        starts = starts_of(lengths_ref, me, slots)
        row = lax.broadcasted_iota(jnp.int32, (picks.shape[0], 1), 0)
        index = jnp.zeros_like(row)
        for j in range(slots):
            far, slot = holder_of(dealing_ref, me, slots, count, me * slots + j)
            base = jnp.where(far == 0, slot * span, jnp.where(far < 0, slots * span, (slots + 1) * span))
            index = jnp.where(row >= starts[j], base + row - starts[j], index)
        column = lax.broadcasted_iota(jnp.int32, picks.shape, 1)
        picks[...] = jnp.where(column == index, 1.0, 0.0).astype(BF)

    out = (
        dot_nn(picks[:, : slots * span], own_ref[...])
        + dot_nn(picks[:, slots * span : (slots + 1) * span], low_ref[...])
        + dot_nn(picks[:, (slots + 1) * span :], high_ref[...])
    ).astype(BF)
    out_ref[...] = out
    turned_ref[...] = out.T


def cotangent_arrived(lengths, dealing, me, own, low, high, rows):
    span, width = low.shape
    slots = own.shape[0] // span
    tile = 512
    column = lambda n: pl.BlockSpec((n, tile), lambda j, *s: (0, j))
    return pl.pallas_call(
        functools.partial(arrive_kernel, slots, dealing.shape[0]),
        grid_spec=pltpu.PrefetchScalarGridSpec(
            num_scalar_prefetch=3,
            grid=(width // tile,),
            in_specs=[column(own.shape[0]), column(span), column(span)],
            out_specs=[column(rows), pl.BlockSpec((tile, rows), lambda j, *s: (j, 0))],
            scratch_shapes=[pltpu.VMEM((rows, (slots + 2) * span), BF)],
        ),
        out_shape=[
            jax.ShapeDtypeStruct((rows, width), BF),
            jax.ShapeDtypeStruct((width, rows), BF),
        ],
        compiler_params=pltpu.CompilerParams(vmem_limit_bytes=VMEM),
        cost_estimate=COST,
        name="cotangent_arrived",
    )(lengths, dealing, me, own, low, high)


def deal_kernel(slots, count, span, lengths_ref, dealing_ref, me_ref, hidden_ref, part_ref, other_ref, own_ref, up_ref, down_ref, picks):
    @pl.when(pl.program_id(0) == 0)
    def _():
        me = me_ref[0]
        starts = starts_of(lengths_ref, me, slots)

        def zone(chosen):
            start, length = jnp.int32(0), jnp.int32(0)
            for j in range(slots):
                start = jnp.where(chosen[j], starts[j], start)
                length = jnp.where(chosen[j], lengths_ref[me, j], length)
            return start, length

        held = [dealing_ref[me * slots + k] for k in range(slots)]
        far = [holder_of(dealing_ref, me, slots, count, me * slots + j)[0] for j in range(slots)]
        zones = [zone([held[k] == me * slots + j for j in range(slots)]) for k in range(slots)]
        zones.append(zone([far[j] == 1 for j in range(slots)]))
        zones.append(zone([far[j] == -1 for j in range(slots)]))
        row = lax.broadcasted_iota(jnp.int32, (picks.shape[0], 1), 0)
        index = jnp.full_like(row, -1)
        for k, (start, length) in enumerate(zones):
            offset = row - k * span
            index = jnp.where((offset >= 0) & (offset < length), start + offset, index)
        column = lax.broadcasted_iota(jnp.int32, picks.shape, 1)
        picks[...] = jnp.where(column == index, 1.0, 0.0).astype(BF)

    final = hidden_ref[...] + (part_ref[...].astype(F32) + other_ref[...].astype(F32))
    out = dot_nn(picks[...], final.astype(BF)).astype(BF)
    own_ref[...] = out[: slots * span]
    up_ref[...] = out[slots * span : (slots + 1) * span]
    down_ref[...] = out[(slots + 1) * span :]


def rows_dealt(lengths, dealing, me, hidden, part, other, slots, span):
    rows, width = hidden.shape
    tile = 512
    column = lambda n: pl.BlockSpec((n, tile), lambda j, *s: (0, j))
    return pl.pallas_call(
        functools.partial(deal_kernel, slots, dealing.shape[0], span),
        grid_spec=pltpu.PrefetchScalarGridSpec(
            num_scalar_prefetch=3,
            grid=(width // tile,),
            in_specs=[column(rows)] * 3,
            out_specs=[column(slots * span), column(span), column(span)],
            scratch_shapes=[pltpu.VMEM(((slots + 2) * span, rows), BF)],
        ),
        out_shape=[
            jax.ShapeDtypeStruct((slots * span, width), BF),
            jax.ShapeDtypeStruct((span, width), BF),
            jax.ShapeDtypeStruct((span, width), BF),
        ],
        compiler_params=pltpu.CompilerParams(vmem_limit_bytes=VMEM),
        cost_estimate=COST,
        name="rows_dealt",
    )(lengths, dealing, me, hidden, part, other)


def norm_kernel(tokens_ref, gain_ref, normed_ref, turned_ref):
    data = tokens_ref[...].astype(F32)
    inverse = lax.rsqrt(jnp.mean(data * data, axis=1, keepdims=True) + EPSILON)
    normed = (data * inverse * gain_ref[...]).astype(BF)
    normed_ref[...] = normed
    turned_ref[...] = normed.T


def first_norm(tokens, gain, tile=128):
    rows, width = tokens.shape
    flat = pl.BlockSpec((tile, width), lambda i: (i, 0))
    return pl.pallas_call(
        norm_kernel,
        grid=(rows // tile,),
        in_specs=[flat, pl.BlockSpec((1, width), lambda i: (0, 0))],
        out_specs=[flat, pl.BlockSpec((width, tile), lambda i: (0, i))],
        out_shape=[
            jax.ShapeDtypeStruct((rows, width), BF),
            jax.ShapeDtypeStruct((width, rows), BF),
        ],
        compiler_params=pltpu.CompilerParams(vmem_limit_bytes=VMEM),
        cost_estimate=COST,
        name="first_norm",
    )(tokens, gain[None, :])


def hidden_kernel(tokens_ref, part_ref, other_ref, gain_ref, hidden_ref, normed_ref, turned_ref):
    hidden = tokens_ref[...].astype(F32) + (part_ref[...].astype(F32) + other_ref[...].astype(F32))
    inverse = lax.rsqrt(jnp.mean(hidden * hidden, axis=1, keepdims=True) + EPSILON)
    normed = (hidden * inverse * gain_ref[...]).astype(BF)
    hidden_ref[...] = hidden
    normed_ref[...] = normed
    turned_ref[...] = normed.T


def hidden_and_norm(tokens, part, other, gain, tile=128):
    rows, width = tokens.shape
    flat = pl.BlockSpec((tile, width), lambda i: (i, 0))
    return pl.pallas_call(
        hidden_kernel,
        grid=(rows // tile,),
        in_specs=[flat, flat, flat, pl.BlockSpec((1, width), lambda i: (0, 0))],
        out_specs=[flat, flat, pl.BlockSpec((width, tile), lambda i: (0, i))],
        out_shape=[
            jax.ShapeDtypeStruct((rows, width), F32),
            jax.ShapeDtypeStruct((rows, width), BF),
            jax.ShapeDtypeStruct((width, rows), BF),
        ],
        compiler_params=pltpu.CompilerParams(vmem_limit_bytes=VMEM),
        cost_estimate=COST,
        name="hidden_and_norm",
    )(tokens, part, other, gain[None, :])


def norm_back(d_normed, source, gain):
    inverse = lax.rsqrt(jnp.mean(source * source, axis=1, keepdims=True) + EPSILON)
    scaled = d_normed * gain
    back = inverse * scaled - source * (inverse * inverse * inverse) * jnp.mean(
        scaled * source, axis=1, keepdims=True
    )
    return back, jnp.sum(d_normed * source * inverse, axis=0, keepdims=True)


def accumulate(ref, value):
    @pl.when(pl.program_id(0) == 0)
    def _():
        ref[...] = value

    @pl.when(pl.program_id(0) > 0)
    def _():
        ref[...] += value


def branch_kernel(
    part_ref, other_ref, hidden_ref, d_final_ref, gain_ref, out_ref,
    d_hidden_ref, turned_ref, d_mixed_ref, d_gain_ref,
):
    back, d_gain = norm_back(part_ref[...].astype(F32) + other_ref[...].astype(F32), hidden_ref[...], gain_ref[...])
    accumulate(d_gain_ref, d_gain)
    d_hidden = d_final_ref[...].astype(F32) + back
    d_hidden_ref[...] = d_hidden
    d_branch = d_hidden.astype(BF)
    turned_ref[...] = d_branch.T
    d_mixed_ref[...] = dot_nt(d_branch, out_ref[...]).astype(BF)


def branch_back(part, other, hidden, d_final, gain, w_out, tile=128):
    rows, width = hidden.shape
    channels = w_out.shape[0]
    flat = pl.BlockSpec((tile, width), lambda i: (i, 0))
    line = pl.BlockSpec((1, width), lambda i: (0, 0))
    return pl.pallas_call(
        branch_kernel,
        grid=(rows // tile,),
        in_specs=[flat, flat, flat, flat, line, pl.BlockSpec((channels, width), lambda i: (0, 0))],
        out_specs=[
            flat,
            pl.BlockSpec((width, tile), lambda i: (0, i)),
            pl.BlockSpec((tile, channels), lambda i: (i, 0)),
            line,
        ],
        out_shape=[
            jax.ShapeDtypeStruct((rows, width), F32),
            jax.ShapeDtypeStruct((width, rows), BF),
            jax.ShapeDtypeStruct((rows, channels), BF),
            jax.ShapeDtypeStruct((1, width), F32),
        ],
        compiler_params=pltpu.CompilerParams(vmem_limit_bytes=VMEM),
        cost_estimate=COST,
        name="branch_back",
    )(part, other, hidden, d_final, gain[None, :], w_out)


def input_kernel(
    part_ref, other_ref, tokens_ref, d_hidden_ref, gain_ref, taps_ref, ffn_ref, logit_ref, out_ref, small_ref
):
    tokens = tokens_ref[...].astype(F32)
    gain = gain_ref[...]
    taps, heads = taps_ref.shape[0], logit_ref.shape[0]
    back, d_gain = norm_back(part_ref[...].astype(F32) + other_ref[...].astype(F32), tokens, gain)
    out_ref[...] = (d_hidden_ref[...] + back).astype(BF)
    inverse = lax.rsqrt(jnp.mean(tokens * tokens, axis=1, keepdims=True) + EPSILON)
    d_beta = dot_nn(logit_ref[...].astype(BF), (tokens * inverse * gain).astype(BF))

    @pl.when(pl.program_id(0) == 0)
    def _():
        small_ref[...] = jnp.zeros_like(small_ref)
        small_ref[0:taps, 0 : taps_ref.shape[1]] = taps_ref[...]
        small_ref[taps : taps + 1, :] = ffn_ref[...]

    small_ref[taps + 1 : taps + 2, :] += d_gain
    small_ref[taps + 2 : taps + 2 + heads, :] += d_beta


def input_back(part, other, tokens, d_hidden, gain, g_taps, g_ffn_gain, d_logit, tile=128):
    rows, width = tokens.shape
    flat = pl.BlockSpec((tile, width), lambda i: (i, 0))
    line = pl.BlockSpec((1, width), lambda i: (0, 0))
    height = -(-(g_taps.shape[0] + 2 + d_logit.shape[0]) // 8) * 8
    return pl.pallas_call(
        input_kernel,
        grid=(rows // tile,),
        in_specs=[flat, flat, flat, flat, line]
        + [
            pl.BlockSpec(g_taps.shape, lambda i: (0, 0)),
            line,
            pl.BlockSpec((d_logit.shape[0], tile), lambda i: (0, i)),
        ],
        out_specs=[flat, pl.BlockSpec((height, width), lambda i: (0, 0))],
        out_shape=[
            jax.ShapeDtypeStruct((rows, width), BF),
            jax.ShapeDtypeStruct((height, width), F32),
        ],
        compiler_params=pltpu.CompilerParams(vmem_limit_bytes=VMEM),
        cost_estimate=COST,
        name="input_back",
    )(part, other, tokens, d_hidden, gain[None, :], g_taps, g_ffn_gain, d_logit)


def product_kernel(count, turned, small, *refs):
    lefts, weights, out_ref = refs[:count], refs[count : 2 * count], refs[-1]
    dot = dot_nt if turned else dot_nn
    out = dot(lefts[0][...], weights[0][...])
    for left, weight in zip(lefts[1:], weights[1:]):
        out = out + dot(left[...], weight[...])
    if small:
        out = out + lax.dot_general(
            refs[2 * count][...].astype(BF), refs[2 * count + 1][...], (((0,), (1,)), ((), ())),
            preferred_element_type=F32,
        )
    out_ref[...] = out.astype(out_ref.dtype)


def product(lefts, weights, turned, dtype=F32, small=(), tile=512):
    width = weights[0].shape[0 if turned else 1]
    whole = lambda x: pl.BlockSpec(x.shape, lambda j: (0, 0))
    left_specs, arrays = [], []
    for left in lefts:
        if isinstance(left, tuple):
            array, index = left
            rows = array.shape[1]
            left_specs.append(
                pl.BlockSpec((None,) + array.shape[1:], lambda j, index=index: (index, 0, 0))
            )
            arrays.append(array)
        else:
            rows = left.shape[0]
            left_specs.append(whole(left))
            arrays.append(left)
    if turned:
        parts = [pl.BlockSpec((tile, w.shape[1]), lambda j: (j, 0)) for w in weights]
    else:
        parts = [pl.BlockSpec((w.shape[0], tile), lambda j: (0, j)) for w in weights]
    more = [whole(small[0]), pl.BlockSpec((tile, small[1].shape[1]), lambda j: (j, 0))] if small else []
    return pl.pallas_call(
        functools.partial(product_kernel, len(lefts), turned, bool(small)),
        grid=(width // tile,),
        in_specs=left_specs + parts + more,
        out_specs=pl.BlockSpec((rows, tile), lambda j: (0, j)),
        out_shape=jax.ShapeDtypeStruct((rows, width), dtype),
        compiler_params=pltpu.CompilerParams(vmem_limit_bytes=VMEM),
        cost_estimate=COST,
        name="product",
    )(*arrays, *weights, *small)


def fold_kernel(plan, cuts, *refs):
    count = 1 if cuts is None else sum(cuts)
    ins, outs = refs[:-count], refs[-count:]
    start, first = 0, 0
    for index, (width, terms) in enumerate(plan):
        part = None
        for ref, column in terms:
            term = ins[ref][:, column : column + width].astype(F32)
            part = term if part is None else part + term
        if cuts is None:
            outs[0][:, start : start + width] = part.astype(outs[0].dtype)
            start += width
        else:
            piece = width // cuts[index]
            for i in range(cuts[index]):
                outs[first + i][...] = part[:, i * piece : (i + 1) * piece]
            first += cuts[index]


def fold(streams, height, cuts=None):
    step = height
    while step % 2 == 0 and step > 96 and (step // 2) % 8 == 0:
        step //= 2
    arrays, plan = [], []
    for width, terms in streams:
        places = []
        for array, row, column in terms:
            known = [i for i, (a, r) in enumerate(arrays) if a is array and r == row]
            if not known:
                arrays.append((array, row))
            places.append((known[0] if known else len(arrays) - 1, column))
        plan.append((width, places))
    if cuts is None:
        widths, kind = [sum(width for width, _ in streams)], BF
    else:
        widths = [w // n for (w, _), n in zip(streams, cuts) for _ in range(n)]
        kind = F32
    return pl.pallas_call(
        functools.partial(fold_kernel, plan, cuts),
        grid=(height // step,),
        in_specs=[
            pl.BlockSpec((step, array.shape[1]), lambda i, r=row // step: (r + i, 0))
            for array, row in arrays
        ],
        out_specs=[pl.BlockSpec((step, width), lambda i: (i, 0)) for width in widths],
        out_shape=[jax.ShapeDtypeStruct((height, width), kind) for width in widths],
        compiler_params=pltpu.CompilerParams(vmem_limit_bytes=VMEM),
        cost_estimate=COST,
        name="fold",
    )(*[array for array, _ in arrays])


def added_kernel(a_ref, b_ref, out_ref):
    out_ref[...] = a_ref[...] + b_ref[...]


def added(a, b):
    return pl.pallas_call(
        added_kernel,
        out_shape=jax.ShapeDtypeStruct(a.shape, a.dtype),
        compiler_params=pltpu.CompilerParams(vmem_limit_bytes=VMEM),
        cost_estimate=COST,
        name="added",
    )(a, b)


def wgrad_kernel(plan, order_ref, *refs):
    lefts, rights = refs[: len(refs) - 2 - len(plan)], refs[len(refs) - 2 - len(plan) : -2]
    out_ref, packed = refs[-2:]
    block = lefts[0].shape[1]
    count = packed.shape[1] // block
    step = pl.program_id(0)

    @pl.when(step == 0)
    def _():
        for part, left_ref in enumerate(lefts):
            for i in range(count):
                packed[part, i * block : (i + 1) * block, :] = left_ref[order_ref[i]]

    for (part, first, steps), right_ref in zip(plan, rights):

        @pl.when((step >= first) & (step < first + steps))
        def _(right_ref=right_ref, part=part):
            out_ref[...] = dot_nn(packed[part], right_ref[...]).astype(out_ref.dtype)


def wgrad(order, parts, tile=512):
    count = order.shape[0]
    lefts = [left for left, _ in parts]
    rights = [right for _, several in parts for right in several]
    block, tokens = lefts[0].shape[1:]
    tile = next(t for t in (tile, 384, 256, 128) if all(r.shape[1] % t == 0 for r in rights))
    plan, first = [], 0
    for part, (_, several) in enumerate(parts):
        for right in several:
            plan.append((part, first, right.shape[1] // tile))
            first += right.shape[1] // tile
    return pl.pallas_call(
        functools.partial(wgrad_kernel, plan),
        grid_spec=pltpu.PrefetchScalarGridSpec(
            num_scalar_prefetch=1,
            grid=(first,),
            in_specs=[pl.BlockSpec(left.shape, lambda j, order: (0, 0, 0)) for left in lefts]
            + [
                pl.BlockSpec(
                    (tokens, tile), lambda j, order, s=s, n=n: (0, jnp.clip(j - s, 0, n - 1))
                )
                for _, s, n in plan
            ],
            out_specs=pl.BlockSpec((count * block, tile), lambda j, order: (0, j)),
            scratch_shapes=[pltpu.VMEM((len(lefts), count * block, tokens), BF)],
        ),
        out_shape=jax.ShapeDtypeStruct((count * block, first * tile), BF),
        compiler_params=pltpu.CompilerParams(vmem_limit_bytes=VMEM),
        cost_estimate=COST,
        name="wgrad",
    )(order, *lefts, *rights)


def plane_kernel(order_ref, left_ref, right_ref, out_ref):
    total = dot_nn(left_ref[0], right_ref[0])
    for i in range(1, left_ref.shape[0]):
        total = total + dot_nn(left_ref[i], right_ref[i])
    out_ref[...] = total.astype(out_ref.dtype)


def wgrad_plane(order, left, right, blocks):
    parts, width, tokens = left.shape
    columns = right.shape[2]
    height = width // blocks
    return pl.pallas_call(
        plane_kernel,
        grid_spec=pltpu.PrefetchScalarGridSpec(
            num_scalar_prefetch=1,
            grid=(order.shape[0],),
            in_specs=[
                pl.BlockSpec((parts, height, tokens), lambda j, order: (0, order[j], 0)),
                pl.BlockSpec(right.shape, lambda j, order: (0, 0, 0)),
            ],
            out_specs=pl.BlockSpec((height, columns), lambda j, order: (j, 0)),
        ),
        out_shape=jax.ShapeDtypeStruct((order.shape[0] * height, columns), BF),
        compiler_params=pltpu.CompilerParams(vmem_limit_bytes=VMEM),
        cost_estimate=COST,
        name="wgrad_plane",
    )(order, left, right)


def ffn_kernel(normed_ref, d_final_ref, gate_ref, up_ref, down_ref, inner_ref, d_gate_ref, d_up_ref):
    gate = dot_nn(normed_ref[...], gate_ref[...])
    lift = dot_nn(normed_ref[...], up_ref[...])
    d_inner = dot_nt(d_final_ref[...], down_ref[...])
    sig = jax.nn.sigmoid(gate)
    silu = gate * sig
    inner_ref[...] = (silu * lift).astype(BF)
    d_gate_ref[...] = (d_inner * lift * sig * (1.0 + gate * (1.0 - sig))).astype(BF)
    d_up_ref[...] = (d_inner * silu).astype(BF)


def ffn(normed, d_final, w_gate, w_up, w_down, tile=256):
    rows, width = normed.shape
    hidden = w_gate.shape[1]
    whole = pl.BlockSpec((rows, width), lambda j: (0, 0))
    column = pl.BlockSpec((width, tile), lambda j: (0, j))
    out = pl.BlockSpec((rows, tile), lambda j: (0, j))
    shape = jax.ShapeDtypeStruct((rows, hidden), BF)
    return pl.pallas_call(
        ffn_kernel,
        grid=(hidden // tile,),
        in_specs=[whole, whole, column, column, pl.BlockSpec((tile, width), lambda j: (j, 0))],
        out_specs=[out, out, out],
        out_shape=[shape, shape, shape],
        compiler_params=pltpu.CompilerParams(vmem_limit_bytes=VMEM),
        cost_estimate=COST,
        name="ffn",
    )(normed, d_final, w_gate, w_up, w_down)


def swap(x, axis, bit):
    size = lax.axis_size(axis)
    return lax.ppermute(x, axis, [(i, i ^ (1 << bit)) for i in range(size)])


def flips_of(count, bits):
    flips = []
    for position in reversed(range(count)):
        flips.append(
            sum(((position >> (len(bits) - 1 - rank)) & 1) << bit for rank, bit in enumerate(bits))
        )
    return jnp.array(flips, jnp.int32)


def halve(terms, bits):
    for bit in bits:
        half = terms[0].shape[0] // 2
        out = sum(t[:half].astype(F32) for t in terms).astype(BF)
        terms = [t[half:] for t in terms] + [swap(out, "dp", bit)]
    return terms


def total(terms):
    return sum(t.astype(F32) for t in terms)


def after(value, *others):
    return lax.optimization_barrier((value,) + others)[0]


class Order:
    def __init__(self):
        self.last = ()

    def gate(self, *values):
        if self.last:
            values = lax.optimization_barrier(tuple(values) + self.last)[: len(values)]
        return values if len(values) > 1 else values[0]

    def mark(self, *values):
        self.last = values
        return values if len(values) > 1 else values[0]


def stream(*arrays):
    return arrays[0].shape[1], [(array, 0, 0) for array in arrays]


def joined(streams, got):
    column, out = 0, []
    for width, terms in streams:
        out.append((width, terms + [(got, 0, column)]))
        column += width
    return out


def on_device(
    tokens,
    cotangent,
    lengths,
    dealing,
    attn_gain,
    w_query,
    w_key,
    w_value,
    w_house,
    w_beta,
    conv_taps,
    w_out,
    ffn_gain,
    w_gate,
    w_up,
    w_down,
):
    rows, width = tokens.shape
    slots, span = cotangent.shape[:2]
    size = lax.axis_size("dp")
    me = lax.axis_index("dp").astype(jnp.int32)
    me1 = me.reshape(1)
    block = width // size
    bits = list(range(size.bit_length() - 1))
    plane, line = bits[:2], bits[2:]
    up = [(i, i + 1) for i in range(size - 1)]
    down = [(i + 1, i) for i in range(size - 1)]
    first = size // 2
    groups = [[i + j for j in range(4)] for i in range(0, size, 4)]
    order_line = (me >> 2) ^ flips_of(size // 4, [b - 2 for b in line])
    order_plane = (jnp.arange(4, dtype=jnp.int32)[:, None] + 4 * order_line[None, :]).reshape(-1)
    order_zxy = me ^ flips_of(size, line + plane)
    order_xyz = me ^ flips_of(size, bits)
    order = Order()

    def sharded(turned):
        return turned.reshape(size, block, turned.shape[1])

    cot_up, cot_down = order.mark(*slots_to_send(dealing, me1, cotangent))
    cot_low = lax.ppermute(cot_up, "dp", up)
    cot_high = lax.ppermute(cot_down, "dp", down)

    normed1, normed1_t = order.mark(*first_norm(order.gate(tokens), attn_gain))
    plane_normed = lax.all_gather(normed1_t, "dp", axis_index_groups=groups)
    normed = order.gate(normed1)
    logit = lax.dot_general(
        w_beta, normed, (((0,), (1,)), ((), ())), preferred_element_type=F32
    )
    query = dot_nn(normed, w_query).astype(BF)
    key = dot_nn(normed, w_key).astype(BF)
    value = dot_nn(normed, w_value).astype(BF)
    house = dot_nn(normed, w_house)
    order.mark(query, key, value, house, logit)
    mixed, kept = order.mark(
        *mixer_forward(lengths, me1, logit, conv_taps, house, order.gate(query), key, value)
    )
    cot_low, cot_high = order.mark(*order.gate(cot_low, cot_high))
    attn_part = order.mark(product([order.gate(mixed)], [w_out], False, BF))
    attn_other = swap(attn_part, "tensor", 0)
    cot_low = order.gate(cot_low)
    d_final, d_final_t = order.mark(
        *cotangent_arrived(lengths, dealing, me1, cotangent.reshape(-1, width), cot_low, cot_high, rows)
    )
    hidden, normed2, normed2_t = order.mark(
        *hidden_and_norm(tokens, attn_part, order.gate(attn_other), ffn_gain)
    )
    inner, d_gate, d_up = order.mark(*ffn(order.gate(normed2), d_final, w_gate, w_up, w_down))

    def gated(streams):
        arrays = []
        for _, terms in streams:
            for array, _, _ in terms:
                if not any(array is known for known in arrays):
                    arrays.append(array)
        after = order.gate(*arrays)
        after = list(after) if isinstance(after, tuple) else [after]
        return [
            (w, [(next(n for a, n in zip(arrays, after) if a is array), r, c) for array, r, c in terms])
            for w, terms in streams
        ]

    def leave(streams, height, bit):
        streams = gated(streams)
        got = swap(order.mark(fold(streams, height)[0]), "dp", bit)
        return joined([(w, [(a, r + height, c) for a, r, c in terms]) for w, terms in streams], got)

    def finish(streams, cuts):
        out = fold(gated(streams), block, cuts)
        order.mark(out[0])
        return out

    def wgrad_of(rows_order, *parts):
        left, rights = parts[0]
        parts = [(left, [order.gate(rights[0])] + list(rights[1:]))] + list(parts[1:])
        return order.mark(wgrad(rows_order, parts))

    quarter = width // 4
    columns = query.shape[1]
    heights = [quarter >> (i + 1) for i in range(len(line))]
    d_final_s = sharded(d_final_t)

    ffn_all = wgrad_of(order_plane, (sharded(normed2_t), [d_gate, d_up]))
    ffn_sum = lax.psum_scatter(
        ffn_all, "dp", scatter_dimension=0, tiled=True, axis_index_groups=groups
    )
    down_leave = wgrad_of(order_zxy[:first], (d_final_s, [inner]))
    down_got = swap(down_leave, "dp", line[0])
    d_norm2_part = order.mark(product([order.gate(d_gate), d_up], [w_gate, w_up], True, BF))
    d_norm2_other = swap(d_norm2_part, "tensor", 0)
    down_stay = wgrad_of(order_zxy[first:], (d_final_s, [inner]))
    downs = [stream(down_stay, down_got)]
    d_hidden, d_branch_t, d_mixed, g_ffn_gain = order.mark(
        *branch_back(d_norm2_part, order.gate(d_norm2_other), hidden, d_final, ffn_gain, w_out)
    )
    branch = sharded(d_branch_t)

    out_leave = wgrad_of(order_xyz[:first], (branch, [mixed]))
    out_got = swap(out_leave, "dp", 0)

    d_four, d_logit, g_taps = order.mark(
        *mixer_backward(
            lengths, me1, logit, conv_taps, house, query, key, value, order.gate(d_mixed), kept
        )
    )
    plane_four = lax.all_to_all(d_four, "dp", 0, 0, axis_index_groups=groups)
    out_stay = wgrad_of(order_xyz[first:], (branch, [mixed]))
    height = width // 2
    for bit in line[1:]:
        height //= 2
        downs = leave(downs, height, bit)
    down_part = order.mark(product([order.gate(inner)], [w_down], False, BF))
    down_other = swap(down_part, "tensor", 0)
    outs = leave([stream(out_stay, out_got)], quarter, 1)
    d_norm1_part = order.mark(
        product(
            [(order.gate(d_four), i) for i in range(4)],
            [w_query, w_key, w_value, w_house], True, BF, small=(d_logit, w_beta),
        )
    )
    d_norm1_other = swap(d_norm1_part, "tensor", 0)
    dealt, deal_up, deal_down = order.mark(
        *rows_dealt(lengths, dealing, me1, hidden, *order.gate(down_part, down_other), slots, span)
    )
    input_grad, small = order.mark(
        *input_back(
            d_norm1_part, order.gate(d_norm1_other), tokens, d_hidden, attn_gain, g_taps, g_ffn_gain, d_logit
        )
    )
    lines = size // 4
    attn_leave = order.mark(
        wgrad_plane(order_line[: lines // 2], plane_normed, order.gate(plane_four), lines)
    )
    attn_got = swap(attn_leave, "dp", line[0])
    attn_stay = order.mark(
        wgrad_plane(order_line[lines // 2 :], plane_normed, order.gate(plane_four), lines)
    )
    ffns = leave([stream(ffn_sum)] + outs, heights[0], line[0])
    height //= 2
    downs = leave(downs, height, 0)
    out_low = lax.ppermute(deal_up, "dp", up)
    out_high = lax.ppermute(deal_down, "dp", down)
    attns = [stream(attn_stay, attn_got)]
    attn_height = width // 2
    for bit in line[1:]:
        attn_height //= 2
        attns = leave(attns, attn_height, bit)
    height //= 2
    downs = leave(downs, height, 1)
    for height, bit in zip(heights[1:], line[1:]):
        ffns = leave(ffns, height, bit)
    small_got = None

    def small_step(bit):
        nonlocal small, small_got
        if small_got is not None:
            small = order.mark(added(small, order.gate(small_got)))
        small_got = None if bit is None else swap(small, "dp", bit)

    small_bits = list(bits)
    small_step(small_bits.pop(0))
    attn_sum = order.mark(fold(gated(attns), width // lines)[0])
    plane_rows = lax.all_to_all(
        attn_sum.reshape(4, block, columns), "dp", 0, 0, axis_index_groups=groups
    )
    out_low, out_high = order.mark(*order.gate(out_low, out_high))
    small_step(small_bits.pop(0))
    (g_down,) = finish(downs, [1])
    while small_bits:
        small_step(small_bits.pop(0))
    small_step(None)
    g_gate, g_up, g_out = finish(ffns, [2, 1])
    g_query, g_key, g_value, g_house = order.gate(plane_rows).astype(F32)

    taps = conv_taps.shape[0]
    per_row = lax.dynamic_slice_in_dim(small[taps:], me * block, block, axis=1)
    taps_total = small[:taps, :columns]
    held_from = lax.dynamic_slice_in_dim(dealing, me * slots, slots) // slots - me
    output = jnp.where(
        (held_from == -1)[:, None, None],
        out_low[None],
        jnp.where(
            (held_from == 1)[:, None, None], out_high[None], dealt.reshape(slots, span, width)
        ),
    )
    return (
        output,
        input_grad,
        per_row[1],
        g_query,
        g_key,
        g_value,
        g_house,
        per_row[2 : 2 + d_logit.shape[0]].T,
        taps_total,
        g_out.T,
        per_row[0],
        g_gate,
        g_up,
        g_down.T,
    )


def solution(mesh):
    in_specs = (
        P("dp", None),
        P("dp", None, None),
        P(),
        P(),
        P(),
        P(None, "tensor"),
        P(None, "tensor"),
        P(None, "tensor"),
        P(None, "tensor"),
        P(None, "tensor"),
        P(None, "tensor"),
        P("tensor", None),
        P(),
        P(None, "tensor"),
        P(None, "tensor"),
        P("tensor", None),
    )
    out_specs = (
        P("dp", None, None),
        P("dp", None),
        P("dp"),
        P("dp", "tensor"),
        P("dp", "tensor"),
        P("dp", "tensor"),
        P("dp", "tensor"),
        P("dp", "tensor"),
        P(None, "tensor"),
        P("tensor", "dp"),
        P("dp"),
        P("dp", "tensor"),
        P("dp", "tensor"),
        P("tensor", "dp"),
    )
    return jax.shard_map(
        on_device, mesh=mesh, in_specs=in_specs, out_specs=out_specs, check_vma=False
    )
```

time: 571 us -> 482 us (0.84)
  Pallas kernels: 99.2 us -> 232 us
  other arithmetic: 84.6 us -> 3.35 us
  matrix products: 86.8 us -> 13.7 us
  waiting for transfers between devices: 201 us -> 146 us
  local copies, waits for them, and re-layouts: 32.9 us -> 19.4 us
  between operations: 5.77 us -> 14.7 us
  starting transfers between devices: 54.6 us -> 46.5 us
    pallas_call x18 -> x35, Pallas kernels: 99.2 us -> 232 us  [the longest x5 34.9 us: wgrad(): pl.pallas_call(functools.partial(wgrad_kernel, plan), grid_spec=pltpu.Pre...]
    ppermute x40 -> x18, waiting for transfers between devices: 179 us -> 110 us  [swap(): return lax.ppermute(x, axis, [(i, i ^ 1 << bit) for i in range(size)])]
    dot_general x14 -> x4, matrix products: 49.6 us -> 11.2 us  [dot_nn(): lax.dot_general(a, b, (((1,), (0,)), ((), ())), preferred_element_type=F32)]
    convert_element_type x24 -> x1, other arithmetic: 36.5 us -> 0.09 us  [on_device(): g_query, g_key, g_value, g_house = order.gate(plane_rows).astype(F32)]
    dot_general x10 -> x1, matrix products: 37.2 us -> 2.53 us  [on_device(): lax.dot_general(w_beta, normed, (((0,), (1,)), ((), ())), preferred_eleme...]
    all_to_all x0 -> x2, waiting for transfers between devices: none -> 24.2 us  [the longest x1 24.2 us: on_device(): plane_four = lax.all_to_all(d_four, 'dp', 0, 0, axis_index_groups=groups)]
    reduce_sum x10 -> x0, other arithmetic: 15.7 us -> none  [the longest x1 4.19 us: on_device(): g_ffn_gain = jnp.sum(d_norm2 * hidden * inverse2, axis=0)]
    ppermute x4, waiting for transfers between devices: 22 us -> 7.57 us  [the longest x1 6.01 us: on_device(): cot_high = lax.ppermute(cot_down, 'dp', down)]
  transfers between devices with their start and end apart: 44 -> 26, of which waited for: 24 -> 11; matrix products, arithmetic and copies ran while one was open for 25% -> 5% of each run, Pallas kernels for 12% -> 47%
where the time goes in v2:
time: 482 us; the launch traced here: 476 us
  Pallas kernels  232 us (48%)
  waiting for transfers between devices  146 us (30%)
  starting transfers between devices  46.5 us (10%)
  local copies, waits for them, and re-layouts  19.4 us (4%)
  between operations  14.7 us (3%)
  matrix products  13.7 us (3%)
    ppermute x18, waiting for transfers between devices, swap(): return lax.ppermute(x, axis, [(i, i ^ 1 << bit) for i in range(size)])  110 us
    pallas_call x5, Pallas kernels, wgrad(): pl.pallas_call(functools.partial(wgrad_kernel, plan), grid_spec=pltpu.Pre...  34.9 us
    pallas_call x4, Pallas kernels, product(): pl.pallas_call(functools.partial(product_kernel, len(lefts), turned, bool...  34.1 us
    pallas_call x10, Pallas kernels, fold(): pl.pallas_call(functools.partial(fold_kernel, plan, cuts), grid=(height /...  30.4 us
    pallas_call x1, Pallas kernels, mixer_forward(): pl.pallas_call(functools.partial(forward_kernel, heads, lengths.shape[1])...  29.4 us
    ppermute x18, starting transfers between devices, swap(): return lax.ppermute(x, axis, [(i, i ^ 1 << bit) for i in range(size)])  26.8 us
    all_to_all x1, waiting for transfers between devices, on_device(): plane_four = lax.all_to_all(d_four, 'dp', 0, 0, axis_index_groups=groups)  24.2 us
    pallas_call x1, Pallas kernels, mixer_backward(): pl.pallas_call(functools.partial(backward_kernel, heads, lengths.shape[1]...  21.3 us
  transfers between devices with their start and end apart: 26, of which 11 were waited for; matrix products, arithmetic and copies ran while one was open for 5% of the time, Pallas kernels for 47%

profile of v2, /device:TPU:0, one launch (start us, length us, event | category | flops | bytes accessed | tf_op | source)
XLA Modules:
  0.0 475.9 jit_solution(11948832282354985792)
XLA Ops:
  8.5 4.2 slots_to_send.1
  12.7 4.3 first_norm.1
  17.0 4.9 %collective-permute-start = (bf16[256,1536]{1,0:T(8,128)(2,1)}, bf16[256,1536]{1,0:T(8,128)(2,1)S(1)}, u32[]{:S(2)}, u32[]{:S(2)}) collective-permute-start(bf16[256,1536]{1,0:T(8,128)(2,1)} %get-tuple-element.110), channel_id=1, source_target_pairs={{0,2},{2,4},{4,6},{6,8},{8,10},{10,12},{12,14},{14,16},{16,18},{18... | collective-permute-start | bytes 2359304 | tf_op jit(solution)/shard_map/ppermute | solution.py:1023
  24.0 2.5 convolution_bitcast_fusion.logit_ref
  26.5 4.1 convolution_convert_fusion.v_ref
  30.6 2.3 convolution_convert_fusion.1.k_ref
  32.9 2.3 convolution_convert_fusion.2.q_ref
  35.2 2.5 fusion.5.house_ref
  37.7 29.4 %mixer_forward.1 = (bf16[512,768]{1,0:T(8,128)(2,1)}, bf16[6,8,256,256]{3,2,1,0:T(8,128)(2,1)}) custom-call(s32[16,3]{1,0:T(8,128)} %copy.37.lengths_ref, s32[1]{0:T(128)} %bitcast.me_ref, f32[6,512]{1,0:T(8,128)} %convolution_bitcast_fusion.logit_ref, f32[4,768]{1,0:T(4,128)} %taps_ref.3, f32[512,768]{1,0:T(8,128)} %fusion.5.house_ref, ...), custom_call_target="tpu_custom_call" | custom-call | tf_op jit(solution)/shard_map/mixer_forward/pallas_call | solution.py:201
  67.1 1.5 collective-permute-done.low_ref
  68.7 6.0 %collective-permute-done.1.high_ref = bf16[256,1536]{1,0:T(8,128)(2,1)} collective-permute-done((bf16[256,1536]{1,0:T(8,128)(2,1)}, bf16[256,1536]{1,0:T(8,128)(2,1)}, u32[]{:S(2)}, u32[]{:S(2)}) %collective-permute-start.1) | collective-permute-done | bytes 786464 | tf_op jit(solution)/shard_map/ppermute | solution.py:1024
  74.7 4.7 product.4.part_ref
  80.6 7.0 %cotangent_arrived.1 = (bf16[512,1536]{1,0:T(8,128)(2,1)}, bf16[1536,512]{1,0:T(8,128)(2,1)}) custom-call(s32[16,3]{1,0:T(8,128)} %copy.37.lengths_ref, s32[48]{0:T(128)} %dealing_ref.5, s32[1]{0:T(128)} %bitcast.me_ref, bf16[768,1536]{1,0:T(8,128)(2,1)} %bitcast.38, bf16[256,1536]{1,0:T(8,128)(2,1)} %copy-done.12, ...), custom_call_target="tpu_custom_call" | custom-call | tf_op jit(solution)/shard_map/cotangent_arrived/pallas_call | solution.py:467
  88.7 5.7 %hidden_and_norm.1 = (f32[512,1536]{1,0:T(8,128)}, bf16[512,1536]{1,0:T(8,128)(2,1)}, bf16[1536,512]{1,0:T(8,128)(2,1)}) custom-call(bf16[512,1536]{1,0:T(8,128)(2,1)} %tokens_ref.4, bf16[512,1536]{1,0:T(8,128)(2,1)} %product.4.part_ref, bf16[512,1536]{1,0:T(8,128)(2,1)} %copy-done.10, f32[1,1536]{1,0:T(1,128)} %broadcast_in_dim.42.gain_ref), custom_call_target="tpu_custom_call" | custom-call | tf_op jit(solution)/shard_map/hidden_and_norm/pallas_call | solution.py:581
  94.4 17.0 %ffn.1 = (bf16[512,2048]{1,0:T(8,128)(2,1)}, bf16[512,2048]{1,0:T(8,128)(2,1)}, bf16[512,2048]{1,0:T(8,128)(2,1)}) custom-call(bf16[512,1536]{1,0:T(8,128)(2,1)} %get-tuple-element.127.normed_ref, bf16[512,1536]{1,0:T(8,128)(2,1)} %get-tuple-element.121.d_final_ref, bf16[1536,2048]{1,0:T(8,128)(2,1)} %refs_2_.1, bf16[1536,2048]{1,0:T(8,128)(2,1)} %refs_3_.1, ...), custom_call_target="tpu_custom_call" | custom-call | tf_op jit(solution)/shard_map/ffn/pallas_call | solution.py:915
  111.4 13.4 %wgrad.5 = bf16[1536,4096]{1,0:T(8,128)(2,1)} custom-call(s32[16]{0:T(128)} %add.30.order_ref, bf16[16,96,512]{2,1,0:T(8,128)(2,1)} %bitcast.44, bf16[512,2048]{1,0:T(8,128)(2,1)} %get-tuple-element.133.refs_1_.refs_0_, bf16[512,2048]{1,0:T(8,128)(2,1)} %get-tuple-element.130.refs_2_.refs_1_), custom_call_target="tpu_custom_call" | custom-call | tf_op jit(solution)/shard_map/wgrad/pallas_call | solution.py:846
  126.1 6.4 %wgrad.6 = bf16[768,2048]{1,0:T(8,128)(2,1)} custom-call(s32[8]{0:T(128)} %get-tuple-element.219.order_ref, bf16[16,96,512]{2,1,0:T(8,128)(2,1)} %bitcast.39, bf16[512,2048]{1,0:T(8,128)(2,1)} %get-tuple-element.148.refs_1_.refs_0_), custom_call_target="tpu_custom_call" | custom-call | tf_op jit(solution)/shard_map/wgrad/pallas_call | solution.py:846
  132.5 1.7 collective-permute-start.3
  134.2 11.7 %product.5.part_ref = bf16[512,1536]{1,0:T(8,128)(2,1)} custom-call(bf16[512,2048]{1,0:T(8,128)(2,1)} %get-tuple-element.133.refs_1_.refs_0_, bf16[512,2048]{1,0:T(8,128)(2,1)} %get-tuple-element.130.refs_2_.refs_1_, bf16[1536,2048]{1,0:T(8,128)(2,1)} %refs_2_.1, bf16[1536,2048]{1,0:T(8,128)(2,1)} %refs_3_.1), custom_call_target="tpu_custom_call" | custom-call | tf_op jit(solution)/shard_map/product/pallas_call | solution.py:737
  146.5 6.4 %wgrad.7.refs_0_ = bf16[768,2048]{1,0:T(8,128)(2,1)} custom-call(s32[8]{0:T(128)} %get-tuple-element.220.order_ref, bf16[16,96,512]{2,1,0:T(8,128)(2,1)} %bitcast.40, bf16[512,2048]{1,0:T(8,128)(2,1)} %get-tuple-element.148.refs_1_.refs_0_), custom_call_target="tpu_custom_call" | custom-call | tf_op jit(solution)/shard_map/wgrad/pallas_call | solution.py:846
  152.9 9.3 %branch_back.1 = (f32[512,1536]{1,0:T(8,128)}, bf16[1536,512]{1,0:T(8,128)(2,1)}, bf16[512,768]{1,0:T(8,128)(2,1)}, f32[1,1536]{1,0:T(1,128)}) custom-call(bf16[512,1536]{1,0:T(8,128)(2,1)} %product.5.part_ref, bf16[512,1536]{1,0:T(8,128)(2,1)} %collective-permute-done.4.other_ref, f32[512,1536]{1,0:T(8,128)} %get-tuple-element.124.hidden_ref, ...), custom_call_target="tpu_custom_call" | custom-call | tf_op jit(solution)/shard_map/branch_back/pallas_call | solution.py:634
  162.3 4.3 wgrad.8
  168.0 21.3 %mixer_backward.1 = (bf16[4,512,768]{2,1,0:T(8,128)(2,1)}, f32[6,512]{1,0:T(8,128)}, f32[4,768]{1,0:T(4,128)}) custom-call(s32[16,3]{1,0:T(8,128)} %copy.37.lengths_ref, s32[1]{0:T(128)} %bitcast.me_ref, f32[6,512]{1,0:T(8,128)} %convolution_bitcast_fusion.logit_ref, f32[4,768]{1,0:T(4,128)} %taps_ref.3, f32[512,768]{1,0:T(8,128)} %fusion.5.house_ref, ...), custom_call_target="tpu_custom_call" | custom-call | tf_op jit(solution)/shard_map/mixer_backward/pallas_call | solution.py:346
  189.3 4.9 %all-to-all-start = ((bf16[4,512,768]{2,1,0:T(8,128)(2,1)}), bf16[4,512,768]{2,1,0:T(8,128)(2,1)}, u32[]{:S(2)}, u32[]{:S(2)}) async-start(bf16[4,512,768]{2,1,0:T(8,128)(2,1)} %get-tuple-element.151.refs_0_.refs_1_.refs_2_.refs_3_), calls=%async_computation | async-start | bytes 6291456 | tf_op jit(solution)/shard_map/all_to_all | solution.py:1108
  195.2 4.4 wgrad.9.refs_0_.refs_1_.refs_2_.refs_3_
  199.6 3.5 collective-permute-done.3.refs_1_
  203.1 1.7 copy-done
  204.8 4.0 fold.10
  208.8 7.4 %product.6.part_ref = bf16[512,1536]{1,0:T(8,128)(2,1)} custom-call(bf16[512,2048]{1,0:T(8,128)(2,1)} %get-tuple-element.148.refs_1_.refs_0_, bf16[2048,1536]{1,0:T(8,128)(2,1)} %refs_1_.3), custom_call_target="tpu_custom_call" | custom-call | tf_op jit(solution)/shard_map/product/pallas_call | solution.py:737
  216.2 4.8 %collective-permute-done.6.refs_1_.refs_2_.refs_3_.refs_4_ = bf16[768,768]{1,0:T(8,128)(2,1)} collective-permute-done((bf16[768,768]{1,0:T(8,128)(2,1)}, bf16[768,768]{1,0:T(8,128)(2,1)}, u32[]{:S(2)}, u32[]{:S(2)}) %collective-permute-start.6) | collective-permute-done | bytes 1179680 | tf_op jit(solution)/shard_map/ppermute | solution.py:929
  221.0 3.4 fold.11
  224.4 10.4 %product.7.part_ref = bf16[512,1536]{1,0:T(8,128)(2,1)} custom-call(bf16[4,512,768]{2,1,0:T(8,128)(2,1)} %get-tuple-element.151.refs_0_.refs_1_.refs_2_.refs_3_, bf16[4,512,768]{2,1,0:T(8,128)(2,1)} %get-tuple-element.151.refs_0_.refs_1_.refs_2_.refs_3_, bf16[4,512,768]{2,1,0:T(8,128)(2,1)} %get-tuple-element.151.refs_0_.refs_1_.refs_2_.refs_3_, ...), custom_call_target="tpu_custom_call" | custom-call | tf_op jit(solution)/shard_map/product/pallas_call | solution.py:737
  234.8 2.5 collective-permute-start.11
  239.3 8.5 %rows_dealt.1 = (bf16[768,1536]{1,0:T(8,128)(2,1)}, bf16[256,1536]{1,0:T(8,128)(2,1)}, bf16[256,1536]{1,0:T(8,128)(2,1)}) custom-call(s32[16,3]{1,0:T(8,128)} %copy.37.lengths_ref, s32[48]{0:T(128)} %dealing_ref.5, s32[1]{0:T(128)} %bitcast.me_ref, f32[512,1536]{1,0:T(8,128)} %get-tuple-element.124.hidden_ref, bf16[512,1536]{1,0:T(8,128)(2,1)} %product.6.part_ref, ...), custom_call_target="tpu_custom_call" | custom-call | tf_op jit(solution)/shard_map/rows_dealt/pallas_call | solution.py:523
  247.7 6.4 %input_back.1 = (bf16[512,1536]{1,0:T(8,128)(2,1)}, f32[16,1536]{1,0:T(8,128)}) custom-call(bf16[512,1536]{1,0:T(8,128)(2,1)} %product.7.part_ref, bf16[512,1536]{1,0:T(8,128)(2,1)} %collective-permute-done.9.other_ref, bf16[512,1536]{1,0:T(8,128)(2,1)} %tokens_ref.4, f32[512,1536]{1,0:T(8,128)} %get-tuple-element.138.d_hidden_ref, ...), custom_call_target="tpu_custom_call" | custom-call | tf_op jit(solution)/shard_map/input_back/pallas_call | solution.py:682
  254.1 24.2 %all-to-all-done.right_ref = bf16[4,512,768]{2,1,0:T(8,128)(2,1)} async-done(((bf16[4,512,768]{2,1,0:T(8,128)(2,1)}), bf16[4,512,768]{2,1,0:T(8,128)(2,1)}, u32[]{:S(2)}, u32[]{:S(2)}) %all-to-all-start) | async-done | bytes 3145760 | tf_op jit(solution)/shard_map/all_to_all | solution.py:1108
  278.3 6.7 %wgrad_plane.2 = bf16[768,768]{1,0:T(8,128)(2,1)} custom-call(s32[2]{0:T(128)} %get-tuple-element.213.order_ref, bf16[4,1536,512]{2,1,0:T(8,128)(2,1)} %bitcast.36, bf16[4,512,768]{2,1,0:T(8,128)(2,1)} %all-to-all-done.right_ref), custom_call_target="tpu_custom_call" | custom-call | tf_op jit(solution)/shard_map/wgrad_plane/pallas_call | solution.py:879
  285.0 6.8 %wgrad_plane.3.refs_0_ = bf16[768,768]{1,0:T(8,128)(2,1)} custom-call(s32[2]{0:T(128)} %get-tuple-element.214.order_ref, bf16[4,1536,512]{2,1,0:T(8,128)(2,1)} %bitcast.37, bf16[4,512,768]{2,1,0:T(8,128)(2,1)} %all-to-all-done.right_ref), custom_call_target="tpu_custom_call" | custom-call | tf_op jit(solution)/shard_map/wgrad_plane/pallas_call | solution.py:879
  291.8 4.1 reduce-scatter.2.cloned.1.call-done.refs_0_
  295.9 2.7 fold.12
  298.5 1.5 collective-permute-start.14
  300.6 5.9 %collective-permute-done.11.refs_2_ = bf16[384,2048]{1,0:T(8,128)(2,1)S(1)} collective-permute-done((bf16[384,2048]{1,0:T(8,128)(2,1)}, bf16[384,2048]{1,0:T(8,128)(2,1)S(1)}, u32[]{:S(2)}, u32[]{:S(2)}) %collective-permute-start.11) | collective-permute-done | bytes 1572896 | tf_op jit(solution)/shard_map/ppermute | solution.py:929
  307.7 2.5 fold.13
  310.1 4.6 collective-permute-start.15
  314.7 1.9 collective-permute-start.7
  318.0 53.9 %collective-permute-done.10.refs_1_ = bf16[768,768]{1,0:T(8,128)(2,1)} collective-permute-done((bf16[768,768]{1,0:T(8,128)(2,1)}, bf16[768,768]{1,0:T(8,128)(2,1)}, u32[]{:S(2)}, u32[]{:S(2)}) %collective-permute-start.10) | collective-permute-done | bytes 1179680 | tf_op jit(solution)/shard_map/ppermute | solution.py:929
  371.9 3.4 fold.14
  377.1 2.3 fold.15
  380.7 4.0 collective-permute-start.16
  384.7 2.7 fold.16
  387.5 16.9 %collective-permute-done.13.refs_2_ = bf16[384,768]{1,0:T(8,128)(2,1)} collective-permute-done((bf16[384,768]{1,0:T(8,128)(2,1)}, bf16[384,768]{1,0:T(8,128)(2,1)}, u32[]{:S(2)}, u32[]{:S(2)}) %collective-permute-start.13) | collective-permute-done | bytes 589856 | tf_op jit(solution)/shard_map/ppermute | solution.py:929
  404.3 3.6 fold.17
  408.6 1.6 added.4.a_ref
  412.4 2.7 fold.18
  415.8 1.6 added.5.a_ref
  417.4 2.4 collective-permute-start.19
  419.8 5.2 %all-to-all-start.1 = ((bf16[4,96,768]{2,1,0:T(8,128)(2,1)}), bf16[4,96,768]{2,1,0:T(8,128)(2,1)S(1)}, u32[]{:S(2)}, u32[]{:S(2)}) async-start(bf16[4,96,768]{2,1,0:T(8,128)(2,1)} %bitcast.9), calls=%async_computation.2 | async-start | bytes 1179648 | tf_op jit(solution)/shard_map/all_to_all | solution.py:1165
  425.0 9.0 %collective-permute-done.19.b_ref = f32[16,1536]{1,0:T(8,128)S(1)} collective-permute-done((f32[16,1536]{1,0:T(8,128)}, f32[16,1536]{1,0:T(8,128)S(1)}, u32[]{:S(2)}, u32[]{:S(2)}) %collective-permute-start.19) | collective-permute-done | bytes 98336 | tf_op jit(solution)/shard_map/ppermute | solution.py:929
  434.7 1.6 added.6.a_ref
  436.3 3.0 collective-permute-start.20
  439.3 3.2 select_select_fusion
  442.5 16.1 %collective-permute-done.20.b_ref = f32[16,1536]{1,0:T(8,128)S(1)} collective-permute-done((f32[16,1536]{1,0:T(8,128)}, f32[16,1536]{1,0:T(8,128)S(1)}, u32[]{:S(2)}, u32[]{:S(2)}) %collective-permute-start.20) | collective-permute-done | bytes 98336 | tf_op jit(solution)/shard_map/ppermute | solution.py:929
  459.2 1.6 added.7
  464.3 3.2 fold.19
  (106 shorter events, 27.7 us)
Async XLA Ops:
  7.2 271.1 %all-gather.3.cloned.1.call-start = ((), (), s32[]{:S(2)}) async-start(), calls=%async_computation.4 | async-start | bytes 7864320 | tf_op jit(solution)/shard_map/all_gather | solution.py:1027
  12.7 10.6 %copy-start.24 = (s32[16,3]{0,1:T(4,128)S(1)}, s32[16,3]{0,1:T(4,128)}, u32[]{:S(2)}) copy-start(s32[16,3]{0,1:T(4,128)} %param.21) | copy-start | bytes 580
  12.7 11.3 %copy-start.21 = (bf16[1536,6]{0,1:T(8,128)(2,1)S(1)}, bf16[1536,6]{0,1:T(8,128)(2,1)}, u32[]{:S(2)}) copy-start(bf16[1536,6]{0,1:T(8,128)(2,1)} %param.28) | copy-start | bytes 55300
  17.0 9.5 %copy-start.8 = (bf16[1536,768]{1,0:T(8,128)(2,1)S(1)}, bf16[1536,768]{1,0:T(8,128)(2,1)}, u32[]{:S(2)}) copy-start(bf16[1536,768]{1,0:T(8,128)(2,1)} %refs_6_.1) | copy-start | bytes 7077892
  17.0 278.9 %reduce-scatter.2.cloned.1.call-start = ((), (), s32[]{:S(2)}) async-start(), calls=%async_computation.3 | async-start | bytes 15728640 | tf_op jit(solution)/shard_map/reduce_scatter | solution.py:1086
  17.0 51.6 %collective-permute-start = (bf16[256,1536]{1,0:T(8,128)(2,1)}, bf16[256,1536]{1,0:T(8,128)(2,1)S(1)}, u32[]{:S(2)}, u32[]{:S(2)}) collective-permute-start(bf16[256,1536]{1,0:T(8,128)(2,1)} %get-tuple-element.110), channel_id=1, source_target_pairs={{0,2},{2,4},{4,6},{6,8},{8,10},{10,12},{12,14},{14,16},{16,18},{18... | collective-permute-start | bytes 2359304 | tf_op jit(solution)/shard_map/ppermute | solution.py:1023
  22.0 52.7 %collective-permute-start.1 = (bf16[256,1536]{1,0:T(8,128)(2,1)}, bf16[256,1536]{1,0:T(8,128)(2,1)}, u32[]{:S(2)}, u32[]{:S(2)}) collective-permute-start(bf16[256,1536]{1,0:T(8,128)(2,1)} %get-tuple-element.111), channel_id=1, source_target_pairs={{2,0},{4,2},{6,4},{8,6},{10,8},{12,10},{14,12},{16,14},{18,16},{20... | collective-permute-start | bytes 2359304 | tf_op jit(solution)/shard_map/ppermute | solution.py:1024
  26.5 4.1 copy-start.7
  26.5 4.1 copy-start.11
  30.6 2.3 copy-start.6
  32.9 2.3 copy-start.5
  68.7 10.7 %copy-start.12 = (bf16[256,1536]{1,0:T(8,128)(2,1)}, bf16[256,1536]{1,0:T(8,128)(2,1)S(1)}, u32[]{:S(2)}) copy-start(bf16[256,1536]{1,0:T(8,128)(2,1)S(1)} %collective-permute-done.low_ref) | copy-start | bytes 2359300
  74.7 4.7 copy-start.27
  74.7 5.3 %copy-start.22 = (f32[1536]{0:T(1024)S(1)}, f32[1536]{0:T(1024)}, u32[]{:S(2)}) copy-start(f32[1536]{0:T(1024)} %param.31) | copy-start | bytes 18436
  79.4 8.2 %collective-permute-start.2 = (bf16[512,1536]{1,0:T(8,128)(2,1)}, bf16[512,1536]{1,0:T(8,128)(2,1)S(1)}, u32[]{:S(2)}, u32[]{:S(2)}) collective-permute-start(bf16[512,1536]{1,0:T(8,128)(2,1)} %product.4.part_ref), channel_id=1, source_target_pairs={{0,1},{1,0},{2,3},{3,2},{4,5},{5,4},{6,7},{7,6},{8,9},{9,8},{10,11... | collective-permute-start | bytes 4718600 | tf_op jit(solution)/shard_map/ppermute | solution.py:929
  87.6 1.2 copy-start.10
  124.8 0.7 copy-start.25
  124.8 0.7 copy-start.26
  132.5 70.6 %collective-permute-start.3 = (bf16[768,2048]{1,0:T(8,128)(2,1)}, bf16[768,2048]{1,0:T(8,128)(2,1)S(1)}, u32[]{:S(2)}, u32[]{:S(2)}) collective-permute-start(bf16[768,2048]{1,0:T(8,128)(2,1)} %wgrad.6), channel_id=1, source_target_pairs={{0,8},{2,10},{4,12},{6,14},{8,0},{10,2},{12,4},{14,6},{16,24},{18,... | collective-permute-start | bytes 9437192 | tf_op jit(solution)/shard_map/ppermute | solution.py:929
  145.9 7.1 %collective-permute-start.4 = (bf16[512,1536]{1,0:T(8,128)(2,1)}, bf16[512,1536]{1,0:T(8,128)(2,1)}, u32[]{:S(2)}, u32[]{:S(2)}) collective-permute-start(bf16[512,1536]{1,0:T(8,128)(2,1)} %product.5.part_ref), channel_id=1, source_target_pairs={{0,1},{1,0},{2,3},{3,2},{4,5},{5,4},{6,7},{7,6},{8,9},{9,8},{10,11... | collective-permute-start | bytes 4718600 | tf_op jit(solution)/shard_map/ppermute | solution.py:929
  166.6 54.4 %collective-permute-start.6 = (bf16[768,768]{1,0:T(8,128)(2,1)}, bf16[768,768]{1,0:T(8,128)(2,1)}, u32[]{:S(2)}, u32[]{:S(2)}) collective-permute-start(bf16[768,768]{1,0:T(8,128)(2,1)} %wgrad.8), channel_id=1, source_target_pairs={{0,2},{2,0},{4,6},{6,4},{8,10},{10,8},{12,14},{14,12},{16,18},{18,... | collective-permute-start | bytes 3538952 | tf_op jit(solution)/shard_map/ppermute | solution.py:929
  189.3 89.0 %all-to-all-start = ((bf16[4,512,768]{2,1,0:T(8,128)(2,1)}), bf16[4,512,768]{2,1,0:T(8,128)(2,1)}, u32[]{:S(2)}, u32[]{:S(2)}) async-start(bf16[4,512,768]{2,1,0:T(8,128)(2,1)} %get-tuple-element.151.refs_0_.refs_1_.refs_2_.refs_3_), calls=%async_computation | async-start | bytes 6291456 | tf_op jit(solution)/shard_map/all_to_all | solution.py:1108
  203.1 1.7 copy-start
  216.2 23.1 %collective-permute-start.5 = (bf16[512,1536]{1,0:T(8,128)(2,1)}, bf16[512,1536]{1,0:T(8,128)(2,1)}, u32[]{:S(2)}, u32[]{:S(2)}) collective-permute-start(bf16[512,1536]{1,0:T(8,128)(2,1)} %product.6.part_ref), channel_id=1, source_target_pairs={{0,1},{1,0},{2,3},{3,2},{4,5},{5,4},{6,7},{7,6},{8,9},{9,8},{10,11... | collective-permute-start | bytes 4718600 | tf_op jit(solution)/shard_map/ppermute | solution.py:929
  224.4 12.9 %copy-start.14 = (bf16[384,768]{1,0:T(8,128)(2,1)S(1)}, bf16[384,768]{1,0:T(8,128)(2,1)}, u32[]{:S(2)}) copy-start(bf16[384,768]{1,0:T(8,128)(2,1)} %fold.11) | copy-start | bytes 1769476
  234.7 13.0 %collective-permute-start.9 = (bf16[512,1536]{1,0:T(8,128)(2,1)}, bf16[512,1536]{1,0:T(8,128)(2,1)}, u32[]{:S(2)}, u32[]{:S(2)}) collective-permute-start(bf16[512,1536]{1,0:T(8,128)(2,1)} %product.7.part_ref), channel_id=1, source_target_pairs={{0,1},{1,0},{2,3},{3,2},{4,5},{5,4},{6,7},{7,6},{8,9},{9,8},{10,11... | collective-permute-start | bytes 4718600 | tf_op jit(solution)/shard_map/ppermute | solution.py:929
  234.8 71.7 %collective-permute-start.11 = (bf16[384,2048]{1,0:T(8,128)(2,1)}, bf16[384,2048]{1,0:T(8,128)(2,1)S(1)}, u32[]{:S(2)}, u32[]{:S(2)}) collective-permute-start(bf16[384,2048]{1,0:T(8,128)(2,1)} %fold.10), channel_id=1, source_target_pairs={{0,16},{2,18},{4,20},{6,22},{8,24},{10,26},{12,28},{14,30},{16,0},... | collective-permute-start | bytes 4718600 | tf_op jit(solution)/shard_map/ppermute | solution.py:929
  237.3 54.5 %collective-permute-start.12 = (bf16[384,768]{1,0:T(8,128)(2,1)S(1)}, bf16[384,768]{1,0:T(8,128)(2,1)S(1)}, u32[]{:S(2)}, u32[]{:S(2)}) collective-permute-start(bf16[384,768]{1,0:T(8,128)(2,1)S(1)} %copy-done.14), channel_id=1, source_target_pairs={{0,4},{2,6},{4,0},{6,2},{8,12},{10,14},{12,8},{14,10},{16,20},{18,... | collective-permute-start | bytes 1769480 | tf_op jit(solution)/shard_map/ppermute | solution.py:929
  291.8 4.1 copy-start.3
  298.5 82.2 %collective-permute-start.14 = (bf16[192,4864]{1,0:T(8,128)(2,1)}, bf16[192,4864]{1,0:T(8,128)(2,1)S(1)}, u32[]{:S(2)}, u32[]{:S(2)}) collective-permute-start(bf16[192,4864]{1,0:T(8,128)(2,1)} %fold.12), channel_id=1, source_target_pairs={{0,8},{2,10},{4,12},{6,14},{8,0},{10,2},{12,4},{14,6},{16,24},{18,... | collective-permute-start | bytes 5603336 | tf_op jit(solution)/shard_map/ppermute | solution.py:929
  300.0 71.8 %collective-permute-start.10 = (bf16[768,768]{1,0:T(8,128)(2,1)}, bf16[768,768]{1,0:T(8,128)(2,1)}, u32[]{:S(2)}, u32[]{:S(2)}) collective-permute-start(bf16[768,768]{1,0:T(8,128)(2,1)} %wgrad_plane.2), channel_id=1, source_target_pairs={{0,8},{2,10},{4,12},{6,14},{8,0},{10,2},{12,4},{14,6},{16,24},{18,... | collective-permute-start | bytes 3538952 | tf_op jit(solution)/shard_map/ppermute | solution.py:929
  306.5 1.2 copy-start.1
  310.1 66.1 %collective-permute-start.15 = (bf16[192,2048]{1,0:T(8,128)(2,1)}, bf16[192,2048]{1,0:T(8,128)(2,1)S(1)}, u32[]{:S(2)}, u32[]{:S(2)}) collective-permute-start(bf16[192,2048]{1,0:T(8,128)(2,1)} %fold.13), channel_id=1, source_target_pairs={{0,2},{2,0},{4,6},{6,4},{8,10},{10,8},{12,14},{14,12},{16,18},{18,... | collective-permute-start | bytes 2359304 | tf_op jit(solution)/shard_map/ppermute | solution.py:929
  314.7 93.2 %collective-permute-start.7 = (bf16[256,1536]{1,0:T(8,128)(2,1)}, bf16[256,1536]{1,0:T(8,128)(2,1)S(1)}, u32[]{:S(2)}, u32[]{:S(2)}) collective-permute-start(bf16[256,1536]{1,0:T(8,128)(2,1)} %get-tuple-element.154), channel_id=1, source_target_pairs={{0,2},{2,4},{4,6},{6,8},{8,10},{10,12},{12,14},{14,16},{16,18},{18... | collective-permute-start | bytes 2359304 | tf_op jit(solution)/shard_map/ppermute | solution.py:1143
  316.7 91.2 %collective-permute-start.8 = (bf16[256,1536]{1,0:T(8,128)(2,1)}, bf16[256,1536]{1,0:T(8,128)(2,1)}, u32[]{:S(2)}, u32[]{:S(2)}) collective-permute-start(bf16[256,1536]{1,0:T(8,128)(2,1)} %get-tuple-element.155), channel_id=1, source_target_pairs={{2,0},{4,2},{6,4},{8,6},{10,8},{12,10},{14,12},{16,14},{18,16},{20... | collective-permute-start | bytes 2359304 | tf_op jit(solution)/shard_map/ppermute | solution.py:1144
  375.3 5.4 %copy-start.16 = (f32[16,1536]{1,0:T(8,128)S(1)}, f32[16,1536]{1,0:T(8,128)}, u32[]{:S(2)}) copy-start(f32[16,1536]{1,0:T(8,128)} %get-tuple-element.160.a_ref) | copy-start | bytes 294916
  375.3 29.1 %collective-permute-start.13 = (bf16[384,768]{1,0:T(8,128)(2,1)}, bf16[384,768]{1,0:T(8,128)(2,1)}, u32[]{:S(2)}, u32[]{:S(2)}) collective-permute-start(bf16[384,768]{1,0:T(8,128)(2,1)} %fold.14), channel_id=1, source_target_pairs={{0,16},{2,18},{4,20},{6,22},{8,24},{10,26},{12,28},{14,30},{16,0},... | collective-permute-start | bytes 1769480 | tf_op jit(solution)/shard_map/ppermute | solution.py:929
  376.2 0.9 copy-start.4
  379.4 32.3 %collective-permute-start.18 = (bf16[96,2048]{1,0:T(8,128)(2,1)}, bf16[96,2048]{1,0:T(8,128)(2,1)S(1)}, u32[]{:S(2)}, u32[]{:S(2)}) collective-permute-start(bf16[96,2048]{1,0:T(8,128)(2,1)} %fold.15), channel_id=1, source_target_pairs={{0,4},{2,6},{4,0},{6,2},{8,12},{10,14},{12,8},{14,10},{16,20},{18,... | collective-permute-start | bytes 1179656 | tf_op jit(solution)/shard_map/ppermute | solution.py:929
  380.7 4.0 copy-start.2
  380.7 27.2 %collective-permute-start.16 = (f32[16,1536]{1,0:T(8,128)S(1)}, f32[16,1536]{1,0:T(8,128)S(1)}, u32[]{:S(2)}, u32[]{:S(2)}) collective-permute-start(f32[16,1536]{1,0:T(8,128)S(1)} %copy-done.16), channel_id=1, source_target_pairs={{0,2},{2,0},{4,6},{6,4},{8,10},{10,8},{12,14},{14,12},{16,18},{18,... | collective-permute-start | bytes 294920 | tf_op jit(solution)/shard_map/ppermute | solution.py:929
  387.5 24.1 %copy-start.23 = (s32[48]{0:T(128)S(1)}, s32[48]{0:T(128)}, u32[]{:S(2)}) copy-start(s32[48]{0:T(128)} %dealing_ref.5) | copy-start | bytes 580
  407.9 3.8 copy-start.13
  407.9 0.7 copy-start.17
  410.2 5.0 %collective-permute-start.17 = (f32[16,1536]{1,0:T(8,128)}, f32[16,1536]{1,0:T(8,128)S(1)}, u32[]{:S(2)}, u32[]{:S(2)}) collective-permute-start(f32[16,1536]{1,0:T(8,128)} %added.4.a_ref), channel_id=1, source_target_pairs={{0,4},{2,6},{4,0},{6,2},{8,12},{10,14},{12,8},{14,10},{16,20},{18,... | collective-permute-start | bytes 294920 | tf_op jit(solution)/shard_map/ppermute | solution.py:929
  411.6 52.7 %collective-permute-start.21 = (bf16[96,4864]{1,0:T(8,128)(2,1)}, bf16[96,4864]{1,0:T(8,128)(2,1)}, u32[]{:S(2)}, u32[]{:S(2)}) collective-permute-start(bf16[96,4864]{1,0:T(8,128)(2,1)} %fold.16), channel_id=1, source_target_pairs={{0,16},{2,18},{4,20},{6,22},{8,24},{10,26},{12,28},{14,30},{16,0},... | collective-permute-start | bytes 2801672 | tf_op jit(solution)/shard_map/ppermute | solution.py:929
  411.7 0.7 copy-start.15
  412.4 26.8 %copy-start.9 = (bf16[768,1536]{1,0:T(8,128)(2,1)S(1)}, bf16[768,1536]{1,0:T(8,128)(2,1)}, u32[]{:S(2)}) copy-start(bf16[768,1536]{1,0:T(8,128)(2,1)} %get-tuple-element.157) | copy-start | bytes 7077892
  415.2 0.6 copy-start.19
  417.4 16.6 %collective-permute-start.19 = (f32[16,1536]{1,0:T(8,128)}, f32[16,1536]{1,0:T(8,128)S(1)}, u32[]{:S(2)}, u32[]{:S(2)}) collective-permute-start(f32[16,1536]{1,0:T(8,128)} %added.5.a_ref), channel_id=1, source_target_pairs={{0,8},{2,10},{4,12},{6,14},{8,0},{10,2},{12,4},{14,6},{16,24},{18,... | collective-permute-start | bytes 294920 | tf_op jit(solution)/shard_map/ppermute | solution.py:929
  419.8 47.7 %all-to-all-start.1 = ((bf16[4,96,768]{2,1,0:T(8,128)(2,1)}), bf16[4,96,768]{2,1,0:T(8,128)(2,1)S(1)}, u32[]{:S(2)}, u32[]{:S(2)}) async-start(bf16[4,96,768]{2,1,0:T(8,128)(2,1)} %bitcast.9), calls=%async_computation.2 | async-start | bytes 1179648 | tf_op jit(solution)/shard_map/all_to_all | solution.py:1165
  434.0 0.6 copy-start.18
  436.3 22.3 %collective-permute-start.20 = (f32[16,1536]{1,0:T(8,128)}, f32[16,1536]{1,0:T(8,128)S(1)}, u32[]{:S(2)}, u32[]{:S(2)}) collective-permute-start(f32[16,1536]{1,0:T(8,128)} %added.6.a_ref), channel_id=1, source_target_pairs={{0,16},{2,18},{4,20},{6,22},{8,24},{10,26},{12,28},{14,30},{16,0},... | collective-permute-start | bytes 294920 | tf_op jit(solution)/shard_map/ppermute | solution.py:929
  458.6 0.6 copy-start.20
Sparse Core Ops, SparseCore 0:
  17.1 99.3 all-gather.2
  125.0 170.8 reduce-scatter.1

commit v3 on v2

--- a/solution.py
+++ b/solution.py
@@ -12,6 +12,7 @@
 
 VMEM = 60 << 20
 COST = pl.CostEstimate(flops=0, bytes_accessed=0, transcendentals=0)
+MORE = pl.CostEstimate(flops=1_000_000_000, bytes_accessed=1_000_000, transcendentals=0)
 
 
 def dot_nn(a, b):
@@ -31,60 +32,59 @@
     return high, (x - high.astype(F32)).astype(BF)
 
 
-def dot_split(a, b):
-    a_high, a_low = halves(a)
-    b_high, b_low = halves(b)
-    return dot_nn(a_high, b_high) + (dot_nn(a_high, b_low) + dot_nn(a_low, b_high))
-
-
-def unit_lower_inverse(strict, base):
-    size = strict.shape[0]
-    lanes = 128
-    tiles = size // lanes
-    per_tile = lanes // base
+def split_product(a, b):
+    return dot_nn(a[0], b[0]) + (dot_nn(a[0], b[1]) + dot_nn(a[1], b[0]))
+
+
+def unit_lower_inverses(stricts, base):
+    size, lanes = stricts[0].shape[0], 128
+    tiles, per_tile = size // lanes, lanes // base
     lane = lax.broadcasted_iota(jnp.int32, (base, lanes), 1)
     row = lax.broadcasted_iota(jnp.int32, (base, lanes), 0)
-    owner = lane // base
-    within = lane % base
+    owner, within = lane // base, lane % base
+    pieces = [
+        strict[t * lanes : (t + 1) * lanes, t * lanes : (t + 1) * lanes]
+        for strict in stricts
+        for t in range(tiles)
+    ]
     compact = []
-    for tile in range(tiles):
-        piece = jnp.zeros((base, lanes), F32)
+    for piece in pieces:
+        packed = jnp.zeros((base, lanes), F32)
         for block in range(per_tile):
-            top = tile * lanes + block * base
-            piece = jnp.where(
-                owner == block, strict[top : top + base, tile * lanes : (tile + 1) * lanes], piece
-            )
-        compact.append(piece)
-    solved = [jnp.where(row == within, 1.0, 0.0).astype(F32) for _ in range(tiles)]
+            packed = jnp.where(owner == block, piece[block * base : (block + 1) * base], packed)
+        compact.append(packed)
+    solved = [jnp.where(row == within, 1.0, 0.0).astype(F32)] * len(pieces)
     for step in range(base - 1):
         index = owner * base + step
-        for tile in range(tiles):
-            weight = jnp.take_along_axis(compact[tile], index, axis=1)
-            solved[tile] = solved[tile] - weight * solved[tile][step : step + 1, :]
-    rows = []
-    for tile in range(tiles):
-        for block in range(per_tile):
-            piece = jnp.where(owner == block, solved[tile], 0.0)
-            parts = [jnp.zeros((base, lanes), F32)] * tiles
-            parts[tile] = piece
-            rows.append(jnp.concatenate(parts, axis=1))
-    inverse = jnp.concatenate(rows, axis=0)
+        solved = [
+            s - jnp.take_along_axis(c, index, axis=1) * s[step : step + 1, :]
+            for s, c in zip(solved, compact)
+        ]
+    inverses = [
+        jnp.concatenate([jnp.where(owner == b, s, 0.0) for b in range(per_tile)], axis=0)
+        for s in solved
+    ]
     grown = base * 2
-    row_big = lax.broadcasted_iota(jnp.int32, (size, size), 0)
-    col_big = lax.broadcasted_iota(jnp.int32, (size, size), 1)
-    while grown < size:
-        joined = (row_big // grown == col_big // grown) & (
-            row_big // (grown // 2) != col_big // (grown // 2)
-        )
-        cross = jnp.where(joined, strict, 0.0)
-        inverse = inverse - dot_split(dot_split(inverse, cross), inverse)
+    row = lax.broadcasted_iota(jnp.int32, (lanes, lanes), 0)
+    col = lax.broadcasted_iota(jnp.int32, (lanes, lanes), 1)
+    while grown <= lanes:
+        joined = (row // grown == col // grown) & (row // (grown // 2) != col // (grown // 2))
+        parts = [halves(i) for i in inverses]
+        crosses = [halves(jnp.where(joined, p, 0.0)) for p in pieces]
+        firsts = [halves(split_product(p, c)) for p, c in zip(parts, crosses)]
+        inverses = [i - split_product(f, p) for i, f, p in zip(inverses, firsts, parts)]
         grown *= 2
-    half = size // 2
-    first, second = inverse[:half, :half], inverse[half:, half:]
-    corner = -dot_split(dot_split(second, strict[half:, :half]), first)
-    top = jnp.concatenate([first, jnp.zeros((half, half), F32)], axis=1)
-    bottom = jnp.concatenate([corner, second], axis=1)
-    return jnp.concatenate([top, bottom], axis=0)
+    whole = []
+    parts = [halves(i) for i in inverses]
+    corners = [halves(strict[lanes:, :lanes]) for strict in stricts]
+    firsts = [halves(split_product(parts[2 * n + 1], c)) for n, c in enumerate(corners)]
+    for n, first in enumerate(firsts):
+        corner = -split_product(first, parts[2 * n])
+        top = jnp.concatenate([inverses[2 * n], jnp.zeros((lanes, lanes), F32)], axis=1)
+        whole.append(
+            jnp.concatenate([top, jnp.concatenate([corner, inverses[2 * n + 1]], axis=1)], axis=0)
+        )
+    return whole
 
 
 def shifted_rows(x, amount, place):
@@ -100,6 +100,17 @@
 
 
 PAIRS = ((0, 0), (1, 0), (1, 1))
+
+
+def masks_of(begin, half, a, b):
+    inside = lax.broadcasted_iota(jnp.int32, (half, half), 1) + b * half >= begin[
+        a * half : (a + 1) * half
+    ]
+    if a != b:
+        return inside, inside
+    col = lax.broadcasted_iota(jnp.int32, (half, half), 1)
+    row = lax.broadcasted_iota(jnp.int32, (half, half), 0)
+    return inside & (col <= row), inside & (col < row)
 
 
 def scores_of(query, key, house_dir, begin, half, a, b):
@@ -122,57 +133,64 @@
     )
 
 
-def forward_head(query, key, value, house, logit, taps, begin, place):
-    half = query.shape[0] // 2
-    scaling = query.shape[1] ** (-0.5)
-    conv, inverse = direction(house, taps, place)
-    house_dir = (conv * inverse).astype(BF)
-    beta = 2.0 * jax.nn.sigmoid(logit)
-    raw, cross, know, gram, upto = {}, {}, {}, {}, {}
+def forward_heads(items, begin, place):
+    half = items[0][0].shape[0] // 2
+    scaling = items[0][0].shape[1] ** (-0.5)
+    both = (slice(0, half), slice(half, 2 * half))
+    upto, before = {}, {}
     for a, b in PAIRS:
-        raw[a, b], x, know[a, b], g, upto[a, b], _ = scores_of(
-            query, key, house_dir, begin, half, a, b
-        )
-        beta_cols = beta[:, b * half : (b + 1) * half]
-        cross[a, b] = (x * beta_cols).astype(BF)
-        gram[a, b] = g * beta_cols
+        upto[a, b], before[a, b] = masks_of(begin, half, a, b)
+    heads = []
+    for query, key, value, house, logit, taps in items:
+        conv, inverse = direction(house, taps, place)
+        house_dir = (conv * inverse).astype(BF)
+        beta = 2.0 * jax.nn.sigmoid(logit)
+        cross, know, gram = {}, {}, {}
+        for a, b in PAIRS:
+            left = jnp.concatenate([query[both[a]], house_dir[both[a]]], axis=0)
+            every = dot_nt(left, house_dir[both[b]])
+            beta_cols = beta[:, both[b]]
+            cross[a, b] = jnp.where(upto[a, b], every[:half] * -beta_cols, 0.0).astype(BF)
+            gram[a, b] = jnp.where(before[a, b], every[half:] * beta_cols, 0.0)
+            know[a, b] = jnp.where(
+                before[a, b], dot_nt(house_dir[both[a]], key[both[b]]), 0.0
+            )
+        heads.append((cross, know, gram, query, key.T, value))
+    inverses = unit_lower_inverses([h[2][a, a] for h in heads for a in (0, 1)], 16)
     eye = (
         lax.broadcasted_iota(jnp.int32, (half, half), 0)
         == lax.broadcasted_iota(jnp.int32, (half, half), 1)
     )
-    tail = {}
-    for a in (0, 1):
-        tail[a] = jnp.where(eye, 0.0, unit_lower_inverse(gram[a, a], 32)).astype(BF)
-    z00 = know[0, 0] + dot_nn(tail[0], know[0, 0].astype(BF))
-    z00b = z00.astype(BF)
-    z11 = know[1, 1] + dot_nn(tail[1], know[1, 1].astype(BF))
-    z11b = z11.astype(BF)
-    rest = know[1, 0] - dot_nn(gram[1, 0].astype(BF), z00b)
-    z10 = rest + dot_nn(tail[1], rest.astype(BF))
-    z10b = z10.astype(BF)
-    s00 = raw[0, 0] - dot_nn(cross[0, 0], z00b)
-    s10 = raw[1, 0] - dot_nn(cross[1, 0], z00b) - dot_nn(cross[1, 1], z10b)
-    s11 = raw[1, 1] - dot_nn(cross[1, 1], z11b)
-    s00 = jnp.where(upto[0, 0], s00 * scaling, -1e30)
-    s10 = jnp.where(upto[1, 0], s10 * scaling, -1e30)
-    s11 = jnp.where(upto[1, 1], s11 * scaling, -1e30)
-    top0 = jnp.max(s00, axis=1, keepdims=True)
-    top1 = jnp.maximum(
-        jnp.max(s10, axis=1, keepdims=True), jnp.max(s11, axis=1, keepdims=True)
-    )
-    e00, e10, e11 = jnp.exp(s00 - top0), jnp.exp(s10 - top1), jnp.exp(s11 - top1)
-    sum0 = jnp.sum(e00, axis=1, keepdims=True)
-    sum1 = jnp.sum(e10, axis=1, keepdims=True) + jnp.sum(e11, axis=1, keepdims=True)
-    inv0, inv1 = 1.0 / sum0, 1.0 / sum1
-    p00, p10, p11 = (
-        (e00 * inv0).astype(BF),
-        (e10 * inv1).astype(BF),
-        (e11 * inv1).astype(BF),
-    )
-    mixed0 = dot_nn(p00, value[:half])
-    mixed1 = dot_nn(p10, value[:half]) + dot_nn(p11, value[half:])
-    mixed = jnp.concatenate([mixed0, mixed1], axis=0).astype(BF)
-    return mixed, (p00, p10, p11, z00b, z10b, z11b, tail[0], tail[1])
+    tails = [jnp.where(eye, 0.0, i).astype(BF) for i in inverses]
+    results = []
+    for n, (cross, know, gram, query, key_t, value) in enumerate(heads):
+        tail0, tail1 = tails[2 * n : 2 * n + 2]
+        z00 = (know[0, 0] + dot_nn(tail0, know[0, 0].astype(BF))).astype(BF)
+        z11 = (know[1, 1] + dot_nn(tail1, know[1, 1].astype(BF))).astype(BF)
+        rest = know[1, 0] - dot_nn(gram[1, 0].astype(BF), z00)
+        z10 = (rest + dot_nn(tail1, rest.astype(BF))).astype(BF)
+
+        def score(pair, lefts, rights):
+            out = dot_nn(jnp.concatenate(lefts, axis=1), jnp.concatenate(rights, axis=0))
+            return jnp.where(upto[pair], out * scaling, -1e30)
+
+        q0, q1 = query[both[0]], query[both[1]]
+        s00 = score((0, 0), [q0, cross[0, 0]], [key_t[:, both[0]], z00])
+        s10 = score((1, 0), [q1, cross[1, 0], cross[1, 1]], [key_t[:, both[0]], z00, z10])
+        s11 = score((1, 1), [q1, cross[1, 1]], [key_t[:, both[1]], z11])
+        top0 = jnp.max(s00, axis=1, keepdims=True)
+        top1 = jnp.maximum(
+            jnp.max(s10, axis=1, keepdims=True), jnp.max(s11, axis=1, keepdims=True)
+        )
+        e00, e10, e11 = jnp.exp(s00 - top0), jnp.exp(s10 - top1), jnp.exp(s11 - top1)
+        inv0 = 1.0 / jnp.sum(e00, axis=1, keepdims=True)
+        inv1 = 1.0 / (jnp.sum(e10, axis=1, keepdims=True) + jnp.sum(e11, axis=1, keepdims=True))
+        p00, p10, p11 = (e00 * inv0).astype(BF), (e10 * inv1).astype(BF), (e11 * inv1).astype(BF)
+        mixed0 = dot_nn(p00, value[both[0]])
+        mixed1 = dot_nn(jnp.concatenate([p10, p11], axis=1), value)
+        mixed = jnp.concatenate([mixed0, mixed1], axis=0).astype(BF)
+        results.append((mixed, (p00, p10, p11, z00, z10, z11, tail0, tail1)))
+    return results
 
 
 def forward_kernel(heads, slots, lengths_ref, me_ref, logit_ref, taps_ref, house_ref, q_ref, k_ref, v_ref, mixed_ref, kept_ref):
@@ -181,14 +199,16 @@
     row = lax.broadcasted_iota(jnp.int32, (rows, 1), 0)
     begin = begins(starts_of(lengths_ref, me_ref[0], slots), row)
     place = row - begin
-    for head in range(heads):
-        cols = slice(head * 128, (head + 1) * 128)
-        logit = logit_ref[pl.ds(step * heads + head, 1), :]
-        mixed, kept = forward_head(
-            q_ref[:, cols], k_ref[:, cols], v_ref[:, cols], house_ref[:, cols], logit,
-            taps_ref[:, cols], begin, place,
-        )
-        mixed_ref[:, cols] = mixed
+    columns = [slice(head * 128, (head + 1) * 128) for head in range(heads)]
+    items = [
+        (
+            q_ref[:, cols], k_ref[:, cols], v_ref[:, cols], house_ref[:, cols],
+            logit_ref[pl.ds(step * heads + head, 1), :], taps_ref[:, cols],
+        )
+        for head, cols in enumerate(columns)
+    ]
+    for head, (mixed, kept) in enumerate(forward_heads(items, begin, place)):
+        mixed_ref[:, columns[head]] = mixed
         for slot, item in enumerate(kept):
             kept_ref[head, slot] = item
 
@@ -403,14 +423,16 @@
 
 
 def part_kernel(dealing_ref, me_ref, up_in, down_in, up_out, down_out):
-    up_out[...] = up_in[0]
-    down_out[...] = down_in[0]
+    span = up_in.shape[1]
+    for source, out in ((up_in, up_out), (down_in, down_out)):
+        out[:span] = source[0]
+        out[span:] = jnp.zeros((out.shape[0] - span, out.shape[1]), BF)
 
 
 def slots_to_send(dealing, me, cotangent):
     slots, span, width = cotangent.shape
     tile = 512
-    out = pl.BlockSpec((span, tile), lambda j, dealing, me: (0, j))
+    out = pl.BlockSpec((span + 8, tile), lambda j, dealing, me: (0, j))
 
     def source(by):
         return pl.BlockSpec(
@@ -418,7 +440,7 @@
             lambda j, dealing, me: (slot_taken(dealing, me[0], slots, me[0] + by), 0, j),
         )
 
-    shape = jax.ShapeDtypeStruct((span, width), BF)
+    shape = jax.ShapeDtypeStruct((span + 8, width), BF)
     return pl.pallas_call(
         part_kernel,
         grid_spec=pltpu.PrefetchScalarGridSpec(
@@ -434,9 +456,7 @@
     )(dealing, me, cotangent, cotangent)
 
 
-def arrive_kernel(slots, count, lengths_ref, dealing_ref, me_ref, own_ref, low_ref, high_ref, out_ref, turned_ref, picks):
-    span = low_ref.shape[0]
-
+def arrive_kernel(slots, count, span, lengths_ref, dealing_ref, me_ref, own_ref, low_ref, high_ref, out_ref, picks):
     @pl.when(pl.program_id(0) == 0)
     def _():
         me = me_ref[0]
@@ -450,40 +470,38 @@
         column = lax.broadcasted_iota(jnp.int32, picks.shape, 1)
         picks[...] = jnp.where(column == index, 1.0, 0.0).astype(BF)
 
-    out = (
+    out_ref[...] = (
         dot_nn(picks[:, : slots * span], own_ref[...])
-        + dot_nn(picks[:, slots * span : (slots + 1) * span], low_ref[...])
-        + dot_nn(picks[:, (slots + 1) * span :], high_ref[...])
+        + dot_nn(picks[:, slots * span : (slots + 1) * span], low_ref[:span])
+        + dot_nn(picks[:, (slots + 1) * span :], high_ref[:span])
     ).astype(BF)
-    out_ref[...] = out
-    turned_ref[...] = out.T
 
 
 def cotangent_arrived(lengths, dealing, me, own, low, high, rows):
-    span, width = low.shape
-    slots = own.shape[0] // span
+    slots, span, width = own.shape
+    own = own.reshape(slots * span, width)
     tile = 512
     column = lambda n: pl.BlockSpec((n, tile), lambda j, *s: (0, j))
     return pl.pallas_call(
-        functools.partial(arrive_kernel, slots, dealing.shape[0]),
+        functools.partial(arrive_kernel, slots, dealing.shape[0], span),
         grid_spec=pltpu.PrefetchScalarGridSpec(
             num_scalar_prefetch=3,
             grid=(width // tile,),
-            in_specs=[column(own.shape[0]), column(span), column(span)],
-            out_specs=[column(rows), pl.BlockSpec((tile, rows), lambda j, *s: (j, 0))],
+            in_specs=[column(own.shape[0]), column(low.shape[0]), column(high.shape[0])],
+            out_specs=column(rows),
             scratch_shapes=[pltpu.VMEM((rows, (slots + 2) * span), BF)],
         ),
-        out_shape=[
-            jax.ShapeDtypeStruct((rows, width), BF),
-            jax.ShapeDtypeStruct((width, rows), BF),
-        ],
+        out_shape=jax.ShapeDtypeStruct((rows, width), BF),
         compiler_params=pltpu.CompilerParams(vmem_limit_bytes=VMEM),
         cost_estimate=COST,
         name="cotangent_arrived",
     )(lengths, dealing, me, own, low, high)
 
 
-def deal_kernel(slots, count, span, lengths_ref, dealing_ref, me_ref, hidden_ref, part_ref, other_ref, own_ref, up_ref, down_ref, picks):
+def deal_kernel(
+    slots, count, span, lengths_ref, dealing_ref, me_ref, hidden_ref, upper_ref, lower_ref, other_upper_ref, other_lower_ref,
+    own_ref, up_ref, down_ref, picks,
+):
     @pl.when(pl.program_id(0) == 0)
     def _():
         me = me_ref[0]
@@ -509,14 +527,16 @@
         column = lax.broadcasted_iota(jnp.int32, picks.shape, 1)
         picks[...] = jnp.where(column == index, 1.0, 0.0).astype(BF)
 
-    final = hidden_ref[...] + (part_ref[...].astype(F32) + other_ref[...].astype(F32))
+    share = jnp.concatenate([upper_ref[...], lower_ref[...]], axis=0).astype(F32)
+    other = jnp.concatenate([other_upper_ref[...], other_lower_ref[...]], axis=0).astype(F32)
+    final = hidden_ref[...] + (share + other)
     out = dot_nn(picks[...], final.astype(BF)).astype(BF)
     own_ref[...] = out[: slots * span]
     up_ref[...] = out[slots * span : (slots + 1) * span]
     down_ref[...] = out[(slots + 1) * span :]
 
 
-def rows_dealt(lengths, dealing, me, hidden, part, other, slots, span):
+def rows_dealt(lengths, dealing, me, hidden, shares, slots, span):
     rows, width = hidden.shape
     tile = 512
     column = lambda n: pl.BlockSpec((n, tile), lambda j, *s: (0, j))
@@ -525,7 +545,7 @@
         grid_spec=pltpu.PrefetchScalarGridSpec(
             num_scalar_prefetch=3,
             grid=(width // tile,),
-            in_specs=[column(rows)] * 3,
+            in_specs=[column(rows)] + [column(rows // 2)] * 4,
             out_specs=[column(slots * span), column(span), column(span)],
             scratch_shapes=[pltpu.VMEM(((slots + 2) * span, rows), BF)],
         ),
@@ -537,7 +557,7 @@
         compiler_params=pltpu.CompilerParams(vmem_limit_bytes=VMEM),
         cost_estimate=COST,
         name="rows_dealt",
-    )(lengths, dealing, me, hidden, part, other)
+    )(lengths, dealing, me, hidden, *shares)
 
 
 def norm_kernel(tokens_ref, gain_ref, normed_ref, turned_ref):
@@ -566,32 +586,49 @@
     )(tokens, gain[None, :])
 
 
-def hidden_kernel(tokens_ref, part_ref, other_ref, gain_ref, hidden_ref, normed_ref, turned_ref):
-    hidden = tokens_ref[...].astype(F32) + (part_ref[...].astype(F32) + other_ref[...].astype(F32))
+def shares_of(halves_of, step_count):
+    upper, lower, other_upper, other_lower = halves_of
+    above = pl.program_id(0) < step_count // 2
+    one = jnp.where(above, upper[...], lower[...]).astype(F32)
+    return one + jnp.where(above, other_upper[...], other_lower[...]).astype(F32)
+
+
+def half_specs(rows, tile, width):
+    half = rows // 2 // tile
+    above = pl.BlockSpec((tile, width), lambda i: (jnp.minimum(i, half - 1), 0))
+    below = pl.BlockSpec((tile, width), lambda i: (jnp.maximum(i - half, 0), 0))
+    return [above, below, above, below]
+
+
+def hidden_kernel(steps, tokens_ref, *refs):
+    shares, (gain_ref, hidden_ref, normed_ref) = refs[:4], refs[4:]
+    hidden_body(tokens_ref, shares_of(shares, steps), gain_ref, hidden_ref, normed_ref)
+
+
+def hidden_body(tokens_ref, share, gain_ref, hidden_ref, normed_ref):
+    hidden = tokens_ref[...].astype(F32) + share
     inverse = lax.rsqrt(jnp.mean(hidden * hidden, axis=1, keepdims=True) + EPSILON)
     normed = (hidden * inverse * gain_ref[...]).astype(BF)
     hidden_ref[...] = hidden
     normed_ref[...] = normed
-    turned_ref[...] = normed.T
-
-
-def hidden_and_norm(tokens, part, other, gain, tile=128):
+
+
+def hidden_and_norm(tokens, shares, gain, tile=128):
     rows, width = tokens.shape
     flat = pl.BlockSpec((tile, width), lambda i: (i, 0))
     return pl.pallas_call(
-        hidden_kernel,
+        functools.partial(hidden_kernel, rows // tile),
         grid=(rows // tile,),
-        in_specs=[flat, flat, flat, pl.BlockSpec((1, width), lambda i: (0, 0))],
-        out_specs=[flat, flat, pl.BlockSpec((width, tile), lambda i: (0, i))],
+        in_specs=[flat] + half_specs(rows, tile, width) + [pl.BlockSpec((1, width), lambda i: (0, 0))],
+        out_specs=[flat, flat],
         out_shape=[
             jax.ShapeDtypeStruct((rows, width), F32),
             jax.ShapeDtypeStruct((rows, width), BF),
-            jax.ShapeDtypeStruct((width, rows), BF),
         ],
         compiler_params=pltpu.CompilerParams(vmem_limit_bytes=VMEM),
         cost_estimate=COST,
         name="hidden_and_norm",
-    )(tokens, part, other, gain[None, :])
+    )(tokens, *shares, gain[None, :])
 
 
 def norm_back(d_normed, source, gain):
@@ -614,52 +651,55 @@
 
 
 def branch_kernel(
-    part_ref, other_ref, hidden_ref, d_final_ref, gain_ref, out_ref,
-    d_hidden_ref, turned_ref, d_mixed_ref, d_gain_ref,
+    steps, upper_ref, lower_ref, other_upper_ref, other_lower_ref, hidden_ref, d_final_ref, gain_ref, out_ref,
+    d_hidden_ref, d_branch_ref, d_mixed_ref, d_gain_ref,
 ):
-    back, d_gain = norm_back(part_ref[...].astype(F32) + other_ref[...].astype(F32), hidden_ref[...], gain_ref[...])
+    share = shares_of((upper_ref, lower_ref, other_upper_ref, other_lower_ref), steps)
+    back, d_gain = norm_back(share, hidden_ref[...], gain_ref[...])
     accumulate(d_gain_ref, d_gain)
     d_hidden = d_final_ref[...].astype(F32) + back
     d_hidden_ref[...] = d_hidden
     d_branch = d_hidden.astype(BF)
-    turned_ref[...] = d_branch.T
+    d_branch_ref[...] = d_branch
     d_mixed_ref[...] = dot_nt(d_branch, out_ref[...]).astype(BF)
 
 
-def branch_back(part, other, hidden, d_final, gain, w_out, tile=128):
+def branch_back(shares, hidden, d_final, gain, w_out, tile=128):
     rows, width = hidden.shape
     channels = w_out.shape[0]
     flat = pl.BlockSpec((tile, width), lambda i: (i, 0))
     line = pl.BlockSpec((1, width), lambda i: (0, 0))
     return pl.pallas_call(
-        branch_kernel,
+        functools.partial(branch_kernel, rows // tile),
         grid=(rows // tile,),
-        in_specs=[flat, flat, flat, flat, line, pl.BlockSpec((channels, width), lambda i: (0, 0))],
+        in_specs=half_specs(rows, tile, width)
+        + [flat, flat, line, pl.BlockSpec((channels, width), lambda i: (0, 0))],
         out_specs=[
             flat,
-            pl.BlockSpec((width, tile), lambda i: (0, i)),
+            flat,
             pl.BlockSpec((tile, channels), lambda i: (i, 0)),
             line,
         ],
         out_shape=[
             jax.ShapeDtypeStruct((rows, width), F32),
-            jax.ShapeDtypeStruct((width, rows), BF),
+            jax.ShapeDtypeStruct((rows, width), BF),
             jax.ShapeDtypeStruct((rows, channels), BF),
             jax.ShapeDtypeStruct((1, width), F32),
         ],
         compiler_params=pltpu.CompilerParams(vmem_limit_bytes=VMEM),
         cost_estimate=COST,
         name="branch_back",
-    )(part, other, hidden, d_final, gain[None, :], w_out)
+    )(*shares, hidden, d_final, gain[None, :], w_out)
 
 
 def input_kernel(
-    part_ref, other_ref, tokens_ref, d_hidden_ref, gain_ref, taps_ref, ffn_ref, logit_ref, out_ref, small_ref
+    steps, upper_ref, lower_ref, other_upper_ref, other_lower_ref, tokens_ref, d_hidden_ref, gain_ref, taps_ref, ffn_ref, logit_ref, out_ref, small_ref
 ):
     tokens = tokens_ref[...].astype(F32)
     gain = gain_ref[...]
     taps, heads = taps_ref.shape[0], logit_ref.shape[0]
-    back, d_gain = norm_back(part_ref[...].astype(F32) + other_ref[...].astype(F32), tokens, gain)
+    share = shares_of((upper_ref, lower_ref, other_upper_ref, other_lower_ref), steps)
+    back, d_gain = norm_back(share, tokens, gain)
     out_ref[...] = (d_hidden_ref[...] + back).astype(BF)
     inverse = lax.rsqrt(jnp.mean(tokens * tokens, axis=1, keepdims=True) + EPSILON)
     d_beta = dot_nn(logit_ref[...].astype(BF), (tokens * inverse * gain).astype(BF))
@@ -674,15 +714,16 @@
     small_ref[taps + 2 : taps + 2 + heads, :] += d_beta
 
 
-def input_back(part, other, tokens, d_hidden, gain, g_taps, g_ffn_gain, d_logit, tile=128):
+def input_back(shares, tokens, d_hidden, gain, g_taps, g_ffn_gain, d_logit, tile=128):
     rows, width = tokens.shape
     flat = pl.BlockSpec((tile, width), lambda i: (i, 0))
     line = pl.BlockSpec((1, width), lambda i: (0, 0))
     height = -(-(g_taps.shape[0] + 2 + d_logit.shape[0]) // 8) * 8
     return pl.pallas_call(
-        input_kernel,
+        functools.partial(input_kernel, rows // tile),
         grid=(rows // tile,),
-        in_specs=[flat, flat, flat, flat, line]
+        in_specs=half_specs(rows, tile, width)
+        + [flat, flat, line]
         + [
             pl.BlockSpec(g_taps.shape, lambda i: (0, 0)),
             line,
@@ -696,11 +737,12 @@
         compiler_params=pltpu.CompilerParams(vmem_limit_bytes=VMEM),
         cost_estimate=COST,
         name="input_back",
-    )(part, other, tokens, d_hidden, gain[None, :], g_taps, g_ffn_gain, d_logit)
+    )(*shares, tokens, d_hidden, gain[None, :], g_taps, g_ffn_gain, d_logit)
 
 
 def product_kernel(count, turned, small, *refs):
-    lefts, weights, out_ref = refs[:count], refs[count : 2 * count], refs[-1]
+    lefts, weights = refs[:count], refs[count : 2 * count]
+    upper_ref, lower_ref = refs[-2:]
     dot = dot_nt if turned else dot_nn
     out = dot(lefts[0][...], weights[0][...])
     for left, weight in zip(lefts[1:], weights[1:]):
@@ -710,10 +752,12 @@
             refs[2 * count][...].astype(BF), refs[2 * count + 1][...], (((0,), (1,)), ((), ())),
             preferred_element_type=F32,
         )
-    out_ref[...] = out.astype(out_ref.dtype)
-
-
-def product(lefts, weights, turned, dtype=F32, small=(), tile=512):
+    half = out.shape[0] // 2
+    upper_ref[...] = out[:half].astype(BF)
+    lower_ref[...] = out[half:].astype(BF)
+
+
+def product(lefts, weights, turned, small=(), tile=512):
     width = weights[0].shape[0 if turned else 1]
     whole = lambda x: pl.BlockSpec(x.shape, lambda j: (0, 0))
     left_specs, arrays = [], []
@@ -738,62 +782,53 @@
         functools.partial(product_kernel, len(lefts), turned, bool(small)),
         grid=(width // tile,),
         in_specs=left_specs + parts + more,
-        out_specs=pl.BlockSpec((rows, tile), lambda j: (0, j)),
-        out_shape=jax.ShapeDtypeStruct((rows, width), dtype),
+        out_specs=[pl.BlockSpec((rows // 2, tile), lambda j: (0, j))] * 2,
+        out_shape=[jax.ShapeDtypeStruct((rows // 2, width), BF)] * 2,
         compiler_params=pltpu.CompilerParams(vmem_limit_bytes=VMEM),
         cost_estimate=COST,
         name="product",
     )(*arrays, *weights, *small)
 
 
-def fold_kernel(plan, cuts, *refs):
-    count = 1 if cuts is None else sum(cuts)
+def fold_kernel(plan, *refs):
+    count = 1 + max(out for out, _, _, _ in plan)
     ins, outs = refs[:-count], refs[-count:]
-    start, first = 0, 0
-    for index, (width, terms) in enumerate(plan):
+    for out, start, width, terms in plan:
         part = None
         for ref, column in terms:
             term = ins[ref][:, column : column + width].astype(F32)
             part = term if part is None else part + term
-        if cuts is None:
-            outs[0][:, start : start + width] = part.astype(outs[0].dtype)
-            start += width
-        else:
-            piece = width // cuts[index]
-            for i in range(cuts[index]):
-                outs[first + i][...] = part[:, i * piece : (i + 1) * piece]
-            first += cuts[index]
-
-
-def fold(streams, height, cuts=None):
+        outs[out][:, start : start + width] = part.astype(outs[out].dtype)
+
+
+def fold(outs, height, dtype):
     step = height
     while step % 2 == 0 and step > 96 and (step // 2) % 8 == 0:
         step //= 2
-    arrays, plan = [], []
-    for width, terms in streams:
-        places = []
-        for array, row, column in terms:
-            known = [i for i, (a, r) in enumerate(arrays) if a is array and r == row]
-            if not known:
-                arrays.append((array, row))
-            places.append((known[0] if known else len(arrays) - 1, column))
-        plan.append((width, places))
-    if cuts is None:
-        widths, kind = [sum(width for width, _ in streams)], BF
-    else:
-        widths = [w // n for (w, _), n in zip(streams, cuts) for _ in range(n)]
-        kind = F32
-    return pl.pallas_call(
-        functools.partial(fold_kernel, plan, cuts),
+    arrays, plan, widths = [], [], []
+    for out, streams in enumerate(outs):
+        start = 0
+        for width, terms in streams:
+            places = []
+            for array, row, column in terms:
+                known = [i for i, (a, r) in enumerate(arrays) if a is array and r == row]
+                if not known:
+                    arrays.append((array, row))
+                places.append((known[0] if known else len(arrays) - 1, column))
+            plan.append((out, start, width, places))
+            start += width
+        widths.append(start)
+    return pl.pallas_call(
+        functools.partial(fold_kernel, plan),
         grid=(height // step,),
         in_specs=[
             pl.BlockSpec((step, array.shape[1]), lambda i, r=row // step: (r + i, 0))
             for array, row in arrays
         ],
         out_specs=[pl.BlockSpec((step, width), lambda i: (i, 0)) for width in widths],
-        out_shape=[jax.ShapeDtypeStruct((height, width), kind) for width in widths],
-        compiler_params=pltpu.CompilerParams(vmem_limit_bytes=VMEM),
-        cost_estimate=COST,
+        out_shape=[jax.ShapeDtypeStruct((height, width), dtype) for width in widths],
+        compiler_params=pltpu.CompilerParams(vmem_limit_bytes=VMEM),
+        cost_estimate=MORE,
         name="fold",
     )(*[array for array, _ in arrays])
 
@@ -812,18 +847,24 @@
     )(a, b)
 
 
+def pack(left, order_ref, turned, packed, first=0):
+    size, block, _ = turned.shape
+    around = left.T
+    for i in range(size):
+        turned[i] = around[i * block : (i + 1) * block]
+    for i in range(packed.shape[0] // block):
+        packed[i * block : (i + 1) * block, :] = turned[order_ref[first + i]]
+
+
 def wgrad_kernel(plan, order_ref, *refs):
-    lefts, rights = refs[: len(refs) - 2 - len(plan)], refs[len(refs) - 2 - len(plan) : -2]
-    out_ref, packed = refs[-2:]
-    block = lefts[0].shape[1]
-    count = packed.shape[1] // block
+    lefts, rights = refs[: len(refs) - 3 - len(plan)], refs[len(refs) - 3 - len(plan) : -3]
+    out_ref, turned, packed = refs[-3:]
     step = pl.program_id(0)
 
     @pl.when(step == 0)
     def _():
         for part, left_ref in enumerate(lefts):
-            for i in range(count):
-                packed[part, i * block : (i + 1) * block, :] = left_ref[order_ref[i]]
+            pack(left_ref[...], order_ref, turned, packed.at[part])
 
     for (part, first, steps), right_ref in zip(plan, rights):
 
@@ -832,11 +873,12 @@
             out_ref[...] = dot_nn(packed[part], right_ref[...]).astype(out_ref.dtype)
 
 
-def wgrad(order, parts, tile=512):
+def wgrad(order, size, parts, tile=512):
     count = order.shape[0]
     lefts = [left for left, _ in parts]
     rights = [right for _, several in parts for right in several]
-    block, tokens = lefts[0].shape[1:]
+    tokens, width = lefts[0].shape
+    block = width // size
     tile = next(t for t in (tile, 384, 256, 128) if all(r.shape[1] % t == 0 for r in rights))
     plan, first = [], 0
     for part, (_, several) in enumerate(parts):
@@ -848,7 +890,7 @@
         grid_spec=pltpu.PrefetchScalarGridSpec(
             num_scalar_prefetch=1,
             grid=(first,),
-            in_specs=[pl.BlockSpec(left.shape, lambda j, order: (0, 0, 0)) for left in lefts]
+            in_specs=[pl.BlockSpec(left.shape, lambda j, order: (0, 0)) for left in lefts]
             + [
                 pl.BlockSpec(
                     (tokens, tile), lambda j, order, s=s, n=n: (0, jnp.clip(j - s, 0, n - 1))
@@ -856,7 +898,10 @@
                 for _, s, n in plan
             ],
             out_specs=pl.BlockSpec((count * block, tile), lambda j, order: (0, j)),
-            scratch_shapes=[pltpu.VMEM((len(lefts), count * block, tokens), BF)],
+            scratch_shapes=[
+                pltpu.VMEM((size, block, tokens), BF),
+                pltpu.VMEM((len(lefts), count * block, tokens), BF),
+            ],
         ),
         out_shape=jax.ShapeDtypeStruct((count * block, first * tile), BF),
         compiler_params=pltpu.CompilerParams(vmem_limit_bytes=VMEM),
@@ -894,34 +939,60 @@
     )(order, left, right)
 
 
-def ffn_kernel(normed_ref, d_final_ref, gate_ref, up_ref, down_ref, inner_ref, d_gate_ref, d_up_ref):
+def ffn_kernel(
+    order_ref, normed_ref, d_final_ref, gate_ref, up_ref, down_ref,
+    inner_ref, d_gate_ref, d_up_ref, g_gate_ref, g_up_ref, turned, packed,
+):
+
+    @pl.when(pl.program_id(0) == 0)
+    def _():
+        pack(normed_ref[...], order_ref, turned, packed)
+
     gate = dot_nn(normed_ref[...], gate_ref[...])
     lift = dot_nn(normed_ref[...], up_ref[...])
     d_inner = dot_nt(d_final_ref[...], down_ref[...])
     sig = jax.nn.sigmoid(gate)
     silu = gate * sig
     inner_ref[...] = (silu * lift).astype(BF)
-    d_gate_ref[...] = (d_inner * lift * sig * (1.0 + gate * (1.0 - sig))).astype(BF)
-    d_up_ref[...] = (d_inner * silu).astype(BF)
-
-
-def ffn(normed, d_final, w_gate, w_up, w_down, tile=256):
+    d_gate = (d_inner * lift * sig * (1.0 + gate * (1.0 - sig))).astype(BF)
+    d_up = (d_inner * silu).astype(BF)
+    d_gate_ref[...] = d_gate
+    d_up_ref[...] = d_up
+    g_gate_ref[...] = dot_nn(packed[...], d_gate).astype(BF)
+    g_up_ref[...] = dot_nn(packed[...], d_up).astype(BF)
+
+
+def ffn(order, size, normed, d_final, w_gate, w_up, w_down, tile=512):
     rows, width = normed.shape
-    hidden = w_gate.shape[1]
-    whole = pl.BlockSpec((rows, width), lambda j: (0, 0))
-    column = pl.BlockSpec((width, tile), lambda j: (0, j))
-    out = pl.BlockSpec((rows, tile), lambda j: (0, j))
-    shape = jax.ShapeDtypeStruct((rows, hidden), BF)
+    units = w_gate.shape[1]
+    whole = pl.BlockSpec((rows, width), lambda j, order: (0, 0))
+    column = pl.BlockSpec((width, tile), lambda j, order: (0, j))
+    out = pl.BlockSpec((rows, tile), lambda j, order: (0, j))
+    shape = jax.ShapeDtypeStruct((rows, units), BF)
+    grad = jax.ShapeDtypeStruct((width, units), BF)
     return pl.pallas_call(
         ffn_kernel,
-        grid=(hidden // tile,),
-        in_specs=[whole, whole, column, column, pl.BlockSpec((tile, width), lambda j: (j, 0))],
-        out_specs=[out, out, out],
-        out_shape=[shape, shape, shape],
+        grid_spec=pltpu.PrefetchScalarGridSpec(
+            num_scalar_prefetch=1,
+            grid=(units // tile,),
+            in_specs=[
+                whole,
+                whole,
+                column,
+                column,
+                pl.BlockSpec((tile, width), lambda j, order: (j, 0)),
+            ],
+            out_specs=[out, out, out, column, column],
+            scratch_shapes=[
+                pltpu.VMEM((size, width // size, rows), BF),
+                pltpu.VMEM((width, rows), BF),
+            ],
+        ),
+        out_shape=[shape, shape, shape, grad, grad],
         compiler_params=pltpu.CompilerParams(vmem_limit_bytes=VMEM),
         cost_estimate=COST,
         name="ffn",
-    )(normed, d_final, w_gate, w_up, w_down)
+    )(order, normed, d_final, w_gate, w_up, w_down)
 
 
 def swap(x, axis, bit):
@@ -1016,9 +1087,6 @@
     order_xyz = me ^ flips_of(size, bits)
     order = Order()
 
-    def sharded(turned):
-        return turned.reshape(size, block, turned.shape[1])
-
     cot_up, cot_down = order.mark(*slots_to_send(dealing, me1, cotangent))
     cot_low = lax.ppermute(cot_up, "dp", up)
     cot_high = lax.ppermute(cot_down, "dp", down)
@@ -1037,67 +1105,73 @@
     mixed, kept = order.mark(
         *mixer_forward(lengths, me1, logit, conv_taps, house, order.gate(query), key, value)
     )
-    cot_low, cot_high = order.mark(*order.gate(cot_low, cot_high))
-    attn_part = order.mark(product([order.gate(mixed)], [w_out], False, BF))
-    attn_other = swap(attn_part, "tensor", 0)
-    cot_low = order.gate(cot_low)
-    d_final, d_final_t = order.mark(
-        *cotangent_arrived(lengths, dealing, me1, cotangent.reshape(-1, width), cot_low, cot_high, rows)
-    )
-    hidden, normed2, normed2_t = order.mark(
-        *hidden_and_norm(tokens, attn_part, order.gate(attn_other), ffn_gain)
-    )
-    inner, d_gate, d_up = order.mark(*ffn(order.gate(normed2), d_final, w_gate, w_up, w_down))
-
-    def gated(streams):
+
+    def shares(parts):
+        others = [swap(part, "tensor", 0) for part in parts]
+        return lambda: [*parts, *order.gate(*others)]
+
+    attn_shares = shares(order.mark(*product([order.gate(mixed)], [w_out], False)))
+    hidden, normed2 = order.mark(*hidden_and_norm(tokens, attn_shares(), ffn_gain))
+    d_final = order.mark(
+        cotangent_arrived(
+            lengths, dealing, me1, cotangent, *order.gate(cot_low, cot_high), rows
+        )
+    )
+
+    def gated(outs):
         arrays = []
-        for _, terms in streams:
-            for array, _, _ in terms:
-                if not any(array is known for known in arrays):
-                    arrays.append(array)
+        for streams in outs:
+            for _, terms in streams:
+                for array, _, _ in terms:
+                    if not any(array is known for known in arrays):
+                        arrays.append(array)
         after = order.gate(*arrays)
         after = list(after) if isinstance(after, tuple) else [after]
+        new = lambda array: next(n for a, n in zip(arrays, after) if a is array)
         return [
-            (w, [(next(n for a, n in zip(arrays, after) if a is array), r, c) for array, r, c in terms])
-            for w, terms in streams
+            [(w, [(new(array), r, c) for array, r, c in terms]) for w, terms in streams]
+            for streams in outs
         ]
 
     def leave(streams, height, bit):
-        streams = gated(streams)
-        got = swap(order.mark(fold(streams, height)[0]), "dp", bit)
+        (streams,) = gated([streams])
+        got = swap(order.mark(fold([streams], height, BF)[0]), "dp", bit)
         return joined([(w, [(a, r + height, c) for a, r, c in terms]) for w, terms in streams], got)
 
-    def finish(streams, cuts):
-        out = fold(gated(streams), block, cuts)
+    def finish(outs):
+        out = fold(gated(outs), block, F32)
         order.mark(out[0])
         return out
 
-    def wgrad_of(rows_order, *parts):
-        left, rights = parts[0]
-        parts = [(left, [order.gate(rights[0])] + list(rights[1:]))] + list(parts[1:])
-        return order.mark(wgrad(rows_order, parts))
-
-    quarter = width // 4
+    def wgrad_of(rows_order, left, rights):
+        return order.mark(
+            wgrad(rows_order, size, [(left, [order.gate(rights[0])] + list(rights[1:]))])
+        )
+
+    half, quarter = width // 2, width // 4
     columns = query.shape[1]
     heights = [quarter >> (i + 1) for i in range(len(line))]
-    d_final_s = sharded(d_final_t)
-
-    ffn_all = wgrad_of(order_plane, (sharded(normed2_t), [d_gate, d_up]))
-    ffn_sum = lax.psum_scatter(
-        ffn_all, "dp", scatter_dimension=0, tiled=True, axis_index_groups=groups
-    )
-    down_leave = wgrad_of(order_zxy[:first], (d_final_s, [inner]))
+    lines = size // 4
+
+    def plane_sum(x):
+        return lax.psum_scatter(
+            x, "dp", scatter_dimension=0, tiled=True, axis_index_groups=groups
+        )
+
+    inner, d_gate, d_up, gate_all, up_all = order.mark(
+        *ffn(order_plane, size, order.gate(normed2), d_final, w_gate, w_up, w_down)
+    )
+    gate_sum, up_sum = plane_sum(gate_all), plane_sum(up_all)
+    down_leave = wgrad_of(order_zxy[:first], d_final, [inner])
     down_got = swap(down_leave, "dp", line[0])
-    d_norm2_part = order.mark(product([order.gate(d_gate), d_up], [w_gate, w_up], True, BF))
-    d_norm2_other = swap(d_norm2_part, "tensor", 0)
-    down_stay = wgrad_of(order_zxy[first:], (d_final_s, [inner]))
+    d_norm2_shares = shares(order.mark(*product([order.gate(d_gate), d_up], [w_gate, w_up], True)))
+    down_stay = wgrad_of(order_zxy[first:], d_final, [inner])
     downs = [stream(down_stay, down_got)]
-    d_hidden, d_branch_t, d_mixed, g_ffn_gain = order.mark(
-        *branch_back(d_norm2_part, order.gate(d_norm2_other), hidden, d_final, ffn_gain, w_out)
-    )
-    branch = sharded(d_branch_t)
-
-    out_leave = wgrad_of(order_xyz[:first], (branch, [mixed]))
+    plane_normed = order.mark(order.gate(plane_normed))
+    d_hidden, d_branch, d_mixed, g_ffn_gain = order.mark(
+        *branch_back(d_norm2_shares(), hidden, d_final, ffn_gain, w_out)
+    )
+    out_leave = wgrad_of(order_xyz[:first], d_branch, [mixed])
     out_got = swap(out_leave, "dp", 0)
 
     d_four, d_logit, g_taps = order.mark(
@@ -1106,30 +1180,35 @@
         )
     )
     plane_four = lax.all_to_all(d_four, "dp", 0, 0, axis_index_groups=groups)
-    out_stay = wgrad_of(order_xyz[first:], (branch, [mixed]))
-    height = width // 2
+    out_stay = wgrad_of(order_xyz[first:], d_branch, [mixed])
+    height = half
     for bit in line[1:]:
         height //= 2
         downs = leave(downs, height, bit)
-    down_part = order.mark(product([order.gate(inner)], [w_down], False, BF))
-    down_other = swap(down_part, "tensor", 0)
-    outs = leave([stream(out_stay, out_got)], quarter, 1)
-    d_norm1_part = order.mark(
-        product(
-            [(order.gate(d_four), i) for i in range(4)],
-            [w_query, w_key, w_value, w_house], True, BF, small=(d_logit, w_beta),
-        )
-    )
-    d_norm1_other = swap(d_norm1_part, "tensor", 0)
-    dealt, deal_up, deal_down = order.mark(
-        *rows_dealt(lengths, dealing, me1, hidden, *order.gate(down_part, down_other), slots, span)
-    )
+    d_norm1_shares = shares(
+        order.mark(
+            *product(
+                [(order.gate(d_four), i) for i in range(4)],
+                [w_query, w_key, w_value, w_house], True, small=(d_logit, w_beta),
+            )
+        )
+    )
+    down_shares = shares(order.mark(*product([order.gate(inner)], [w_down], False)))
+    gates = leave([stream(gate_sum)], heights[0], line[0])
     input_grad, small = order.mark(
         *input_back(
-            d_norm1_part, order.gate(d_norm1_other), tokens, d_hidden, attn_gain, g_taps, g_ffn_gain, d_logit
-        )
-    )
-    lines = size // 4
+            d_norm1_shares(), tokens, d_hidden, attn_gain, g_taps, g_ffn_gain, d_logit
+        )
+    )
+    small_bits, small_got = list(bits), None
+
+    def small_step():
+        nonlocal small, small_got
+        if small_got is not None:
+            small = order.mark(added(small, order.gate(small_got)))
+        small_got = swap(small, "dp", small_bits.pop(0)) if small_bits else None
+
+    small_step()
     attn_leave = order.mark(
         wgrad_plane(order_line[: lines // 2], plane_normed, order.gate(plane_four), lines)
     )
@@ -1137,41 +1216,38 @@
     attn_stay = order.mark(
         wgrad_plane(order_line[lines // 2 :], plane_normed, order.gate(plane_four), lines)
     )
-    ffns = leave([stream(ffn_sum)] + outs, heights[0], line[0])
+    attns = [stream(attn_stay, attn_got)]
+    for low, bit in zip(heights[1:], line[1:]):
+        gates = leave(gates, low, bit)
+    outs = leave([stream(out_stay, out_got)], quarter, 1)
+    dealt, deal_up, deal_down = order.mark(
+        *rows_dealt(lengths, dealing, me1, hidden, down_shares(), slots, span)
+    )
+    small_step()
     height //= 2
     downs = leave(downs, height, 0)
-    out_low = lax.ppermute(deal_up, "dp", up)
-    out_high = lax.ppermute(deal_down, "dp", down)
-    attns = [stream(attn_stay, attn_got)]
-    attn_height = width // 2
+    attn_height = half
     for bit in line[1:]:
         attn_height //= 2
         attns = leave(attns, attn_height, bit)
+    (g_gate,) = finish([gates])
+    small_step()
+    ups = leave([stream(up_sum)] + outs, heights[0], line[0])
+    out_low = lax.ppermute(deal_up, "dp", up)
+    out_high = lax.ppermute(deal_down, "dp", down)
     height //= 2
     downs = leave(downs, height, 1)
-    for height, bit in zip(heights[1:], line[1:]):
-        ffns = leave(ffns, height, bit)
-    small_got = None
-
-    def small_step(bit):
-        nonlocal small, small_got
-        if small_got is not None:
-            small = order.mark(added(small, order.gate(small_got)))
-        small_got = None if bit is None else swap(small, "dp", bit)
-
-    small_bits = list(bits)
-    small_step(small_bits.pop(0))
-    attn_sum = order.mark(fold(gated(attns), width // lines)[0])
+    attn_sum = order.mark(fold(gated([attns]), width // lines, BF)[0])
     plane_rows = lax.all_to_all(
         attn_sum.reshape(4, block, columns), "dp", 0, 0, axis_index_groups=groups
     )
+    for low, bit in zip(heights[1:], line[1:]):
+        ups = leave(ups, low, bit)
+    (g_down,) = finish([downs])
     out_low, out_high = order.mark(*order.gate(out_low, out_high))
-    small_step(small_bits.pop(0))
-    (g_down,) = finish(downs, [1])
-    while small_bits:
-        small_step(small_bits.pop(0))
-    small_step(None)
-    g_gate, g_up, g_out = finish(ffns, [2, 1])
+    while small_got is not None:
+        small_step()
+    g_up, g_out = finish([[up_one] for up_one in ups])
     g_query, g_key, g_value, g_house = order.gate(plane_rows).astype(F32)
 
     taps = conv_taps.shape[0]

time: 482 us -> 429 us (0.89)
  waiting for transfers between devices: 146 us -> 92.8 us
  Pallas kernels: 232 us -> 219 us
  starting transfers between devices: 46.5 us -> 58.1 us
    ppermute x18 -> x24, waiting for transfers between devices: 110 us -> 73.6 us  [swap(): return lax.ppermute(x, axis, [(i, i ^ 1 << bit) for i in range(size)])]
    all_to_all x1, waiting for transfers between devices: 24.2 us -> 0.01 us  [on_device(): plane_four = lax.all_to_all(d_four, 'dp', 0, 0, axis_index_groups=groups)]
    ppermute x18 -> x24, starting transfers between devices: 26.8 us -> 40.8 us  [swap(): return lax.ppermute(x, axis, [(i, i ^ 1 << bit) for i in range(size)])]
    pallas_call x15 -> x18, Pallas kernels: 75.8 us -> 87.6 us  [the longest x13 34.8 us: fold(): pl.pallas_call(functools.partial(fold_kernel, plan), grid=(height // step...]
    pallas_call x1, Pallas kernels: 29.4 us -> 17.8 us  [mixer_forward(): pl.pallas_call(functools.partial(forward_kernel, heads, lengths.shape[1])...]
    pallas_call x5 -> x4, Pallas kernels: 34.9 us -> 23.5 us  [wgrad(): pl.pallas_call(functools.partial(wgrad_kernel, plan), grid_spec=pltpu.Pre...]
    reduce_scatter x1 -> x2, waiting for transfers between devices: 4.07 us -> 11.4 us  [plane_sum(): lax.psum_scatter(x, 'dp', scatter_dimension=0, tiled=True, axis_index_gro...]
    unnamed x58 -> x66, local copies, waits for them, and re-layouts: 10.6 us -> 14.2 us
  transfers between devices with their start and end apart: 26 -> 33, of which waited for: 11 -> 13; matrix products, arithmetic and copies ran while one was open for 5% -> 6% of each run, Pallas kernels for 47% -> 50%
where the time goes in v3:
time: 429 us; the launch traced here: 423 us
  Pallas kernels  219 us (51%)
  waiting for transfers between devices  92.8 us (22%)
  starting transfers between devices  58.1 us (14%)
  local copies, waits for them, and re-layouts  23 us (5%)
  between operations  14.5 us (3%)
  matrix products  12 us (3%)
    ppermute x24, waiting for transfers between devices, swap(): return lax.ppermute(x, axis, [(i, i ^ 1 << bit) for i in range(size)])  73.6 us
    ppermute x24, starting transfers between devices, swap(): return lax.ppermute(x, axis, [(i, i ^ 1 << bit) for i in range(size)])  40.8 us
    pallas_call x13, Pallas kernels, fold(): pl.pallas_call(functools.partial(fold_kernel, plan), grid=(height // step...  34.8 us
    pallas_call x4, Pallas kernels, product(): pl.pallas_call(functools.partial(product_kernel, len(lefts), turned, bool...  33.2 us
    pallas_call x1, Pallas kernels, ffn(): pl.pallas_call(ffn_kernel, grid_spec=pltpu.PrefetchScalarGridSpec(num_sca...  24.6 us
    pallas_call x4, Pallas kernels, wgrad(): pl.pallas_call(functools.partial(wgrad_kernel, plan), grid_spec=pltpu.Pre...  23.5 us
    pallas_call x1, Pallas kernels, mixer_backward(): pl.pallas_call(functools.partial(backward_kernel, heads, lengths.shape[1]...  21 us
    pallas_call x1, Pallas kernels, mixer_forward(): pl.pallas_call(functools.partial(forward_kernel, heads, lengths.shape[1])...  17.8 us
  transfers between devices with their start and end apart: 33, of which 13 were waited for; matrix products, arithmetic and copies ran while one was open for 6% of the time, Pallas kernels for 50%

profile of v3, /device:TPU:0, one launch (start us, length us, event | category | flops | bytes accessed | tf_op | source)
XLA Modules:
  0.0 423.3 jit_solution(15230549865582344046)
XLA Ops:
  8.5 4.1 slots_to_send.1
  12.6 4.4 %first_norm.1 = (bf16[512,1536]{1,0:T(8,128)(2,1)}, bf16[1536,512]{1,0:T(8,128)(2,1)}) custom-call(bf16[512,1536]{1,0:T(8,128)(2,1)} %tokens_ref.4, f32[1,1536]{1,0:T(1,128)} %broadcast_in_dim.41.gain_ref), custom_call_target="tpu_custom_call" | custom-call | tf_op jit(solution)/shard_map/first_norm/pallas_call | solution.py:574
  17.1 4.9 %collective-permute-start.2 = (bf16[264,1536]{1,0:T(8,128)(2,1)}, bf16[264,1536]{1,0:T(8,128)(2,1)S(1)}, u32[]{:S(2)}, u32[]{:S(2)}) collective-permute-start(bf16[264,1536]{1,0:T(8,128)(2,1)} %get-tuple-element.124), channel_id=1, source_target_pairs={{0,2},{2,4},{4,6},{6,8},{8,10},{10,12},{12,14},{14,16},{16,18},{18... | collective-permute-start | bytes 2433032 | tf_op jit(solution)/shard_map/ppermute | solution.py:1091
  23.3 3.8 convolution_convert_fusion.v_ref
  27.1 2.3 convolution_convert_fusion.1.k_ref
  29.4 2.3 convolution_convert_fusion.2.q_ref
  31.7 2.5 fusion.5.house_ref
  36.0 17.8 %mixer_forward.1 = (bf16[512,768]{1,0:T(8,128)(2,1)}, bf16[6,8,256,256]{3,2,1,0:T(8,128)(2,1)}) custom-call(s32[16,3]{1,0:T(8,128)} %copy.37.lengths_ref, s32[1]{0:T(128)} %bitcast.me_ref, f32[6,512]{1,0:T(8,128)} %convolution_bitcast_fusion.logit_ref, f32[4,768]{1,0:T(4,128)} %taps_ref.3, f32[512,768]{1,0:T(8,128)} %fusion.5.house_ref, ...), custom_call_target="tpu_custom_call" | custom-call | tf_op jit(solution)/shard_map/mixer_forward/pallas_call | solution.py:221
  53.8 4.6 %product.4 = (bf16[256,1536]{1,0:T(8,128)(2,1)}, bf16[256,1536]{1,0:T(8,128)(2,1)}) custom-call(bf16[512,768]{1,0:T(8,128)(2,1)} %get-tuple-element.164.refs_0_.refs_1_, bf16[768,1536]{1,0:T(8,128)(2,1)} %out_ref.1), custom_call_target="tpu_custom_call" | custom-call | tf_op jit(solution)/shard_map/product/pallas_call | solution.py:781
  63.0 5.6 %hidden_and_norm.1 = (f32[512,1536]{1,0:T(8,128)}, bf16[512,1536]{1,0:T(8,128)(2,1)}) custom-call(bf16[512,1536]{1,0:T(8,128)(2,1)} %tokens_ref.4, bf16[256,1536]{1,0:T(8,128)(2,1)} %get-tuple-element.132.refs_0_, bf16[256,1536]{1,0:T(8,128)(2,1)} %get-tuple-element.133.refs_1_, bf16[256,1536]{1,0:T(8,128)(2,1)} %copy-done.13, bf16[256,1536]{1,0:T(8,128)(2,1)} %copy-done.14, ...), custom_call_target="tpu_custom_call" | custom-call | tf_op jit(solution)/shard_map/hidden_and_norm/pallas_call | solution.py:619
  68.6 1.7 collective-permute-done.2.low_ref
  70.3 5.4 %collective-permute-done.3.high_ref = bf16[264,1536]{1,0:T(8,128)(2,1)} collective-permute-done((bf16[264,1536]{1,0:T(8,128)(2,1)}, bf16[264,1536]{1,0:T(8,128)(2,1)}, u32[]{:S(2)}, u32[]{:S(2)}) %collective-permute-start.3) | collective-permute-done | bytes 811040 | tf_op jit(solution)/shard_map/ppermute | solution.py:1092
  75.7 6.5 %cotangent_arrived.1.d_final_ref.refs_0_ = bf16[512,1536]{1,0:T(8,128)(2,1)} custom-call(s32[16,3]{1,0:T(8,128)} %copy.37.lengths_ref, s32[48]{0:T(128)} %dealing_ref.5, s32[1]{0:T(128)} %bitcast.me_ref, bf16[768,1536]{1,0:T(8,128)(2,1)} %bitcast.35, bf16[264,1536]{1,0:T(8,128)(2,1)} %copy-done.11, bf16[264,1536]{1,0:T(8,128)(2,1)} %collective-permute-done.3.high_ref), custom_call_target="tpu_custom_call" | custom-call | tf_op jit(solution)/shard_map/cotangent_arrived/pallas_call | solution.py:485
  82.2 24.6 %ffn.1 = (bf16[512,2048]{1,0:T(8,128)(2,1)}, bf16[512,2048]{1,0:T(8,128)(2,1)}, bf16[512,2048]{1,0:T(8,128)(2,1)}, bf16[1536,2048]{1,0:T(8,128)(2,1)}, bf16[1536,2048]{1,0:T(8,128)(2,1)}) custom-call(s32[16]{0:T(128)} %add.32.order_ref, bf16[512,1536]{1,0:T(8,128)(2,1)} %get-tuple-element.140.normed_ref, ...), custom_call_target="tpu_custom_call" | custom-call | tf_op jit(solution)/shard_map/ffn/pallas_call | solution.py:973
  108.2 7.1 %wgrad.4 = bf16[768,2048]{1,0:T(8,128)(2,1)} custom-call(s32[8]{0:T(128)} %get-tuple-element.248.order_ref, bf16[512,1536]{1,0:T(8,128)(2,1)} %cotangent_arrived.1.d_final_ref.refs_0_, bf16[512,2048]{1,0:T(8,128)(2,1)} %get-tuple-element.170.refs_1_.refs_0_), custom_call_target="tpu_custom_call" | custom-call | tf_op jit(solution)/shard_map/wgrad/pallas_call | solution.py:888
  116.8 11.4 %product.5 = (bf16[256,1536]{1,0:T(8,128)(2,1)}, bf16[256,1536]{1,0:T(8,128)(2,1)}) custom-call(bf16[512,2048]{1,0:T(8,128)(2,1)} %get-tuple-element.147.refs_0_, bf16[512,2048]{1,0:T(8,128)(2,1)} %get-tuple-element.143.refs_1_, bf16[1536,2048]{1,0:T(8,128)(2,1)} %refs_2_.1, bf16[1536,2048]{1,0:T(8,128)(2,1)} %refs_3_.1), custom_call_target="tpu_custom_call" | custom-call | tf_op jit(solution)/shard_map/product/pallas_call | solution.py:781
  129.4 6.9 %wgrad.5.refs_0_ = bf16[768,2048]{1,0:T(8,128)(2,1)} custom-call(s32[8]{0:T(128)} %get-tuple-element.247.order_ref, bf16[512,1536]{1,0:T(8,128)(2,1)} %cotangent_arrived.1.d_final_ref.refs_0_, bf16[512,2048]{1,0:T(8,128)(2,1)} %get-tuple-element.170.refs_1_.refs_0_), custom_call_target="tpu_custom_call" | custom-call | tf_op jit(solution)/shard_map/wgrad/pallas_call | solution.py:888
  136.3 9.0 %branch_back.1 = (f32[512,1536]{1,0:T(8,128)}, bf16[512,1536]{1,0:T(8,128)(2,1)}, bf16[512,768]{1,0:T(8,128)(2,1)}, f32[1,1536]{1,0:T(1,128)}) custom-call(bf16[256,1536]{1,0:T(8,128)(2,1)} %get-tuple-element.148.upper_ref, bf16[256,1536]{1,0:T(8,128)(2,1)} %get-tuple-element.149.lower_ref, bf16[256,1536]{1,0:T(8,128)(2,1)} %collective-permute-done.4.other_upper_ref, ...), custom_call_target="tpu_custom_call" | custom-call | tf_op jit(solution)/shard_map/branch_back/pallas_call | solution.py:672
  145.3 4.8 %wgrad.6 = bf16[768,768]{1,0:T(8,128)(2,1)} custom-call(s32[8]{0:T(128)} %get-tuple-element.246.order_ref, bf16[512,1536]{1,0:T(8,128)(2,1)} %get-tuple-element.156.refs_0_, bf16[512,768]{1,0:T(8,128)(2,1)} %get-tuple-element.164.refs_0_.refs_1_), custom_call_target="tpu_custom_call" | custom-call | tf_op jit(solution)/shard_map/wgrad/pallas_call | solution.py:888
  150.0 21.0 %mixer_backward.1 = (bf16[4,512,768]{2,1,0:T(8,128)(2,1)}, f32[6,512]{1,0:T(8,128)}, f32[4,768]{1,0:T(4,128)}) custom-call(s32[16,3]{1,0:T(8,128)} %copy.37.lengths_ref, s32[1]{0:T(128)} %bitcast.me_ref, f32[6,512]{1,0:T(8,128)} %convolution_bitcast_fusion.logit_ref, f32[4,768]{1,0:T(4,128)} %taps_ref.3, f32[512,768]{1,0:T(8,128)} %fusion.5.house_ref, ...), custom_call_target="tpu_custom_call" | custom-call | tf_op jit(solution)/shard_map/mixer_backward/pallas_call | solution.py:366
  171.0 4.9 %all-to-all-start = ((bf16[4,512,768]{2,1,0:T(8,128)(2,1)}), bf16[4,512,768]{2,1,0:T(8,128)(2,1)}, u32[]{:S(2)}, u32[]{:S(2)}) async-start(bf16[4,512,768]{2,1,0:T(8,128)(2,1)} %get-tuple-element.167.refs_0_.refs_1_.refs_2_.refs_3_), calls=%async_computation.1 | async-start | bytes 6291456 | tf_op jit(solution)/shard_map/all_to_all | solution.py:1182
  176.9 4.8 %wgrad.7.refs_0_.refs_1_.refs_2_.refs_3_ = bf16[768,768]{1,0:T(8,128)(2,1)} custom-call(s32[8]{0:T(128)} %get-tuple-element.245.order_ref, bf16[512,1536]{1,0:T(8,128)(2,1)} %get-tuple-element.156.refs_0_, bf16[512,768]{1,0:T(8,128)(2,1)} %get-tuple-element.164.refs_0_.refs_1_), custom_call_target="tpu_custom_call" | custom-call | tf_op jit(solution)/shard_map/wgrad/pallas_call | solution.py:888
  181.7 3.2 collective-permute-done.6.refs_1_
  184.8 1.6 copy-done
  186.5 4.0 fold.13
  190.5 10.0 %product.6 = (bf16[256,1536]{1,0:T(8,128)(2,1)}, bf16[256,1536]{1,0:T(8,128)(2,1)}) custom-call(bf16[4,512,768]{2,1,0:T(8,128)(2,1)} %get-tuple-element.167.refs_0_.refs_1_.refs_2_.refs_3_, bf16[4,512,768]{2,1,0:T(8,128)(2,1)} %get-tuple-element.167.refs_0_.refs_1_.refs_2_.refs_3_, bf16[4,512,768]{2,1,0:T(8,128)(2,1)} %get-tuple-element.167.refs_0_.refs_1_.refs_2_.refs_3_, ...), custom_call_target="tpu_custom_call" | custom-call | tf_op jit(solution)/shard_map/product/pallas_call | solution.py:781
  201.0 7.2 %product.7 = (bf16[256,1536]{1,0:T(8,128)(2,1)}, bf16[256,1536]{1,0:T(8,128)(2,1)}) custom-call(bf16[512,2048]{1,0:T(8,128)(2,1)} %get-tuple-element.170.refs_1_.refs_0_, bf16[2048,1536]{1,0:T(8,128)(2,1)} %refs_1_.3), custom_call_target="tpu_custom_call" | custom-call | tf_op jit(solution)/shard_map/product/pallas_call | solution.py:781
  208.2 7.9 %reduce-scatter.3.cloned.1.call-done.refs_0_ = bf16[384,2048]{1,0:T(8,128)(2,1)} async-done(((bf16[1536,2048]{1,0:T(8,128)(2,1)}), bf16[384,2048]{1,0:T(8,128)(2,1)}) %reduce-scatter.3.cloned.1.call-update) | async-done | bytes 1572880 | tf_op jit(solution)/shard_map/reduce_scatter | solution.py:1157
  216.0 1.9 fold.14
  217.9 3.2 collective-permute-start.10
  221.2 2.2 collective-permute-start.15
  224.9 7.0 %input_back.1 = (bf16[512,1536]{1,0:T(8,128)(2,1)}, f32[16,1536]{1,0:T(8,128)}) custom-call(bf16[256,1536]{1,0:T(8,128)(2,1)} %get-tuple-element.168.upper_ref, bf16[256,1536]{1,0:T(8,128)(2,1)} %get-tuple-element.169.lower_ref, bf16[256,1536]{1,0:T(8,128)(2,1)} %copy-done.12, bf16[256,1536]{1,0:T(8,128)(2,1)} %collective-permute-done.12.other_lower_ref, ...), custom_call_target="tpu_custom_call" | custom-call | tf_op jit(solution)/shard_map/input_back/pallas_call | solution.py:722
  231.9 6.8 %wgrad_plane.2 = bf16[768,768]{1,0:T(8,128)(2,1)} custom-call(s32[2]{0:T(128)} %get-tuple-element.241.order_ref, bf16[4,1536,512]{2,1,0:T(8,128)(2,1)} %bitcast.33, bf16[4,512,768]{2,1,0:T(8,128)(2,1)} %all-to-all-done.right_ref), custom_call_target="tpu_custom_call" | custom-call | tf_op jit(solution)/shard_map/wgrad_plane/pallas_call | solution.py:924
  238.9 17.2 %collective-permute-done.10.refs_1_ = bf16[192,2048]{1,0:T(8,128)(2,1)} collective-permute-done((bf16[192,2048]{1,0:T(8,128)(2,1)}, bf16[192,2048]{1,0:T(8,128)(2,1)}, u32[]{:S(2)}, u32[]{:S(2)}) %collective-permute-start.10) | collective-permute-done | bytes 786464 | tf_op jit(solution)/shard_map/ppermute | solution.py:1000
  256.1 6.7 %wgrad_plane.3.refs_0_ = bf16[768,768]{1,0:T(8,128)(2,1)} custom-call(s32[2]{0:T(128)} %get-tuple-element.242.order_ref, bf16[4,1536,512]{2,1,0:T(8,128)(2,1)} %bitcast.34, bf16[4,512,768]{2,1,0:T(8,128)(2,1)} %all-to-all-done.right_ref), custom_call_target="tpu_custom_call" | custom-call | tf_op jit(solution)/shard_map/wgrad_plane/pallas_call | solution.py:924
  262.8 2.0 fold.15
  264.8 5.2 %collective-permute-done.9.refs_1_.refs_2_.refs_3_.refs_4_ = bf16[768,768]{1,0:T(8,128)(2,1)S(1)} collective-permute-done((bf16[768,768]{1,0:T(8,128)(2,1)}, bf16[768,768]{1,0:T(8,128)(2,1)S(1)}, u32[]{:S(2)}, u32[]{:S(2)}) %collective-permute-start.9) | collective-permute-done | bytes 1179680 | tf_op jit(solution)/shard_map/ppermute | solution.py:1000
  271.0 3.4 fold.16
  274.7 2.1 collective-permute-start.20
  276.7 7.8 %rows_dealt.1 = (bf16[768,1536]{1,0:T(8,128)(2,1)}, bf16[256,1536]{1,0:T(8,128)(2,1)}, bf16[256,1536]{1,0:T(8,128)(2,1)}) custom-call(s32[16,3]{1,0:T(8,128)} %copy.37.lengths_ref, s32[48]{0:T(128)} %dealing_ref.5, s32[1]{0:T(128)} %bitcast.me_ref, f32[512,1536]{1,0:T(8,128)} %get-tuple-element.136.hidden_ref, ...), custom_call_target="tpu_custom_call" | custom-call | tf_op jit(solution)/shard_map/rows_dealt/pallas_call | solution.py:543
  285.2 1.6 added.4.a_ref
  286.8 1.6 collective-permute-start.19
  288.4 5.0 %collective-permute-done.15.refs_2_ = bf16[384,2048]{1,0:T(8,128)(2,1)S(1)} collective-permute-done((bf16[384,2048]{1,0:T(8,128)(2,1)}, bf16[384,2048]{1,0:T(8,128)(2,1)S(1)}, u32[]{:S(2)}, u32[]{:S(2)}) %collective-permute-start.15) | collective-permute-done | bytes 1572896 | tf_op jit(solution)/shard_map/ppermute | solution.py:1000
  294.6 2.5 fold.17
  297.0 10.4 %collective-permute-start.17 = (bf16[192,2048]{1,0:T(8,128)(2,1)}, bf16[192,2048]{1,0:T(8,128)(2,1)S(1)}, u32[]{:S(2)}, u32[]{:S(2)}) collective-permute-start(bf16[192,2048]{1,0:T(8,128)(2,1)} %fold.17), channel_id=1, source_target_pairs={{0,2},{2,0},{4,6},{6,4},{8,10},{10,8},{12,14},{14,12},{16,18},{18,... | collective-permute-start | bytes 2359304 | tf_op jit(solution)/shard_map/ppermute | solution.py:1000
  307.4 3.4 fold.18
  311.6 2.2 fold.19
  316.1 3.5 reduce-scatter.5.cloned.1.call-done.refs_0_
  320.4 2.3 fold.20
  322.7 3.9 collective-permute-start.23
  326.6 1.7 collective-permute-start.24
  331.9 2.3 fold.21
  334.2 6.2 %collective-permute-start.22 = (bf16[96,2048]{1,0:T(8,128)(2,1)}, bf16[96,2048]{1,0:T(8,128)(2,1)}, u32[]{:S(2)}, u32[]{:S(2)}) collective-permute-start(bf16[96,2048]{1,0:T(8,128)(2,1)} %fold.21), channel_id=1, source_target_pairs={{0,4},{2,6},{4,0},{6,2},{8,12},{10,14},{12,8},{14,10},{16,20},{18,... | collective-permute-start | bytes 1179656 | tf_op jit(solution)/shard_map/ppermute | solution.py:1000
  340.4 21.8 %collective-permute-done.24.refs_2_ = bf16[384,768]{1,0:T(8,128)(2,1)} collective-permute-done((bf16[384,768]{1,0:T(8,128)(2,1)}, bf16[384,768]{1,0:T(8,128)(2,1)}, u32[]{:S(2)}, u32[]{:S(2)}) %collective-permute-start.24) | collective-permute-done | bytes 589856 | tf_op jit(solution)/shard_map/ppermute | solution.py:1000
  362.2 5.9 %collective-permute-start.25 = (f32[16,1536]{1,0:T(8,128)S(1)}, f32[16,1536]{1,0:T(8,128)S(1)}, u32[]{:S(2)}, u32[]{:S(2)}) collective-permute-start(f32[16,1536]{1,0:T(8,128)S(1)} %copy-done.17), channel_id=1, source_target_pairs={{0,8},{2,10},{4,12},{6,14},{8,0},{10,2},{12,4},{14,6},{16,24},{18,... | collective-permute-start | bytes 294920 | tf_op jit(solution)/shard_map/ppermute | solution.py:1000
  368.1 3.5 fold.22
  371.6 3.5 all-to-all-start.1
  376.1 2.3 fold.23
  378.4 2.6 fold.24
  381.0 7.0 %collective-permute-done.25.b_ref = f32[16,1536]{1,0:T(8,128)S(1)} collective-permute-done((f32[16,1536]{1,0:T(8,128)S(1)}, f32[16,1536]{1,0:T(8,128)S(1)}, u32[]{:S(2)}, u32[]{:S(2)}) %collective-permute-start.25) | collective-permute-done | bytes 98336 | tf_op jit(solution)/shard_map/ppermute | solution.py:1000
  388.7 1.6 added.6.a_ref
  390.3 3.4 select_select_fusion
  393.7 12.4 %collective-permute-done.26.b_ref = f32[16,1536]{1,0:T(8,128)S(1)} collective-permute-done((f32[16,1536]{1,0:T(8,128)}, f32[16,1536]{1,0:T(8,128)S(1)}, u32[]{:S(2)}, u32[]{:S(2)}) %collective-permute-start.26) | collective-permute-done | bytes 98336 | tf_op jit(solution)/shard_map/ppermute | solution.py:1000
  412.7 2.5 fold.25
  (131 shorter events, 36.2 us)
Async XLA Ops:
  7.2 129.1 %all-gather.3.cloned.1.call-start = ((), (), s32[]{:S(2)}) async-start(), calls=%async_computation.6 | async-start | bytes 7864320 | tf_op jit(solution)/shard_map/all_gather | solution.py:1095
  12.6 10.7 %copy-start.9 = (bf16[1536,768]{1,0:T(8,128)(2,1)S(1)}, bf16[1536,768]{1,0:T(8,128)(2,1)}, u32[]{:S(2)}) copy-start(bf16[1536,768]{1,0:T(8,128)(2,1)} %refs_6_.1) | copy-start | bytes 7077892
  17.0 199.0 %reduce-scatter.3.cloned.1.call-start = ((), (), s32[]{:S(2)}) async-start(), calls=%async_computation.4 | async-start | bytes 7864320 | tf_op jit(solution)/shard_map/reduce_scatter | solution.py:1157
  17.1 53.2 %collective-permute-start.2 = (bf16[264,1536]{1,0:T(8,128)(2,1)}, bf16[264,1536]{1,0:T(8,128)(2,1)S(1)}, u32[]{:S(2)}, u32[]{:S(2)}) collective-permute-start(bf16[264,1536]{1,0:T(8,128)(2,1)} %get-tuple-element.124), channel_id=1, source_target_pairs={{0,2},{2,4},{4,6},{6,8},{8,10},{10,12},{12,14},{14,16},{16,18},{18... | collective-permute-start | bytes 2433032 | tf_op jit(solution)/shard_map/ppermute | solution.py:1091
  22.0 53.8 %collective-permute-start.3 = (bf16[264,1536]{1,0:T(8,128)(2,1)}, bf16[264,1536]{1,0:T(8,128)(2,1)}, u32[]{:S(2)}, u32[]{:S(2)}) collective-permute-start(bf16[264,1536]{1,0:T(8,128)(2,1)} %get-tuple-element.125), channel_id=1, source_target_pairs={{2,0},{4,2},{6,4},{8,6},{10,8},{12,10},{14,12},{16,14},{18,16},{20... | collective-permute-start | bytes 2433032 | tf_op jit(solution)/shard_map/ppermute | solution.py:1092
  23.3 3.8 copy-start.8
  23.3 3.8 copy-start.10
  27.1 2.3 copy-start.7
  29.4 2.3 copy-start.6
  31.7 2.5 copy-start.23
  34.2 1.1 copy-start.26
  53.8 5.1 %copy-start.29 = (s32[4]{0:T(128)S(1)}, s32[4]{0:T(128)}, u32[]{:S(2)}) copy-start(s32[4]{0:T(128)} %constant.36.clone) | copy-start | bytes 52
  53.8 5.7 %copy-start.24 = (f32[1536]{0:T(1024)S(1)}, f32[1536]{0:T(1024)}, u32[]{:S(2)}) copy-start(f32[1536]{0:T(1024)} %param.31) | copy-start | bytes 18436
  58.4 2.5 collective-permute-start
  58.4 3.6 collective-permute-start.1
  60.9 1.1 copy-start.13
  62.0 0.9 copy-start.14
  70.3 5.5 %copy-start.11 = (bf16[264,1536]{1,0:T(8,128)(2,1)}, bf16[264,1536]{1,0:T(8,128)(2,1)S(1)}, u32[]{:S(2)}) copy-start(bf16[264,1536]{1,0:T(8,128)(2,1)S(1)} %collective-permute-done.2.low_ref) | copy-start | bytes 2433028
  106.8 212.7 %reduce-scatter.5.cloned.1.call-start = ((), (), s32[]{:S(2)}) async-start(), calls=%async_computation.5 | async-start | bytes 7864320 | tf_op jit(solution)/shard_map/reduce_scatter | solution.py:1157
  106.9 0.7 copy-start.27
  106.9 0.7 copy-start.28
  115.3 69.6 %collective-permute-start.6 = (bf16[768,2048]{1,0:T(8,128)(2,1)}, bf16[768,2048]{1,0:T(8,128)(2,1)S(1)}, u32[]{:S(2)}, u32[]{:S(2)}) collective-permute-start(bf16[768,2048]{1,0:T(8,128)(2,1)} %wgrad.4), channel_id=1, source_target_pairs={{0,8},{2,10},{4,12},{6,14},{8,0},{10,2},{12,4},{14,6},{16,24},{18,... | collective-permute-start | bytes 9437192 | tf_op jit(solution)/shard_map/ppermute | solution.py:1000
  128.3 8.0 %collective-permute-start.4 = (bf16[256,1536]{1,0:T(8,128)(2,1)}, bf16[256,1536]{1,0:T(8,128)(2,1)}, u32[]{:S(2)}, u32[]{:S(2)}) collective-permute-start(bf16[256,1536]{1,0:T(8,128)(2,1)} %get-tuple-element.148.upper_ref), channel_id=1, source_target_pairs={{0,1},{1,0},{2,3},{3,2},{4,5},{5,4},{6,7},{7,6},{8,9},{9,8},{10,11... | collective-permute-start | bytes 2359304 | tf_op jit(solution)/shard_map/ppermute | solution.py:1000
  128.3 8.0 %collective-permute-start.5 = (bf16[256,1536]{1,0:T(8,128)(2,1)}, bf16[256,1536]{1,0:T(8,128)(2,1)}, u32[]{:S(2)}, u32[]{:S(2)}) collective-permute-start(bf16[256,1536]{1,0:T(8,128)(2,1)} %get-tuple-element.149.lower_ref), channel_id=1, source_target_pairs={{0,1},{1,0},{2,3},{3,2},{4,5},{5,4},{6,7},{7,6},{8,9},{9,8},{10,11... | collective-permute-start | bytes 2359304 | tf_op jit(solution)/shard_map/ppermute | solution.py:1000
  171.0 60.9 %all-to-all-start = ((bf16[4,512,768]{2,1,0:T(8,128)(2,1)}), bf16[4,512,768]{2,1,0:T(8,128)(2,1)}, u32[]{:S(2)}, u32[]{:S(2)}) async-start(bf16[4,512,768]{2,1,0:T(8,128)(2,1)} %get-tuple-element.167.refs_0_.refs_1_.refs_2_.refs_3_), calls=%async_computation.1 | async-start | bytes 6291456 | tf_op jit(solution)/shard_map/all_to_all | solution.py:1182
  184.8 1.6 copy-start
  200.5 23.5 %collective-permute-start.11 = (bf16[256,1536]{1,0:T(8,128)(2,1)}, bf16[256,1536]{1,0:T(8,128)(2,1)S(1)}, u32[]{:S(2)}, u32[]{:S(2)}) collective-permute-start(bf16[256,1536]{1,0:T(8,128)(2,1)} %get-tuple-element.168.upper_ref), channel_id=1, source_target_pairs={{0,1},{1,0},{2,3},{3,2},{4,5},{5,4},{6,7},{7,6},{8,9},{9,8},{10,11... | collective-permute-start | bytes 2359304 | tf_op jit(solution)/shard_map/ppermute | solution.py:1000
  200.5 23.5 %collective-permute-start.12 = (bf16[256,1536]{1,0:T(8,128)(2,1)}, bf16[256,1536]{1,0:T(8,128)(2,1)}, u32[]{:S(2)}, u32[]{:S(2)}) collective-permute-start(bf16[256,1536]{1,0:T(8,128)(2,1)} %get-tuple-element.169.lower_ref), channel_id=1, source_target_pairs={{0,1},{1,0},{2,3},{3,2},{4,5},{5,4},{6,7},{7,6},{8,9},{9,8},{10,11... | collective-permute-start | bytes 2359304 | tf_op jit(solution)/shard_map/ppermute | solution.py:1000
  217.9 38.2 %collective-permute-start.10 = (bf16[192,2048]{1,0:T(8,128)(2,1)}, bf16[192,2048]{1,0:T(8,128)(2,1)}, u32[]{:S(2)}, u32[]{:S(2)}) collective-permute-start(bf16[192,2048]{1,0:T(8,128)(2,1)} %fold.14), channel_id=1, source_target_pairs={{0,8},{2,10},{4,12},{6,14},{8,0},{10,2},{12,4},{14,6},{16,24},{18,... | collective-permute-start | bytes 2359304 | tf_op jit(solution)/shard_map/ppermute | solution.py:1000
  221.2 48.8 %collective-permute-start.9 = (bf16[768,768]{1,0:T(8,128)(2,1)}, bf16[768,768]{1,0:T(8,128)(2,1)S(1)}, u32[]{:S(2)}, u32[]{:S(2)}) collective-permute-start(bf16[768,768]{1,0:T(8,128)(2,1)} %wgrad.6), channel_id=1, source_target_pairs={{0,2},{2,0},{4,6},{6,4},{8,10},{10,8},{12,14},{14,12},{16,18},{18,... | collective-permute-start | bytes 3538952 | tf_op jit(solution)/shard_map/ppermute | solution.py:1000
  221.2 72.2 %collective-permute-start.15 = (bf16[384,2048]{1,0:T(8,128)(2,1)}, bf16[384,2048]{1,0:T(8,128)(2,1)S(1)}, u32[]{:S(2)}, u32[]{:S(2)}) collective-permute-start(bf16[384,2048]{1,0:T(8,128)(2,1)} %fold.13), channel_id=1, source_target_pairs={{0,16},{2,18},{4,20},{6,22},{8,24},{10,26},{12,28},{14,30},{16,0},... | collective-permute-start | bytes 4718600 | tf_op jit(solution)/shard_map/ppermute | solution.py:1000
  224.0 0.9 copy-start.12
  231.9 7.0 %copy-start.15 = (bf16[256,1536]{1,0:T(8,128)(2,1)S(1)}, bf16[256,1536]{1,0:T(8,128)(2,1)}, u32[]{:S(2)}) copy-start(bf16[256,1536]{1,0:T(8,128)(2,1)} %get-tuple-element.171.upper_ref) | copy-start | bytes 2359300
  238.8 68.7 %collective-permute-start.21 = (bf16[768,768]{1,0:T(8,128)(2,1)}, bf16[768,768]{1,0:T(8,128)(2,1)}, u32[]{:S(2)}, u32[]{:S(2)}) collective-permute-start(bf16[768,768]{1,0:T(8,128)(2,1)} %wgrad_plane.2), channel_id=1, source_target_pairs={{0,8},{2,10},{4,12},{6,14},{8,0},{10,2},{12,4},{14,6},{16,24},{18,... | collective-permute-start | bytes 3538952 | tf_op jit(solution)/shard_map/ppermute | solution.py:1000
  238.9 35.7 %collective-permute-start.7 = (bf16[256,1536]{1,0:T(8,128)(2,1)S(1)}, bf16[256,1536]{1,0:T(8,128)(2,1)}, u32[]{:S(2)}, u32[]{:S(2)}) collective-permute-start(bf16[256,1536]{1,0:T(8,128)(2,1)S(1)} %copy-done.15), channel_id=1, source_target_pairs={{0,1},{1,0},{2,3},{3,2},{4,5},{5,4},{6,7},{7,6},{8,9},{9,8},{10,11... | collective-permute-start | bytes 2359304 | tf_op jit(solution)/shard_map/ppermute | solution.py:1000
  256.1 20.6 %collective-permute-start.8 = (bf16[256,1536]{1,0:T(8,128)(2,1)}, bf16[256,1536]{1,0:T(8,128)(2,1)}, u32[]{:S(2)}, u32[]{:S(2)}) collective-permute-start(bf16[256,1536]{1,0:T(8,128)(2,1)} %get-tuple-element.172.lower_ref), channel_id=1, source_target_pairs={{0,1},{1,0},{2,3},{3,2},{4,5},{5,4},{6,7},{7,6},{8,9},{9,8},{10,11... | collective-permute-start | bytes 2359304 | tf_op jit(solution)/shard_map/ppermute | solution.py:1000
  264.8 9.9 %copy-start.30 = (bf16[96,2048]{1,0:T(8,128)(2,1)S(1)}, bf16[96,2048]{1,0:T(8,128)(2,1)}, u32[]{:S(2)}) copy-start(bf16[96,2048]{1,0:T(8,128)(2,1)} %fold.15) | copy-start | bytes 1179652
  264.8 12.0 %copy-start.18 = (f32[16,1536]{1,0:T(8,128)S(1)}, f32[16,1536]{1,0:T(8,128)}, u32[]{:S(2)}) copy-start(f32[16,1536]{1,0:T(8,128)} %get-tuple-element.177.a_ref) | copy-start | bytes 294916
  269.9 1.0 copy-start.2
  274.3 45.2 %collective-permute-start.18 = (bf16[384,768]{1,0:T(8,128)(2,1)}, bf16[384,768]{1,0:T(8,128)(2,1)S(1)}, u32[]{:S(2)}, u32[]{:S(2)}) collective-permute-start(bf16[384,768]{1,0:T(8,128)(2,1)} %fold.16), channel_id=1, source_target_pairs={{0,4},{2,6},{4,0},{6,2},{8,12},{10,14},{12,8},{14,10},{16,20},{18,... | collective-permute-start | bytes 1769480 | tf_op jit(solution)/shard_map/ppermute | solution.py:1000
  274.7 36.2 %collective-permute-start.20 = (bf16[96,2048]{1,0:T(8,128)(2,1)S(1)}, bf16[96,2048]{1,0:T(8,128)(2,1)S(1)}, u32[]{:S(2)}, u32[]{:S(2)}) collective-permute-start(bf16[96,2048]{1,0:T(8,128)(2,1)S(1)} %copy-done.30), channel_id=1, source_target_pairs={{0,16},{2,18},{4,20},{6,22},{8,24},{10,26},{12,28},{14,30},{16,0},... | collective-permute-start | bytes 1179656 | tf_op jit(solution)/shard_map/ppermute | solution.py:1000
  276.7 7.8 %collective-permute-start.16 = (f32[16,1536]{1,0:T(8,128)S(1)}, f32[16,1536]{1,0:T(8,128)S(1)}, u32[]{:S(2)}, u32[]{:S(2)}) collective-permute-start(f32[16,1536]{1,0:T(8,128)S(1)} %copy-done.18), channel_id=1, source_target_pairs={{0,2},{2,0},{4,6},{6,4},{8,10},{10,8},{12,14},{14,12},{16,18},{18,... | collective-permute-start | bytes 294920 | tf_op jit(solution)/shard_map/ppermute | solution.py:1000
  284.5 0.6 copy-start.21
  286.8 27.0 %collective-permute-start.19 = (f32[16,1536]{1,0:T(8,128)}, f32[16,1536]{1,0:T(8,128)S(1)}, u32[]{:S(2)}, u32[]{:S(2)}) collective-permute-start(f32[16,1536]{1,0:T(8,128)} %added.4.a_ref), channel_id=1, source_target_pairs={{0,4},{2,6},{4,0},{6,2},{8,12},{10,14},{12,8},{14,10},{16,20},{18,... | collective-permute-start | bytes 294920 | tf_op jit(solution)/shard_map/ppermute | solution.py:1000
  293.4 1.1 copy-start.1
  297.0 34.0 %collective-permute-start.17 = (bf16[192,2048]{1,0:T(8,128)(2,1)}, bf16[192,2048]{1,0:T(8,128)(2,1)S(1)}, u32[]{:S(2)}, u32[]{:S(2)}) collective-permute-start(bf16[192,2048]{1,0:T(8,128)(2,1)} %fold.17), channel_id=1, source_target_pairs={{0,2},{2,0},{4,6},{6,4},{8,10},{10,8},{12,14},{14,12},{16,18},{18,... | collective-permute-start | bytes 2359304 | tf_op jit(solution)/shard_map/ppermute | solution.py:1000
  310.8 0.8 copy-start.31
  313.8 0.6 copy-start.20
  316.1 14.9 %copy-start.25 = (s32[48]{0:T(128)S(1)}, s32[48]{0:T(128)}, u32[]{:S(2)}) copy-start(s32[48]{0:T(128)} %dealing_ref.5) | copy-start | bytes 580
  319.5 0.9 copy-start.3
  322.7 52.4 %collective-permute-start.23 = (bf16[192,2816]{1,0:T(8,128)(2,1)}, bf16[192,2816]{1,0:T(8,128)(2,1)S(1)}, u32[]{:S(2)}, u32[]{:S(2)}) collective-permute-start(bf16[192,2816]{1,0:T(8,128)(2,1)} %fold.20), channel_id=1, source_target_pairs={{0,8},{2,10},{4,12},{6,14},{8,0},{10,2},{12,4},{14,6},{16,24},{18,... | collective-permute-start | bytes 3244040 | tf_op jit(solution)/shard_map/ppermute | solution.py:1000
  326.6 35.6 %collective-permute-start.24 = (bf16[384,768]{1,0:T(8,128)(2,1)}, bf16[384,768]{1,0:T(8,128)(2,1)}, u32[]{:S(2)}, u32[]{:S(2)}) collective-permute-start(bf16[384,768]{1,0:T(8,128)(2,1)} %fold.18), channel_id=1, source_target_pairs={{0,16},{2,18},{4,20},{6,22},{8,24},{10,26},{12,28},{14,30},{16,0},... | collective-permute-start | bytes 1769480 | tf_op jit(solution)/shard_map/ppermute | solution.py:1000
  328.3 52.7 %collective-permute-start.13 = (bf16[256,1536]{1,0:T(8,128)(2,1)}, bf16[256,1536]{1,0:T(8,128)(2,1)S(1)}, u32[]{:S(2)}, u32[]{:S(2)}) collective-permute-start(bf16[256,1536]{1,0:T(8,128)(2,1)} %get-tuple-element.186), channel_id=1, source_target_pairs={{0,2},{2,4},{4,6},{6,8},{8,10},{10,12},{12,14},{14,16},{16,18},{18... | collective-permute-start | bytes 2359304 | tf_op jit(solution)/shard_map/ppermute | solution.py:1236
  329.6 51.4 %collective-permute-start.14 = (bf16[256,1536]{1,0:T(8,128)(2,1)}, bf16[256,1536]{1,0:T(8,128)(2,1)S(1)}, u32[]{:S(2)}, u32[]{:S(2)}) collective-permute-start(bf16[256,1536]{1,0:T(8,128)(2,1)} %get-tuple-element.187), channel_id=1, source_target_pairs={{2,0},{4,2},{6,4},{8,6},{10,8},{12,10},{14,12},{16,14},{18,16},{20... | collective-permute-start | bytes 2359304 | tf_op jit(solution)/shard_map/ppermute | solution.py:1237
  331.0 31.2 %copy-start.17 = (f32[16,1536]{1,0:T(8,128)S(1)}, f32[16,1536]{1,0:T(8,128)}, u32[]{:S(2)}) copy-start(f32[16,1536]{1,0:T(8,128)} %added.5.a_ref) | copy-start | bytes 294916
  331.0 0.9 copy-start.5
  334.2 44.2 %collective-permute-start.22 = (bf16[96,2048]{1,0:T(8,128)(2,1)}, bf16[96,2048]{1,0:T(8,128)(2,1)}, u32[]{:S(2)}, u32[]{:S(2)}) collective-permute-start(bf16[96,2048]{1,0:T(8,128)(2,1)} %fold.21), channel_id=1, source_target_pairs={{0,4},{2,6},{4,0},{6,2},{8,12},{10,14},{12,8},{14,10},{16,20},{18,... | collective-permute-start | bytes 1179656 | tf_op jit(solution)/shard_map/ppermute | solution.py:1000
  362.2 25.8 %collective-permute-start.25 = (f32[16,1536]{1,0:T(8,128)S(1)}, f32[16,1536]{1,0:T(8,128)S(1)}, u32[]{:S(2)}, u32[]{:S(2)}) collective-permute-start(f32[16,1536]{1,0:T(8,128)S(1)} %copy-done.17), channel_id=1, source_target_pairs={{0,8},{2,10},{4,12},{6,14},{8,0},{10,2},{12,4},{14,6},{16,24},{18,... | collective-permute-start | bytes 294920 | tf_op jit(solution)/shard_map/ppermute | solution.py:1000
  371.6 43.6 %all-to-all-start.1 = ((bf16[4,96,768]{2,1,0:T(8,128)(2,1)}), bf16[4,96,768]{2,1,0:T(8,128)(2,1)S(1)}, u32[]{:S(2)}, u32[]{:S(2)}) async-start(bf16[4,96,768]{2,1,0:T(8,128)(2,1)} %bitcast.38), calls=%async_computation.3 | async-start | bytes 1179648 | tf_op jit(solution)/shard_map/all_to_all | solution.py:1241
  375.1 1.0 copy-start.4
  378.4 33.4 %collective-permute-start.27 = (bf16[96,2816]{1,0:T(8,128)(2,1)}, bf16[96,2816]{1,0:T(8,128)(2,1)S(1)}, u32[]{:S(2)}, u32[]{:S(2)}) collective-permute-start(bf16[96,2816]{1,0:T(8,128)(2,1)} %fold.23), channel_id=1, source_target_pairs={{0,16},{2,18},{4,20},{6,22},{8,24},{10,26},{12,28},{14,30},{16,0},... | collective-permute-start | bytes 1622024 | tf_op jit(solution)/shard_map/ppermute | solution.py:1000
  390.3 15.8 %collective-permute-start.26 = (f32[16,1536]{1,0:T(8,128)}, f32[16,1536]{1,0:T(8,128)S(1)}, u32[]{:S(2)}, u32[]{:S(2)}) collective-permute-start(f32[16,1536]{1,0:T(8,128)} %added.6.a_ref), channel_id=1, source_target_pairs={{0,16},{2,18},{4,20},{6,22},{8,24},{10,26},{12,28},{14,30},{16,0},... | collective-permute-start | bytes 294920 | tf_op jit(solution)/shard_map/ppermute | solution.py:1000
  406.1 0.6 copy-start.22
  411.8 0.8 copy-start.16
  (1 other events, 0.6 us)
Sparse Core Ops, SparseCore 0:
  17.1 99.9 all-gather.2
  120.1 95.9 reduce-scatter.2
  219.0 100.4 reduce-scatter.4

commit v4 on v3

--- a/solution.py
+++ b/solution.py
@@ -941,12 +941,13 @@
 
 def ffn_kernel(
     order_ref, normed_ref, d_final_ref, gate_ref, up_ref, down_ref,
-    inner_ref, d_gate_ref, d_up_ref, g_gate_ref, g_up_ref, turned, packed,
+    inner_ref, d_gate_ref, d_up_ref, g_gate_ref, g_up_ref, turned, packed, packed_up,
 ):
 
     @pl.when(pl.program_id(0) == 0)
     def _():
         pack(normed_ref[...], order_ref, turned, packed)
+        pack(normed_ref[...], order_ref, turned, packed_up, turned.shape[0])
 
     gate = dot_nn(normed_ref[...], gate_ref[...])
     lift = dot_nn(normed_ref[...], up_ref[...])
@@ -959,7 +960,7 @@
     d_gate_ref[...] = d_gate
     d_up_ref[...] = d_up
     g_gate_ref[...] = dot_nn(packed[...], d_gate).astype(BF)
-    g_up_ref[...] = dot_nn(packed[...], d_up).astype(BF)
+    g_up_ref[...] = dot_nn(packed_up[...], d_up).astype(BF)
 
 
 def ffn(order, size, normed, d_final, w_gate, w_up, w_down, tile=512):
@@ -985,6 +986,7 @@
             out_specs=[out, out, out, column, column],
             scratch_shapes=[
                 pltpu.VMEM((size, width // size, rows), BF),
+                pltpu.VMEM((width, rows), BF),
                 pltpu.VMEM((width, rows), BF),
             ],
         ),
@@ -1083,6 +1085,10 @@
     groups = [[i + j for j in range(4)] for i in range(0, size, 4)]
     order_line = (me >> 2) ^ flips_of(size // 4, [b - 2 for b in line])
     order_plane = (jnp.arange(4, dtype=jnp.int32)[:, None] + 4 * order_line[None, :]).reshape(-1)
+    order_natural = (
+        jnp.arange(4, dtype=jnp.int32)[:, None] + jnp.arange(0, size, 4, dtype=jnp.int32)[None, :]
+    ).reshape(-1)
+    line_groups = [[i + j for j in range(0, size, 4)] for i in range(4)]
     order_zxy = me ^ flips_of(size, line + plane)
     order_xyz = me ^ flips_of(size, bits)
     order = Order()
@@ -1159,7 +1165,10 @@
         )
 
     inner, d_gate, d_up, gate_all, up_all = order.mark(
-        *ffn(order_plane, size, order.gate(normed2), d_final, w_gate, w_up, w_down)
+        *ffn(
+            jnp.concatenate([order_plane, order_natural]),
+            size, order.gate(normed2), d_final, w_gate, w_up, w_down,
+        )
     )
     gate_sum, up_sum = plane_sum(gate_all), plane_sum(up_all)
     down_leave = wgrad_of(order_zxy[:first], d_final, [inner])
@@ -1232,7 +1241,11 @@
         attns = leave(attns, attn_height, bit)
     (g_gate,) = finish([gates])
     small_step()
-    ups = leave([stream(up_sum)] + outs, heights[0], line[0])
+    outs = leave(outs, heights[0], line[0])
+    up_sum = order.mark(order.gate(up_sum))
+    up_line = lax.psum_scatter(
+        up_sum, "dp", scatter_dimension=0, tiled=True, axis_index_groups=line_groups
+    )
     out_low = lax.ppermute(deal_up, "dp", up)
     out_high = lax.ppermute(deal_down, "dp", down)
     height //= 2
@@ -1242,12 +1255,13 @@
         attn_sum.reshape(4, block, columns), "dp", 0, 0, axis_index_groups=groups
     )
     for low, bit in zip(heights[1:], line[1:]):
-        ups = leave(ups, low, bit)
+        outs = leave(outs, low, bit)
     (g_down,) = finish([downs])
     out_low, out_high = order.mark(*order.gate(out_low, out_high))
     while small_got is not None:
         small_step()
-    g_up, g_out = finish([[up_one] for up_one in ups])
+    (g_out,) = finish([outs])
+    g_up = order.gate(up_line).astype(F32)
     g_query, g_key, g_value, g_house = order.gate(plane_rows).astype(F32)
 
     taps = conv_taps.shape[0]

time: 429 us -> 425 us (level)
  starting transfers between devices: 58.1 us -> 42.5 us
  waiting for transfers between devices: 92.8 us -> 104 us
    ppermute x24, starting transfers between devices: 40.8 us -> 22.2 us  [swap(): return lax.ppermute(x, axis, [(i, i ^ 1 << bit) for i in range(size)])]
    ppermute x24, waiting for transfers between devices: 73.6 us -> 90.2 us  [swap(): return lax.ppermute(x, axis, [(i, i ^ 1 << bit) for i in range(size)])]
  transfers between devices with their start and end apart: 33 -> 34, of which waited for: 13 -> 13; matrix products, arithmetic and copies ran while one was open for 6% -> 6% of each run, Pallas kernels for 50% -> 50%
where the time goes in v4:
time: 425 us; the launch traced here: 419 us
  Pallas kernels  219 us (52%)
  waiting for transfers between devices  104 us (24%)
  starting transfers between devices  42.5 us (10%)
  local copies, waits for them, and re-layouts  19.1 us (4%)
  between operations  14.5 us (3%)
  matrix products  13.7 us (3%)
  other arithmetic  5.9 us (1%)
    ppermute x24, waiting for transfers between devices, swap(): return lax.ppermute(x, axis, [(i, i ^ 1 << bit) for i in range(size)])  90.2 us
    pallas_call x13, Pallas kernels, fold(): pl.pallas_call(functools.partial(fold_kernel, plan), grid=(height // step...  33.9 us
    pallas_call x4, Pallas kernels, product(): pl.pallas_call(functools.partial(product_kernel, len(lefts), turned, bool...  33.1 us
    pallas_call x1, Pallas kernels, ffn(): pl.pallas_call(ffn_kernel, grid_spec=pltpu.PrefetchScalarGridSpec(num_sca...  25.1 us
    pallas_call x4, Pallas kernels, wgrad(): pl.pallas_call(functools.partial(wgrad_kernel, plan), grid_spec=pltpu.Pre...  24 us
    ppermute x24, starting transfers between devices, swap(): return lax.ppermute(x, axis, [(i, i ^ 1 << bit) for i in range(size)])  22.2 us
    pallas_call x1, Pallas kernels, mixer_backward(): pl.pallas_call(functools.partial(backward_kernel, heads, lengths.shape[1]...  20.9 us
    pallas_call x1, Pallas kernels, mixer_forward(): pl.pallas_call(functools.partial(forward_kernel, heads, lengths.shape[1])...  17.8 us
  transfers between devices with their start and end apart: 34, of which 13 were waited for; matrix products, arithmetic and copies ran while one was open for 6% of the time, Pallas kernels for 50%

profile of v4, /device:TPU:0, one launch (start us, length us, event | category | flops | bytes accessed | tf_op | source)
XLA Modules:
  0.0 418.9 jit_solution(5666722852417964637)
XLA Ops:
  8.5 4.1 slots_to_send.1
  12.6 4.4 %first_norm.1 = (bf16[512,1536]{1,0:T(8,128)(2,1)}, bf16[1536,512]{1,0:T(8,128)(2,1)}) custom-call(bf16[512,1536]{1,0:T(8,128)(2,1)} %tokens_ref.4, f32[1,1536]{1,0:T(1,128)} %broadcast_in_dim.43.gain_ref), custom_call_target="tpu_custom_call" | custom-call | tf_op jit(solution)/shard_map/first_norm/pallas_call | solution.py:574
  17.1 4.9 %collective-permute-start.2 = (bf16[264,1536]{1,0:T(8,128)(2,1)}, bf16[264,1536]{1,0:T(8,128)(2,1)S(1)}, u32[]{:S(2)}, u32[]{:S(2)}) collective-permute-start(bf16[264,1536]{1,0:T(8,128)(2,1)} %get-tuple-element.121), channel_id=1, source_target_pairs={{0,2},{2,4},{4,6},{6,8},{8,10},{10,12},{12,14},{14,16},{16,18},{18... | collective-permute-start | bytes 2433032 | tf_op jit(solution)/shard_map/ppermute | solution.py:1097
  24.0 2.5 convolution_bitcast_fusion.logit_ref
  26.5 4.1 convolution_convert_fusion.v_ref
  30.6 2.3 convolution_convert_fusion.1.k_ref
  32.9 2.3 convolution_convert_fusion.2.q_ref
  35.2 2.5 fusion.5.house_ref
  37.7 17.8 %mixer_forward.1 = (bf16[512,768]{1,0:T(8,128)(2,1)}, bf16[6,8,256,256]{3,2,1,0:T(8,128)(2,1)}) custom-call(s32[16,3]{1,0:T(8,128)} %copy.37.lengths_ref, s32[1]{0:T(128)} %bitcast.me_ref, f32[6,512]{1,0:T(8,128)} %convolution_bitcast_fusion.logit_ref, f32[4,768]{1,0:T(4,128)} %taps_ref.3, f32[512,768]{1,0:T(8,128)} %fusion.5.house_ref, ...), custom_call_target="tpu_custom_call" | custom-call | tf_op jit(solution)/shard_map/mixer_forward/pallas_call | solution.py:221
  55.5 4.6 %product.4 = (bf16[256,1536]{1,0:T(8,128)(2,1)}, bf16[256,1536]{1,0:T(8,128)(2,1)}) custom-call(bf16[512,768]{1,0:T(8,128)(2,1)} %get-tuple-element.161.refs_0_.refs_1_, bf16[768,1536]{1,0:T(8,128)(2,1)} %out_ref.1), custom_call_target="tpu_custom_call" | custom-call | tf_op jit(solution)/shard_map/product/pallas_call | solution.py:781
  64.5 5.5 %hidden_and_norm.1 = (f32[512,1536]{1,0:T(8,128)}, bf16[512,1536]{1,0:T(8,128)(2,1)}) custom-call(bf16[512,1536]{1,0:T(8,128)(2,1)} %tokens_ref.4, bf16[256,1536]{1,0:T(8,128)(2,1)} %get-tuple-element.129.refs_0_, bf16[256,1536]{1,0:T(8,128)(2,1)} %get-tuple-element.130.refs_1_, bf16[256,1536]{1,0:T(8,128)(2,1)} %copy-done.12, bf16[256,1536]{1,0:T(8,128)(2,1)} %copy-done.13, ...), custom_call_target="tpu_custom_call" | custom-call | tf_op jit(solution)/shard_map/hidden_and_norm/pallas_call | solution.py:619
  70.3 5.4 %collective-permute-done.3.high_ref = bf16[264,1536]{1,0:T(8,128)(2,1)} collective-permute-done((bf16[264,1536]{1,0:T(8,128)(2,1)}, bf16[264,1536]{1,0:T(8,128)(2,1)}, u32[]{:S(2)}, u32[]{:S(2)}) %collective-permute-start.3) | collective-permute-done | bytes 811040 | tf_op jit(solution)/shard_map/ppermute | solution.py:1098
  75.8 6.5 %cotangent_arrived.1.d_final_ref.refs_0_ = bf16[512,1536]{1,0:T(8,128)(2,1)} custom-call(s32[16,3]{1,0:T(8,128)} %copy.37.lengths_ref, s32[48]{0:T(128)} %dealing_ref.5, s32[1]{0:T(128)} %bitcast.me_ref, bf16[768,1536]{1,0:T(8,128)(2,1)} %bitcast.35, bf16[264,1536]{1,0:T(8,128)(2,1)} %copy-done.10, bf16[264,1536]{1,0:T(8,128)(2,1)} %collective-permute-done.3.high_ref), custom_call_target="tpu_custom_call" | custom-call | tf_op jit(solution)/shard_map/cotangent_arrived/pallas_call | solution.py:485
  82.3 25.1 %ffn.1 = (bf16[512,2048]{1,0:T(8,128)(2,1)}, bf16[512,2048]{1,0:T(8,128)(2,1)}, bf16[512,2048]{1,0:T(8,128)(2,1)}, bf16[1536,2048]{1,0:T(8,128)(2,1)}, bf16[1536,2048]{1,0:T(8,128)(2,1)}) custom-call(s32[32]{0:T(128)} %pad_add_fusion.order_ref, bf16[512,1536]{1,0:T(8,128)(2,1)} %get-tuple-element.137.normed_ref, ...), custom_call_target="tpu_custom_call" | custom-call | tf_op jit(solution)/shard_map/ffn/pallas_call | solution.py:974
  108.7 7.1 %wgrad.4 = bf16[768,2048]{1,0:T(8,128)(2,1)} custom-call(s32[8]{0:T(128)} %get-tuple-element.242.order_ref, bf16[512,1536]{1,0:T(8,128)(2,1)} %cotangent_arrived.1.d_final_ref.refs_0_, bf16[512,2048]{1,0:T(8,128)(2,1)} %get-tuple-element.167.refs_1_.refs_0_), custom_call_target="tpu_custom_call" | custom-call | tf_op jit(solution)/shard_map/wgrad/pallas_call | solution.py:888
  117.4 11.4 %product.5 = (bf16[256,1536]{1,0:T(8,128)(2,1)}, bf16[256,1536]{1,0:T(8,128)(2,1)}) custom-call(bf16[512,2048]{1,0:T(8,128)(2,1)} %get-tuple-element.144.refs_0_, bf16[512,2048]{1,0:T(8,128)(2,1)} %get-tuple-element.140.refs_1_, bf16[1536,2048]{1,0:T(8,128)(2,1)} %refs_2_.1, bf16[1536,2048]{1,0:T(8,128)(2,1)} %refs_3_.1), custom_call_target="tpu_custom_call" | custom-call | tf_op jit(solution)/shard_map/product/pallas_call | solution.py:781
  129.9 7.0 %wgrad.5.refs_0_ = bf16[768,2048]{1,0:T(8,128)(2,1)} custom-call(s32[8]{0:T(128)} %get-tuple-element.241.order_ref, bf16[512,1536]{1,0:T(8,128)(2,1)} %cotangent_arrived.1.d_final_ref.refs_0_, bf16[512,2048]{1,0:T(8,128)(2,1)} %get-tuple-element.167.refs_1_.refs_0_), custom_call_target="tpu_custom_call" | custom-call | tf_op jit(solution)/shard_map/wgrad/pallas_call | solution.py:888
  136.9 9.9 %branch_back.1 = (f32[512,1536]{1,0:T(8,128)}, bf16[512,1536]{1,0:T(8,128)(2,1)}, bf16[512,768]{1,0:T(8,128)(2,1)}, f32[1,1536]{1,0:T(1,128)}) custom-call(bf16[256,1536]{1,0:T(8,128)(2,1)} %get-tuple-element.145.upper_ref, bf16[256,1536]{1,0:T(8,128)(2,1)} %get-tuple-element.146.lower_ref, bf16[256,1536]{1,0:T(8,128)(2,1)} %collective-permute-done.4.other_upper_ref, ...), custom_call_target="tpu_custom_call" | custom-call | tf_op jit(solution)/shard_map/branch_back/pallas_call | solution.py:672
  146.8 4.8 %wgrad.6 = bf16[768,768]{1,0:T(8,128)(2,1)} custom-call(s32[8]{0:T(128)} %get-tuple-element.240.order_ref, bf16[512,1536]{1,0:T(8,128)(2,1)} %get-tuple-element.153.refs_0_, bf16[512,768]{1,0:T(8,128)(2,1)} %get-tuple-element.161.refs_0_.refs_1_), custom_call_target="tpu_custom_call" | custom-call | tf_op jit(solution)/shard_map/wgrad/pallas_call | solution.py:888
  151.6 20.9 %mixer_backward.1 = (bf16[4,512,768]{2,1,0:T(8,128)(2,1)}, f32[6,512]{1,0:T(8,128)}, f32[4,768]{1,0:T(4,128)}) custom-call(s32[16,3]{1,0:T(8,128)} %copy.37.lengths_ref, s32[1]{0:T(128)} %bitcast.me_ref, f32[6,512]{1,0:T(8,128)} %convolution_bitcast_fusion.logit_ref, f32[4,768]{1,0:T(4,128)} %taps_ref.3, f32[512,768]{1,0:T(8,128)} %fusion.5.house_ref, ...), custom_call_target="tpu_custom_call" | custom-call | tf_op jit(solution)/shard_map/mixer_backward/pallas_call | solution.py:366
  172.5 4.7 %all-to-all-start = ((bf16[4,512,768]{2,1,0:T(8,128)(2,1)}), bf16[4,512,768]{2,1,0:T(8,128)(2,1)}, u32[]{:S(2)}, u32[]{:S(2)}) async-start(bf16[4,512,768]{2,1,0:T(8,128)(2,1)} %get-tuple-element.164.refs_0_.refs_1_.refs_2_.refs_3_), calls=%async_computation.1 | async-start | bytes 6291456 | tf_op jit(solution)/shard_map/all_to_all | solution.py:1191
  178.2 5.0 %wgrad.7.refs_0_ = bf16[768,768]{1,0:T(8,128)(2,1)} custom-call(s32[8]{0:T(128)} %get-tuple-element.239.order_ref, bf16[512,1536]{1,0:T(8,128)(2,1)} %get-tuple-element.153.refs_0_, bf16[512,768]{1,0:T(8,128)(2,1)} %get-tuple-element.161.refs_0_.refs_1_), custom_call_target="tpu_custom_call" | custom-call | tf_op jit(solution)/shard_map/wgrad/pallas_call | solution.py:888
  183.2 2.2 collective-permute-done.6.refs_1_
  185.4 1.6 copy-done
  187.0 4.0 fold.13
  191.0 10.0 %product.6 = (bf16[256,1536]{1,0:T(8,128)(2,1)}, bf16[256,1536]{1,0:T(8,128)(2,1)}) custom-call(bf16[4,512,768]{2,1,0:T(8,128)(2,1)} %get-tuple-element.164.refs_0_.refs_1_.refs_2_.refs_3_, bf16[4,512,768]{2,1,0:T(8,128)(2,1)} %get-tuple-element.164.refs_0_.refs_1_.refs_2_.refs_3_, bf16[4,512,768]{2,1,0:T(8,128)(2,1)} %get-tuple-element.164.refs_0_.refs_1_.refs_2_.refs_3_, ...), custom_call_target="tpu_custom_call" | custom-call | tf_op jit(solution)/shard_map/product/pallas_call | solution.py:781
  201.5 7.2 %product.7 = (bf16[256,1536]{1,0:T(8,128)(2,1)}, bf16[256,1536]{1,0:T(8,128)(2,1)}) custom-call(bf16[512,2048]{1,0:T(8,128)(2,1)} %get-tuple-element.167.refs_1_.refs_0_, bf16[2048,1536]{1,0:T(8,128)(2,1)} %refs_1_.3), custom_call_target="tpu_custom_call" | custom-call | tf_op jit(solution)/shard_map/product/pallas_call | solution.py:781
  208.7 7.1 %reduce-scatter.4.cloned.1.call-done.refs_0_ = bf16[384,2048]{1,0:T(8,128)(2,1)} async-done(((bf16[1536,2048]{1,0:T(8,128)(2,1)}), bf16[384,2048]{1,0:T(8,128)(2,1)}) %reduce-scatter.4.cloned.1.call-update) | async-done | bytes 1572880 | tf_op jit(solution)/shard_map/reduce_scatter | solution.py:1163
  215.8 1.9 fold.14
  217.7 3.2 collective-permute-start.10
  220.9 2.2 collective-permute-start.15
  223.7 6.7 %input_back.1 = (bf16[512,1536]{1,0:T(8,128)(2,1)}, f32[16,1536]{1,0:T(8,128)}) custom-call(bf16[256,1536]{1,0:T(8,128)(2,1)} %get-tuple-element.165.upper_ref, bf16[256,1536]{1,0:T(8,128)(2,1)} %get-tuple-element.166.lower_ref, bf16[256,1536]{1,0:T(8,128)(2,1)} %collective-permute-done.11.other_upper_ref, ...), custom_call_target="tpu_custom_call" | custom-call | tf_op jit(solution)/shard_map/input_back/pallas_call | solution.py:722
  230.4 6.7 %wgrad_plane.2 = bf16[768,768]{1,0:T(8,128)(2,1)} custom-call(s32[2]{0:T(128)} %get-tuple-element.235.order_ref, bf16[4,1536,512]{2,1,0:T(8,128)(2,1)} %bitcast.33, bf16[4,512,768]{2,1,0:T(8,128)(2,1)} %all-to-all-done.right_ref), custom_call_target="tpu_custom_call" | custom-call | tf_op jit(solution)/shard_map/wgrad_plane/pallas_call | solution.py:924
  237.7 18.4 %collective-permute-done.10.refs_1_ = bf16[192,2048]{1,0:T(8,128)(2,1)} collective-permute-done((bf16[192,2048]{1,0:T(8,128)(2,1)}, bf16[192,2048]{1,0:T(8,128)(2,1)}, u32[]{:S(2)}, u32[]{:S(2)}) %collective-permute-start.10) | collective-permute-done | bytes 786464 | tf_op jit(solution)/shard_map/ppermute | solution.py:1002
  256.1 6.7 %wgrad_plane.3.refs_0_ = bf16[768,768]{1,0:T(8,128)(2,1)} custom-call(s32[2]{0:T(128)} %get-tuple-element.236.order_ref, bf16[4,1536,512]{2,1,0:T(8,128)(2,1)} %bitcast.34, bf16[4,512,768]{2,1,0:T(8,128)(2,1)} %all-to-all-done.right_ref), custom_call_target="tpu_custom_call" | custom-call | tf_op jit(solution)/shard_map/wgrad_plane/pallas_call | solution.py:924
  262.8 2.0 fold.15
  264.8 5.0 %collective-permute-done.9.refs_1_ = bf16[768,768]{1,0:T(8,128)(2,1)} collective-permute-done((bf16[768,768]{1,0:T(8,128)(2,1)}, bf16[768,768]{1,0:T(8,128)(2,1)}, u32[]{:S(2)}, u32[]{:S(2)}) %collective-permute-start.9) | collective-permute-done | bytes 1179680 | tf_op jit(solution)/shard_map/ppermute | solution.py:1002
  269.8 3.4 fold.16
  273.5 2.1 collective-permute-start.20
  275.7 7.9 %rows_dealt.1 = (bf16[768,1536]{1,0:T(8,128)(2,1)}, bf16[256,1536]{1,0:T(8,128)(2,1)}, bf16[256,1536]{1,0:T(8,128)(2,1)}) custom-call(s32[16,3]{1,0:T(8,128)} %copy.37.lengths_ref, s32[48]{0:T(128)} %dealing_ref.5, s32[1]{0:T(128)} %bitcast.me_ref, f32[512,1536]{1,0:T(8,128)} %get-tuple-element.133.hidden_ref, ...), custom_call_target="tpu_custom_call" | custom-call | tf_op jit(solution)/shard_map/rows_dealt/pallas_call | solution.py:543
  284.2 1.6 added.4.a_ref
  287.4 5.6 %collective-permute-done.15.refs_2_ = bf16[384,2048]{1,0:T(8,128)(2,1)S(1)} collective-permute-done((bf16[384,2048]{1,0:T(8,128)(2,1)S(1)}, bf16[384,2048]{1,0:T(8,128)(2,1)S(1)}, u32[]{:S(2)}, u32[]{:S(2)}) %collective-permute-start.15) | collective-permute-done | bytes 1572896 | tf_op jit(solution)/shard_map/ppermute | solution.py:1002
  294.1 2.5 fold.17
  296.6 8.7 %collective-permute-done.21.refs_1_ = bf16[768,768]{1,0:T(8,128)(2,1)} collective-permute-done((bf16[768,768]{1,0:T(8,128)(2,1)}, bf16[768,768]{1,0:T(8,128)(2,1)}, u32[]{:S(2)}, u32[]{:S(2)}) %collective-permute-start.21) | collective-permute-done | bytes 1179680 | tf_op jit(solution)/shard_map/ppermute | solution.py:1002
  305.3 3.4 fold.18
  308.7 2.2 fold.19
  311.6 1.6 added.5.a_ref
  313.2 2.1 fold.20
  315.3 1.7 collective-permute-start.17
  317.0 4.6 %collective-permute-start.13 = (bf16[256,1536]{1,0:T(8,128)(2,1)}, bf16[256,1536]{1,0:T(8,128)(2,1)}, u32[]{:S(2)}, u32[]{:S(2)}) collective-permute-start(bf16[256,1536]{1,0:T(8,128)(2,1)} %get-tuple-element.183), channel_id=1, source_target_pairs={{0,2},{2,4},{4,6},{6,8},{8,10},{10,12},{12,14},{14,16},{16,18},{18... | collective-permute-start | bytes 2359304 | tf_op jit(solution)/shard_map/ppermute | solution.py:1249
  323.0 4.2 collective-permute-start.23
  327.2 14.2 %collective-permute-done.17.refs_3_ = bf16[192,2048]{1,0:T(8,128)(2,1)S(1)} collective-permute-done((bf16[192,2048]{1,0:T(8,128)(2,1)S(1)}, bf16[192,2048]{1,0:T(8,128)(2,1)S(1)}, u32[]{:S(2)}, u32[]{:S(2)}) %collective-permute-start.17) | collective-permute-done | bytes 786464 | tf_op jit(solution)/shard_map/ppermute | solution.py:1002
  342.2 2.3 fold.21
  344.5 23.3 %collective-permute-done.24.refs_2_ = bf16[384,768]{1,0:T(8,128)(2,1)S(1)} collective-permute-done((bf16[384,768]{1,0:T(8,128)(2,1)S(1)}, bf16[384,768]{1,0:T(8,128)(2,1)S(1)}, u32[]{:S(2)}, u32[]{:S(2)}) %collective-permute-start.24) | collective-permute-done | bytes 589856 | tf_op jit(solution)/shard_map/ppermute | solution.py:1002
  368.7 3.5 fold.22
  372.2 11.2 %collective-permute-done.23.refs_3_ = bf16[192,768]{1,0:T(8,128)(2,1)} collective-permute-done((bf16[192,768]{1,0:T(8,128)(2,1)}, bf16[192,768]{1,0:T(8,128)(2,1)}, u32[]{:S(2)}, u32[]{:S(2)}) %collective-permute-start.23) | collective-permute-done | bytes 294944 | tf_op jit(solution)/shard_map/ppermute | solution.py:1002
  383.4 3.5 all-to-all-start.1
  386.9 1.9 fold.23
  389.5 2.7 fold.24
  392.8 1.6 added.6.a_ref
  394.4 2.8 collective-permute-start.26
  397.3 3.2 select_select_fusion
  405.6 2.0 fold.25
  410.0 1.9 convert_element_type.19
  (139 shorter events, 31.2 us)
Async XLA Ops:
  7.2 129.7 %all-gather.3.cloned.1.call-start = ((), (), s32[]{:S(2)}) async-start(), calls=%async_computation.8 | async-start | bytes 7864320 | tf_op jit(solution)/shard_map/all_gather | solution.py:1101
  12.6 10.7 %copy-start.24 = (s32[16,3]{0,1:T(4,128)S(1)}, s32[16,3]{0,1:T(4,128)}, u32[]{:S(2)}) copy-start(s32[16,3]{0,1:T(4,128)} %param.21) | copy-start | bytes 580
  12.6 11.4 %copy-start.21 = (bf16[1536,6]{0,1:T(8,128)(2,1)S(1)}, bf16[1536,6]{0,1:T(8,128)(2,1)}, u32[]{:S(2)}) copy-start(bf16[1536,6]{0,1:T(8,128)(2,1)} %param.28) | copy-start | bytes 55300
  12.6 13.9 %copy-start.6 = (bf16[1536,768]{1,0:T(8,128)(2,1)S(1)}, bf16[1536,768]{1,0:T(8,128)(2,1)}, u32[]{:S(2)}) copy-start(bf16[1536,768]{1,0:T(8,128)(2,1)} %refs_6_.1) | copy-start | bytes 7077892
  17.0 198.8 %reduce-scatter.4.cloned.1.call-start = ((), (), s32[]{:S(2)}) async-start(), calls=%async_computation.5 | async-start | bytes 7864320 | tf_op jit(solution)/shard_map/reduce_scatter | solution.py:1163
  17.1 53.2 %collective-permute-start.2 = (bf16[264,1536]{1,0:T(8,128)(2,1)}, bf16[264,1536]{1,0:T(8,128)(2,1)S(1)}, u32[]{:S(2)}, u32[]{:S(2)}) collective-permute-start(bf16[264,1536]{1,0:T(8,128)(2,1)} %get-tuple-element.121), channel_id=1, source_target_pairs={{0,2},{2,4},{4,6},{6,8},{8,10},{10,12},{12,14},{14,16},{16,18},{18... | collective-permute-start | bytes 2433032 | tf_op jit(solution)/shard_map/ppermute | solution.py:1097
  22.0 53.8 %collective-permute-start.3 = (bf16[264,1536]{1,0:T(8,128)(2,1)}, bf16[264,1536]{1,0:T(8,128)(2,1)}, u32[]{:S(2)}, u32[]{:S(2)}) collective-permute-start(bf16[264,1536]{1,0:T(8,128)(2,1)} %get-tuple-element.122), channel_id=1, source_target_pairs={{2,0},{4,2},{6,4},{8,6},{10,8},{12,10},{14,12},{16,14},{18,16},{20... | collective-permute-start | bytes 2433032 | tf_op jit(solution)/shard_map/ppermute | solution.py:1098
  26.5 4.1 copy-start.5
  26.5 4.1 copy-start.8
  30.6 2.3 copy-start.4
  32.9 2.3 copy-start.3
  55.5 5.2 %copy-start.27 = (s32[4]{0:T(128)S(1)}, s32[4]{0:T(128)}, u32[]{:S(2)}) copy-start(s32[4]{0:T(128)} %constant.37.clone) | copy-start | bytes 52
  55.5 5.3 %copy-start.22 = (f32[1536]{0:T(1024)S(1)}, f32[1536]{0:T(1024)}, u32[]{:S(2)}) copy-start(f32[1536]{0:T(1024)} %param.31) | copy-start | bytes 18436
  60.0 2.5 collective-permute-start
  60.0 3.6 collective-permute-start.1
  62.5 1.1 copy-start.12
  63.7 0.9 copy-start.13
  70.3 5.5 %copy-start.10 = (bf16[264,1536]{1,0:T(8,128)(2,1)}, bf16[264,1536]{1,0:T(8,128)(2,1)S(1)}, u32[]{:S(2)}) copy-start(bf16[264,1536]{1,0:T(8,128)(2,1)S(1)} %collective-permute-done.2.low_ref) | copy-start | bytes 2433028
  107.3 207.9 %reduce-scatter.6.cloned.1.call-start = ((), (), s32[]{:S(2)}) async-start(), calls=%async_computation.6 | async-start | bytes 7864320 | tf_op jit(solution)/shard_map/reduce_scatter | solution.py:1163
  107.4 0.7 copy-start.25
  107.4 0.7 copy-start.26
  115.8 69.6 %collective-permute-start.6 = (bf16[768,2048]{1,0:T(8,128)(2,1)}, bf16[768,2048]{1,0:T(8,128)(2,1)S(1)}, u32[]{:S(2)}, u32[]{:S(2)}) collective-permute-start(bf16[768,2048]{1,0:T(8,128)(2,1)} %wgrad.4), channel_id=1, source_target_pairs={{0,8},{2,10},{4,12},{6,14},{8,0},{10,2},{12,4},{14,6},{16,24},{18,... | collective-permute-start | bytes 9437192 | tf_op jit(solution)/shard_map/ppermute | solution.py:1002
  128.8 8.1 %collective-permute-start.4 = (bf16[256,1536]{1,0:T(8,128)(2,1)}, bf16[256,1536]{1,0:T(8,128)(2,1)}, u32[]{:S(2)}, u32[]{:S(2)}) collective-permute-start(bf16[256,1536]{1,0:T(8,128)(2,1)} %get-tuple-element.145.upper_ref), channel_id=1, source_target_pairs={{0,1},{1,0},{2,3},{3,2},{4,5},{5,4},{6,7},{7,6},{8,9},{9,8},{10,11... | collective-permute-start | bytes 2359304 | tf_op jit(solution)/shard_map/ppermute | solution.py:1002
  128.8 8.1 %collective-permute-start.5 = (bf16[256,1536]{1,0:T(8,128)(2,1)}, bf16[256,1536]{1,0:T(8,128)(2,1)}, u32[]{:S(2)}, u32[]{:S(2)}) collective-permute-start(bf16[256,1536]{1,0:T(8,128)(2,1)} %get-tuple-element.146.lower_ref), channel_id=1, source_target_pairs={{0,1},{1,0},{2,3},{3,2},{4,5},{5,4},{6,7},{7,6},{8,9},{9,8},{10,11... | collective-permute-start | bytes 2359304 | tf_op jit(solution)/shard_map/ppermute | solution.py:1002
  172.5 57.9 %all-to-all-start = ((bf16[4,512,768]{2,1,0:T(8,128)(2,1)}), bf16[4,512,768]{2,1,0:T(8,128)(2,1)}, u32[]{:S(2)}, u32[]{:S(2)}) async-start(bf16[4,512,768]{2,1,0:T(8,128)(2,1)} %get-tuple-element.164.refs_0_.refs_1_.refs_2_.refs_3_), calls=%async_computation.1 | async-start | bytes 6291456 | tf_op jit(solution)/shard_map/all_to_all | solution.py:1191
  177.2 232.8 %reduce-scatter.8.cloned.1.call-start = ((), (), s32[]{:S(2)}) async-start(), calls=%async_computation.7 | async-start | bytes 1966080 | tf_op jit(solution)/shard_map/reduce_scatter | solution.py:1246
  185.4 1.6 copy-start
  201.0 22.7 %collective-permute-start.11 = (bf16[256,1536]{1,0:T(8,128)(2,1)}, bf16[256,1536]{1,0:T(8,128)(2,1)}, u32[]{:S(2)}, u32[]{:S(2)}) collective-permute-start(bf16[256,1536]{1,0:T(8,128)(2,1)} %get-tuple-element.165.upper_ref), channel_id=1, source_target_pairs={{0,1},{1,0},{2,3},{3,2},{4,5},{5,4},{6,7},{7,6},{8,9},{9,8},{10,11... | collective-permute-start | bytes 2359304 | tf_op jit(solution)/shard_map/ppermute | solution.py:1002
  201.0 22.7 %collective-permute-start.12 = (bf16[256,1536]{1,0:T(8,128)(2,1)}, bf16[256,1536]{1,0:T(8,128)(2,1)}, u32[]{:S(2)}, u32[]{:S(2)}) collective-permute-start(bf16[256,1536]{1,0:T(8,128)(2,1)} %get-tuple-element.166.lower_ref), channel_id=1, source_target_pairs={{0,1},{1,0},{2,3},{3,2},{4,5},{5,4},{6,7},{7,6},{8,9},{9,8},{10,11... | collective-permute-start | bytes 2359304 | tf_op jit(solution)/shard_map/ppermute | solution.py:1002
  208.7 12.3 %copy-start.9 = (bf16[384,2048]{1,0:T(8,128)(2,1)S(1)}, bf16[384,2048]{1,0:T(8,128)(2,1)}, u32[]{:S(2)}) copy-start(bf16[384,2048]{1,0:T(8,128)(2,1)} %fold.13) | copy-start | bytes 4718596
  217.7 38.4 %collective-permute-start.10 = (bf16[192,2048]{1,0:T(8,128)(2,1)}, bf16[192,2048]{1,0:T(8,128)(2,1)}, u32[]{:S(2)}, u32[]{:S(2)}) collective-permute-start(bf16[192,2048]{1,0:T(8,128)(2,1)} %fold.14), channel_id=1, source_target_pairs={{0,8},{2,10},{4,12},{6,14},{8,0},{10,2},{12,4},{14,6},{16,24},{18,... | collective-permute-start | bytes 2359304 | tf_op jit(solution)/shard_map/ppermute | solution.py:1002
  220.9 48.9 %collective-permute-start.9 = (bf16[768,768]{1,0:T(8,128)(2,1)}, bf16[768,768]{1,0:T(8,128)(2,1)}, u32[]{:S(2)}, u32[]{:S(2)}) collective-permute-start(bf16[768,768]{1,0:T(8,128)(2,1)} %wgrad.6), channel_id=1, source_target_pairs={{0,2},{2,0},{4,6},{6,4},{8,10},{10,8},{12,14},{14,12},{16,18},{18,... | collective-permute-start | bytes 3538952 | tf_op jit(solution)/shard_map/ppermute | solution.py:1002
  220.9 72.0 %collective-permute-start.15 = (bf16[384,2048]{1,0:T(8,128)(2,1)S(1)}, bf16[384,2048]{1,0:T(8,128)(2,1)S(1)}, u32[]{:S(2)}, u32[]{:S(2)}) collective-permute-start(bf16[384,2048]{1,0:T(8,128)(2,1)S(1)} %copy-done.9), channel_id=1, source_target_pairs={{0,16},{2,18},{4,20},{6,22},{8,24},{10,26},{12,28},{14,30},{16,0},... | collective-permute-start | bytes 4718600 | tf_op jit(solution)/shard_map/ppermute | solution.py:1002
  237.1 68.2 %collective-permute-start.21 = (bf16[768,768]{1,0:T(8,128)(2,1)}, bf16[768,768]{1,0:T(8,128)(2,1)}, u32[]{:S(2)}, u32[]{:S(2)}) collective-permute-start(bf16[768,768]{1,0:T(8,128)(2,1)} %wgrad_plane.2), channel_id=1, source_target_pairs={{0,8},{2,10},{4,12},{6,14},{8,0},{10,2},{12,4},{14,6},{16,24},{18,... | collective-permute-start | bytes 3538952 | tf_op jit(solution)/shard_map/ppermute | solution.py:1002
  237.7 35.8 %collective-permute-start.7 = (bf16[256,1536]{1,0:T(8,128)(2,1)}, bf16[256,1536]{1,0:T(8,128)(2,1)}, u32[]{:S(2)}, u32[]{:S(2)}) collective-permute-start(bf16[256,1536]{1,0:T(8,128)(2,1)} %get-tuple-element.168.upper_ref), channel_id=1, source_target_pairs={{0,1},{1,0},{2,3},{3,2},{4,5},{5,4},{6,7},{7,6},{8,9},{9,8},{10,11... | collective-permute-start | bytes 2359304 | tf_op jit(solution)/shard_map/ppermute | solution.py:1002
  256.1 19.6 %collective-permute-start.8 = (bf16[256,1536]{1,0:T(8,128)(2,1)}, bf16[256,1536]{1,0:T(8,128)(2,1)}, u32[]{:S(2)}, u32[]{:S(2)}) collective-permute-start(bf16[256,1536]{1,0:T(8,128)(2,1)} %get-tuple-element.169.lower_ref), channel_id=1, source_target_pairs={{0,1},{1,0},{2,3},{3,2},{4,5},{5,4},{6,7},{7,6},{8,9},{9,8},{10,11... | collective-permute-start | bytes 2359304 | tf_op jit(solution)/shard_map/ppermute | solution.py:1002
  264.8 8.7 %copy-start.30 = (bf16[96,2048]{1,0:T(8,128)(2,1)S(1)}, bf16[96,2048]{1,0:T(8,128)(2,1)}, u32[]{:S(2)}) copy-start(bf16[96,2048]{1,0:T(8,128)(2,1)} %fold.15) | copy-start | bytes 1179652
  264.8 10.8 %copy-start.16 = (f32[16,1536]{1,0:T(8,128)S(1)}, f32[16,1536]{1,0:T(8,128)}, u32[]{:S(2)}) copy-start(f32[16,1536]{1,0:T(8,128)} %get-tuple-element.174.a_ref) | copy-start | bytes 294916
  273.2 39.9 %collective-permute-start.18 = (bf16[384,768]{1,0:T(8,128)(2,1)}, bf16[384,768]{1,0:T(8,128)(2,1)}, u32[]{:S(2)}, u32[]{:S(2)}) collective-permute-start(bf16[384,768]{1,0:T(8,128)(2,1)} %fold.16), channel_id=1, source_target_pairs={{0,4},{2,6},{4,0},{6,2},{8,12},{10,14},{12,8},{14,10},{16,20},{18,... | collective-permute-start | bytes 1769480 | tf_op jit(solution)/shard_map/ppermute | solution.py:1002
  273.5 35.2 %collective-permute-start.20 = (bf16[96,2048]{1,0:T(8,128)(2,1)S(1)}, bf16[96,2048]{1,0:T(8,128)(2,1)}, u32[]{:S(2)}, u32[]{:S(2)}) collective-permute-start(bf16[96,2048]{1,0:T(8,128)(2,1)S(1)} %copy-done.30), channel_id=1, source_target_pairs={{0,16},{2,18},{4,20},{6,22},{8,24},{10,26},{12,28},{14,30},{16,0},... | collective-permute-start | bytes 1179656 | tf_op jit(solution)/shard_map/ppermute | solution.py:1002
  275.6 8.0 %collective-permute-start.16 = (f32[16,1536]{1,0:T(8,128)S(1)}, f32[16,1536]{1,0:T(8,128)S(1)}, u32[]{:S(2)}, u32[]{:S(2)}) collective-permute-start(f32[16,1536]{1,0:T(8,128)S(1)} %copy-done.16), channel_id=1, source_target_pairs={{0,2},{2,0},{4,6},{6,4},{8,10},{10,8},{12,14},{14,12},{16,18},{18,... | collective-permute-start | bytes 294920 | tf_op jit(solution)/shard_map/ppermute | solution.py:1002
  283.6 0.6 copy-start.19
  285.8 25.1 %collective-permute-start.19 = (f32[16,1536]{1,0:T(8,128)}, f32[16,1536]{1,0:T(8,128)S(1)}, u32[]{:S(2)}, u32[]{:S(2)}) collective-permute-start(f32[16,1536]{1,0:T(8,128)} %added.4.a_ref), channel_id=1, source_target_pairs={{0,4},{2,6},{4,0},{6,2},{8,12},{10,14},{12,8},{14,10},{16,20},{18,... | collective-permute-start | bytes 294920 | tf_op jit(solution)/shard_map/ppermute | solution.py:1002
  293.0 1.1 copy-start.1
  313.2 2.1 copy-start.11
  313.2 3.8 copy-start.28
  313.2 9.7 %copy-start.23 = (s32[48]{0:T(128)S(1)}, s32[48]{0:T(128)}, u32[]{:S(2)}) copy-start(s32[48]{0:T(128)} %dealing_ref.5) | copy-start | bytes 580
  315.3 26.0 %collective-permute-start.17 = (bf16[192,2048]{1,0:T(8,128)(2,1)S(1)}, bf16[192,2048]{1,0:T(8,128)(2,1)S(1)}, u32[]{:S(2)}, u32[]{:S(2)}) collective-permute-start(bf16[192,2048]{1,0:T(8,128)(2,1)S(1)} %copy-done.11), channel_id=1, source_target_pairs={{0,2},{2,0},{4,6},{6,4},{8,10},{10,8},{12,14},{14,12},{16,18},{18,... | collective-permute-start | bytes 2359304 | tf_op jit(solution)/shard_map/ppermute | solution.py:1002
  317.0 50.8 %collective-permute-start.24 = (bf16[384,768]{1,0:T(8,128)(2,1)S(1)}, bf16[384,768]{1,0:T(8,128)(2,1)S(1)}, u32[]{:S(2)}, u32[]{:S(2)}) collective-permute-start(bf16[384,768]{1,0:T(8,128)(2,1)S(1)} %copy-done.28), channel_id=1, source_target_pairs={{0,16},{2,18},{4,20},{6,22},{8,24},{10,26},{12,28},{14,30},{16,0},... | collective-permute-start | bytes 1769480 | tf_op jit(solution)/shard_map/ppermute | solution.py:1002
  317.0 75.2 %collective-permute-start.13 = (bf16[256,1536]{1,0:T(8,128)(2,1)}, bf16[256,1536]{1,0:T(8,128)(2,1)}, u32[]{:S(2)}, u32[]{:S(2)}) collective-permute-start(bf16[256,1536]{1,0:T(8,128)(2,1)} %get-tuple-element.183), channel_id=1, source_target_pairs={{0,2},{2,4},{4,6},{6,8},{8,10},{10,12},{12,14},{14,16},{16,18},{18... | collective-permute-start | bytes 2359304 | tf_op jit(solution)/shard_map/ppermute | solution.py:1249
  321.6 70.6 %collective-permute-start.14 = (bf16[256,1536]{1,0:T(8,128)(2,1)}, bf16[256,1536]{1,0:T(8,128)(2,1)}, u32[]{:S(2)}, u32[]{:S(2)}) collective-permute-start(bf16[256,1536]{1,0:T(8,128)(2,1)} %get-tuple-element.184), channel_id=1, source_target_pairs={{2,0},{4,2},{6,4},{8,6},{10,8},{12,10},{14,12},{16,14},{18,16},{20... | collective-permute-start | bytes 2359304 | tf_op jit(solution)/shard_map/ppermute | solution.py:1250
  323.0 44.9 %copy-start.15 = (f32[16,1536]{1,0:T(8,128)S(1)}, f32[16,1536]{1,0:T(8,128)}, u32[]{:S(2)}) copy-start(f32[16,1536]{1,0:T(8,128)} %added.5.a_ref) | copy-start | bytes 294916
  323.0 60.4 %collective-permute-start.23 = (bf16[192,768]{1,0:T(8,128)(2,1)}, bf16[192,768]{1,0:T(8,128)(2,1)}, u32[]{:S(2)}, u32[]{:S(2)}) collective-permute-start(bf16[192,768]{1,0:T(8,128)(2,1)} %fold.20), channel_id=1, source_target_pairs={{0,8},{2,10},{4,12},{6,14},{8,0},{10,2},{12,4},{14,6},{16,24},{18,... | collective-permute-start | bytes 884744 | tf_op jit(solution)/shard_map/ppermute | solution.py:1002
  341.3 0.9 copy-start.2
  344.5 44.2 %collective-permute-start.22 = (bf16[96,2048]{1,0:T(8,128)(2,1)}, bf16[96,2048]{1,0:T(8,128)(2,1)S(1)}, u32[]{:S(2)}, u32[]{:S(2)}) collective-permute-start(bf16[96,2048]{1,0:T(8,128)(2,1)} %fold.21), channel_id=1, source_target_pairs={{0,4},{2,6},{4,0},{6,2},{8,12},{10,14},{12,8},{14,10},{16,20},{18,... | collective-permute-start | bytes 1179656 | tf_op jit(solution)/shard_map/ppermute | solution.py:1002
  367.9 0.8 copy-start.29
  367.9 24.3 %collective-permute-start.25 = (f32[16,1536]{1,0:T(8,128)S(1)}, f32[16,1536]{1,0:T(8,128)S(1)}, u32[]{:S(2)}, u32[]{:S(2)}) collective-permute-start(f32[16,1536]{1,0:T(8,128)S(1)} %copy-done.15), channel_id=1, source_target_pairs={{0,8},{2,10},{4,12},{6,14},{8,0},{10,2},{12,4},{14,6},{16,24},{18,... | collective-permute-start | bytes 294920 | tf_op jit(solution)/shard_map/ppermute | solution.py:1002
  383.4 25.4 %all-to-all-start.1 = ((bf16[4,96,768]{2,1,0:T(8,128)(2,1)}), bf16[4,96,768]{2,1,0:T(8,128)(2,1)S(1)}, u32[]{:S(2)}, u32[]{:S(2)}) async-start(bf16[4,96,768]{2,1,0:T(8,128)(2,1)} %bitcast.38), calls=%async_computation.3 | async-start | bytes 1179648 | tf_op jit(solution)/shard_map/all_to_all | solution.py:1254
  388.8 8.5 %copy-start.7 = (bf16[768,1536]{1,0:T(8,128)(2,1)S(1)}, bf16[768,1536]{1,0:T(8,128)(2,1)}, u32[]{:S(2)}) copy-start(bf16[768,1536]{1,0:T(8,128)(2,1)} %get-tuple-element.185) | copy-start | bytes 7077892
  388.8 16.2 %collective-permute-start.27 = (bf16[96,768]{1,0:T(8,128)(2,1)}, bf16[96,768]{1,0:T(8,128)(2,1)S(1)}, u32[]{:S(2)}, u32[]{:S(2)}) collective-permute-start(bf16[96,768]{1,0:T(8,128)(2,1)} %fold.23), channel_id=1, source_target_pairs={{0,16},{2,18},{4,20},{6,22},{8,24},{10,26},{12,28},{14,30},{16,0},... | collective-permute-start | bytes 442376 | tf_op jit(solution)/shard_map/ppermute | solution.py:1002
  388.8 0.8 copy-start.14
  392.2 0.6 copy-start.17
  394.4 6.0 %collective-permute-start.26 = (f32[16,1536]{1,0:T(8,128)}, f32[16,1536]{1,0:T(8,128)S(1)}, u32[]{:S(2)}, u32[]{:S(2)}) collective-permute-start(f32[16,1536]{1,0:T(8,128)} %added.6.a_ref), channel_id=1, source_target_pairs={{0,16},{2,18},{4,20},{6,22},{8,24},{10,26},{12,28},{14,30},{16,0},... | collective-permute-start | bytes 294920 | tf_op jit(solution)/shard_map/ppermute | solution.py:1002
  404.9 0.7 copy-start.31
  (2 other events, 1.3 us)
Sparse Core Ops, SparseCore 0:
  17.2 99.9 all-gather.2
  120.1 95.6 reduce-scatter.3
  218.8 92.2 reduce-scatter.5
  315.4 59.1 reduce-scatter.7

commit v5 on v4

--- a/solution.py
+++ b/solution.py
@@ -1256,12 +1256,12 @@
     )
     for low, bit in zip(heights[1:], line[1:]):
         outs = leave(outs, low, bit)
+    g_up = order.mark(order.gate(up_line).astype(F32))
     (g_down,) = finish([downs])
     out_low, out_high = order.mark(*order.gate(out_low, out_high))
     while small_got is not None:
         small_step()
     (g_out,) = finish([outs])
-    g_up = order.gate(up_line).astype(F32)
     g_query, g_key, g_value, g_house = order.gate(plane_rows).astype(F32)
 
     taps = conv_taps.shape[0]

time: 425 us -> 424 us (level)
    unnamed x66 -> x64, local copies, waits for them, and re-layouts: 10.8 us -> 10.2 us
  transfers between devices with their start and end apart: 34 -> 34, of which waited for: 13 -> 13; matrix products, arithmetic and copies ran while one was open for 6% -> 6% of each run, Pallas kernels for 50% -> 51%
where the time goes in v5:
time: 424 us; the launch traced here: 418 us
  Pallas kernels  220 us (52%)
  waiting for transfers between devices  103 us (24%)
  starting transfers between devices  42.4 us (10%)
  local copies, waits for them, and re-layouts  18.5 us (4%)
  between operations  14.5 us (3%)
  matrix products  13.7 us (3%)
  other arithmetic  5.9 us (1%)
    ppermute x24, waiting for transfers between devices, swap(): return lax.ppermute(x, axis, [(i, i ^ 1 << bit) for i in range(size)])  90.1 us
    pallas_call x13, Pallas kernels, fold(): pl.pallas_call(functools.partial(fold_kernel, plan), grid=(height // step...  33.9 us
    pallas_call x4, Pallas kernels, product(): pl.pallas_call(functools.partial(product_kernel, len(lefts), turned, bool...  33.2 us
    pallas_call x1, Pallas kernels, ffn(): pl.pallas_call(ffn_kernel, grid_spec=pltpu.PrefetchScalarGridSpec(num_sca...  25.1 us
    pallas_call x4, Pallas kernels, wgrad(): pl.pallas_call(functools.partial(wgrad_kernel, plan), grid_spec=pltpu.Pre...  24.1 us
    ppermute x24, starting transfers between devices, swap(): return lax.ppermute(x, axis, [(i, i ^ 1 << bit) for i in range(size)])  22 us
    pallas_call x1, Pallas kernels, mixer_backward(): pl.pallas_call(functools.partial(backward_kernel, heads, lengths.shape[1]...  21 us
    pallas_call x1, Pallas kernels, mixer_forward(): pl.pallas_call(functools.partial(forward_kernel, heads, lengths.shape[1])...  17.7 us
  transfers between devices with their start and end apart: 34, of which 13 were waited for; matrix products, arithmetic and copies ran while one was open for 6% of the time, Pallas kernels for 51%

profile of v5, /device:TPU:0, one launch (start us, length us, event | category | flops | bytes accessed | tf_op | source)
XLA Modules:
  0.0 418.1 jit_solution(5719949201708452396)
XLA Ops:
  8.5 4.1 slots_to_send.1
  12.6 4.4 %first_norm.1 = (bf16[512,1536]{1,0:T(8,128)(2,1)}, bf16[1536,512]{1,0:T(8,128)(2,1)}) custom-call(bf16[512,1536]{1,0:T(8,128)(2,1)} %tokens_ref.4, f32[1,1536]{1,0:T(1,128)} %broadcast_in_dim.43.gain_ref), custom_call_target="tpu_custom_call" | custom-call | tf_op jit(solution)/shard_map/first_norm/pallas_call | solution.py:574
  17.1 4.9 %collective-permute-start.2 = (bf16[264,1536]{1,0:T(8,128)(2,1)}, bf16[264,1536]{1,0:T(8,128)(2,1)S(1)}, u32[]{:S(2)}, u32[]{:S(2)}) collective-permute-start(bf16[264,1536]{1,0:T(8,128)(2,1)} %get-tuple-element.121), channel_id=1, source_target_pairs={{0,2},{2,4},{4,6},{6,8},{8,10},{10,12},{12,14},{14,16},{16,18},{18... | collective-permute-start | bytes 2433032 | tf_op jit(solution)/shard_map/ppermute | solution.py:1097
  24.0 2.5 convolution_bitcast_fusion.logit_ref
  26.5 4.1 convolution_convert_fusion.v_ref
  30.6 2.3 convolution_convert_fusion.1.k_ref
  32.9 2.3 convolution_convert_fusion.2.q_ref
  35.2 2.5 fusion.5.house_ref
  37.7 17.7 %mixer_forward.1 = (bf16[512,768]{1,0:T(8,128)(2,1)}, bf16[6,8,256,256]{3,2,1,0:T(8,128)(2,1)}) custom-call(s32[16,3]{1,0:T(8,128)} %copy.37.lengths_ref, s32[1]{0:T(128)} %bitcast.me_ref, f32[6,512]{1,0:T(8,128)} %convolution_bitcast_fusion.logit_ref, f32[4,768]{1,0:T(4,128)} %taps_ref.3, f32[512,768]{1,0:T(8,128)} %fusion.5.house_ref, ...), custom_call_target="tpu_custom_call" | custom-call | tf_op jit(solution)/shard_map/mixer_forward/pallas_call | solution.py:221
  55.4 4.6 %product.4 = (bf16[256,1536]{1,0:T(8,128)(2,1)}, bf16[256,1536]{1,0:T(8,128)(2,1)}) custom-call(bf16[512,768]{1,0:T(8,128)(2,1)} %get-tuple-element.161.refs_0_.refs_1_, bf16[768,1536]{1,0:T(8,128)(2,1)} %out_ref.1), custom_call_target="tpu_custom_call" | custom-call | tf_op jit(solution)/shard_map/product/pallas_call | solution.py:781
  64.6 5.6 %hidden_and_norm.1 = (f32[512,1536]{1,0:T(8,128)}, bf16[512,1536]{1,0:T(8,128)(2,1)}) custom-call(bf16[512,1536]{1,0:T(8,128)(2,1)} %tokens_ref.4, bf16[256,1536]{1,0:T(8,128)(2,1)} %get-tuple-element.129.refs_0_, bf16[256,1536]{1,0:T(8,128)(2,1)} %get-tuple-element.130.refs_1_, bf16[256,1536]{1,0:T(8,128)(2,1)} %copy-done.12, bf16[256,1536]{1,0:T(8,128)(2,1)} %copy-done.13, ...), custom_call_target="tpu_custom_call" | custom-call | tf_op jit(solution)/shard_map/hidden_and_norm/pallas_call | solution.py:619
  70.3 5.4 %collective-permute-done.3.high_ref = bf16[264,1536]{1,0:T(8,128)(2,1)} collective-permute-done((bf16[264,1536]{1,0:T(8,128)(2,1)}, bf16[264,1536]{1,0:T(8,128)(2,1)}, u32[]{:S(2)}, u32[]{:S(2)}) %collective-permute-start.3) | collective-permute-done | bytes 811040 | tf_op jit(solution)/shard_map/ppermute | solution.py:1098
  75.8 6.5 %cotangent_arrived.1.d_final_ref.refs_0_ = bf16[512,1536]{1,0:T(8,128)(2,1)} custom-call(s32[16,3]{1,0:T(8,128)} %copy.37.lengths_ref, s32[48]{0:T(128)} %dealing_ref.5, s32[1]{0:T(128)} %bitcast.me_ref, bf16[768,1536]{1,0:T(8,128)(2,1)} %bitcast.35, bf16[264,1536]{1,0:T(8,128)(2,1)} %copy-done.10, bf16[264,1536]{1,0:T(8,128)(2,1)} %collective-permute-done.3.high_ref), custom_call_target="tpu_custom_call" | custom-call | tf_op jit(solution)/shard_map/cotangent_arrived/pallas_call | solution.py:485
  82.3 25.1 %ffn.1 = (bf16[512,2048]{1,0:T(8,128)(2,1)}, bf16[512,2048]{1,0:T(8,128)(2,1)}, bf16[512,2048]{1,0:T(8,128)(2,1)}, bf16[1536,2048]{1,0:T(8,128)(2,1)}, bf16[1536,2048]{1,0:T(8,128)(2,1)}) custom-call(s32[32]{0:T(128)} %pad_add_fusion.order_ref, bf16[512,1536]{1,0:T(8,128)(2,1)} %get-tuple-element.137.normed_ref, ...), custom_call_target="tpu_custom_call" | custom-call | tf_op jit(solution)/shard_map/ffn/pallas_call | solution.py:974
  108.8 7.1 %wgrad.4 = bf16[768,2048]{1,0:T(8,128)(2,1)} custom-call(s32[8]{0:T(128)} %get-tuple-element.242.order_ref, bf16[512,1536]{1,0:T(8,128)(2,1)} %cotangent_arrived.1.d_final_ref.refs_0_, bf16[512,2048]{1,0:T(8,128)(2,1)} %get-tuple-element.167.refs_1_.refs_0_), custom_call_target="tpu_custom_call" | custom-call | tf_op jit(solution)/shard_map/wgrad/pallas_call | solution.py:888
  117.4 11.4 %product.5 = (bf16[256,1536]{1,0:T(8,128)(2,1)}, bf16[256,1536]{1,0:T(8,128)(2,1)}) custom-call(bf16[512,2048]{1,0:T(8,128)(2,1)} %get-tuple-element.144.refs_0_, bf16[512,2048]{1,0:T(8,128)(2,1)} %get-tuple-element.140.refs_1_, bf16[1536,2048]{1,0:T(8,128)(2,1)} %refs_2_.1, bf16[1536,2048]{1,0:T(8,128)(2,1)} %refs_3_.1), custom_call_target="tpu_custom_call" | custom-call | tf_op jit(solution)/shard_map/product/pallas_call | solution.py:781
  129.9 7.0 %wgrad.5.refs_0_ = bf16[768,2048]{1,0:T(8,128)(2,1)} custom-call(s32[8]{0:T(128)} %get-tuple-element.241.order_ref, bf16[512,1536]{1,0:T(8,128)(2,1)} %cotangent_arrived.1.d_final_ref.refs_0_, bf16[512,2048]{1,0:T(8,128)(2,1)} %get-tuple-element.167.refs_1_.refs_0_), custom_call_target="tpu_custom_call" | custom-call | tf_op jit(solution)/shard_map/wgrad/pallas_call | solution.py:888
  136.9 9.9 %branch_back.1 = (f32[512,1536]{1,0:T(8,128)}, bf16[512,1536]{1,0:T(8,128)(2,1)}, bf16[512,768]{1,0:T(8,128)(2,1)}, f32[1,1536]{1,0:T(1,128)}) custom-call(bf16[256,1536]{1,0:T(8,128)(2,1)} %get-tuple-element.145.upper_ref, bf16[256,1536]{1,0:T(8,128)(2,1)} %get-tuple-element.146.lower_ref, bf16[256,1536]{1,0:T(8,128)(2,1)} %collective-permute-done.4.other_upper_ref, ...), custom_call_target="tpu_custom_call" | custom-call | tf_op jit(solution)/shard_map/branch_back/pallas_call | solution.py:672
  146.8 4.9 %wgrad.6 = bf16[768,768]{1,0:T(8,128)(2,1)} custom-call(s32[8]{0:T(128)} %get-tuple-element.240.order_ref, bf16[512,1536]{1,0:T(8,128)(2,1)} %get-tuple-element.153.refs_0_, bf16[512,768]{1,0:T(8,128)(2,1)} %get-tuple-element.161.refs_0_.refs_1_), custom_call_target="tpu_custom_call" | custom-call | tf_op jit(solution)/shard_map/wgrad/pallas_call | solution.py:888
  151.7 21.0 %mixer_backward.1 = (bf16[4,512,768]{2,1,0:T(8,128)(2,1)}, f32[6,512]{1,0:T(8,128)}, f32[4,768]{1,0:T(4,128)}) custom-call(s32[16,3]{1,0:T(8,128)} %copy.37.lengths_ref, s32[1]{0:T(128)} %bitcast.me_ref, f32[6,512]{1,0:T(8,128)} %convolution_bitcast_fusion.logit_ref, f32[4,768]{1,0:T(4,128)} %taps_ref.3, f32[512,768]{1,0:T(8,128)} %fusion.5.house_ref, ...), custom_call_target="tpu_custom_call" | custom-call | tf_op jit(solution)/shard_map/mixer_backward/pallas_call | solution.py:366
  172.6 4.7 %all-to-all-start = ((bf16[4,512,768]{2,1,0:T(8,128)(2,1)}), bf16[4,512,768]{2,1,0:T(8,128)(2,1)}, u32[]{:S(2)}, u32[]{:S(2)}) async-start(bf16[4,512,768]{2,1,0:T(8,128)(2,1)} %get-tuple-element.164.refs_0_.refs_1_.refs_2_.refs_3_), calls=%async_computation.1 | async-start | bytes 6291456 | tf_op jit(solution)/shard_map/all_to_all | solution.py:1191
  178.3 5.1 %wgrad.7.refs_0_ = bf16[768,768]{1,0:T(8,128)(2,1)} custom-call(s32[8]{0:T(128)} %get-tuple-element.239.order_ref, bf16[512,1536]{1,0:T(8,128)(2,1)} %get-tuple-element.153.refs_0_, bf16[512,768]{1,0:T(8,128)(2,1)} %get-tuple-element.161.refs_0_.refs_1_), custom_call_target="tpu_custom_call" | custom-call | tf_op jit(solution)/shard_map/wgrad/pallas_call | solution.py:888
  183.4 2.0 collective-permute-done.6.refs_1_
  185.4 1.6 copy-done
  187.0 4.0 fold.13
  191.0 10.0 %product.6 = (bf16[256,1536]{1,0:T(8,128)(2,1)}, bf16[256,1536]{1,0:T(8,128)(2,1)}) custom-call(bf16[4,512,768]{2,1,0:T(8,128)(2,1)} %get-tuple-element.164.refs_0_.refs_1_.refs_2_.refs_3_, bf16[4,512,768]{2,1,0:T(8,128)(2,1)} %get-tuple-element.164.refs_0_.refs_1_.refs_2_.refs_3_, bf16[4,512,768]{2,1,0:T(8,128)(2,1)} %get-tuple-element.164.refs_0_.refs_1_.refs_2_.refs_3_, ...), custom_call_target="tpu_custom_call" | custom-call | tf_op jit(solution)/shard_map/product/pallas_call | solution.py:781
  201.5 7.2 %product.7 = (bf16[256,1536]{1,0:T(8,128)(2,1)}, bf16[256,1536]{1,0:T(8,128)(2,1)}) custom-call(bf16[512,2048]{1,0:T(8,128)(2,1)} %get-tuple-element.167.refs_1_.refs_0_, bf16[2048,1536]{1,0:T(8,128)(2,1)} %refs_1_.3), custom_call_target="tpu_custom_call" | custom-call | tf_op jit(solution)/shard_map/product/pallas_call | solution.py:781
  208.7 7.0 %reduce-scatter.4.cloned.1.call-done.refs_0_ = bf16[384,2048]{1,0:T(8,128)(2,1)} async-done(((bf16[1536,2048]{1,0:T(8,128)(2,1)}), bf16[384,2048]{1,0:T(8,128)(2,1)}) %reduce-scatter.4.cloned.1.call-update) | async-done | bytes 1572880 | tf_op jit(solution)/shard_map/reduce_scatter | solution.py:1163
  215.7 1.9 fold.14
  217.6 3.2 collective-permute-start.10
  220.8 2.2 collective-permute-start.15
  223.5 6.7 %input_back.1 = (bf16[512,1536]{1,0:T(8,128)(2,1)}, f32[16,1536]{1,0:T(8,128)}) custom-call(bf16[256,1536]{1,0:T(8,128)(2,1)} %get-tuple-element.165.upper_ref, bf16[256,1536]{1,0:T(8,128)(2,1)} %get-tuple-element.166.lower_ref, bf16[256,1536]{1,0:T(8,128)(2,1)} %collective-permute-done.11.other_upper_ref, ...), custom_call_target="tpu_custom_call" | custom-call | tf_op jit(solution)/shard_map/input_back/pallas_call | solution.py:722
  230.3 6.7 %wgrad_plane.2 = bf16[768,768]{1,0:T(8,128)(2,1)} custom-call(s32[2]{0:T(128)} %get-tuple-element.235.order_ref, bf16[4,1536,512]{2,1,0:T(8,128)(2,1)} %bitcast.33, bf16[4,512,768]{2,1,0:T(8,128)(2,1)} %all-to-all-done.right_ref), custom_call_target="tpu_custom_call" | custom-call | tf_op jit(solution)/shard_map/wgrad_plane/pallas_call | solution.py:924
  237.6 18.3 %collective-permute-done.10.refs_1_ = bf16[192,2048]{1,0:T(8,128)(2,1)} collective-permute-done((bf16[192,2048]{1,0:T(8,128)(2,1)}, bf16[192,2048]{1,0:T(8,128)(2,1)}, u32[]{:S(2)}, u32[]{:S(2)}) %collective-permute-start.10) | collective-permute-done | bytes 786464 | tf_op jit(solution)/shard_map/ppermute | solution.py:1002
  255.9 6.7 %wgrad_plane.3.refs_0_ = bf16[768,768]{1,0:T(8,128)(2,1)} custom-call(s32[2]{0:T(128)} %get-tuple-element.236.order_ref, bf16[4,1536,512]{2,1,0:T(8,128)(2,1)} %bitcast.34, bf16[4,512,768]{2,1,0:T(8,128)(2,1)} %all-to-all-done.right_ref), custom_call_target="tpu_custom_call" | custom-call | tf_op jit(solution)/shard_map/wgrad_plane/pallas_call | solution.py:924
  262.6 2.0 fold.15
  264.6 5.1 %collective-permute-done.9.refs_1_ = bf16[768,768]{1,0:T(8,128)(2,1)} collective-permute-done((bf16[768,768]{1,0:T(8,128)(2,1)}, bf16[768,768]{1,0:T(8,128)(2,1)}, u32[]{:S(2)}, u32[]{:S(2)}) %collective-permute-start.9) | collective-permute-done | bytes 1179680 | tf_op jit(solution)/shard_map/ppermute | solution.py:1002
  269.7 3.4 fold.16
  273.5 2.2 collective-permute-start.20
  275.7 7.9 %rows_dealt.1 = (bf16[768,1536]{1,0:T(8,128)(2,1)}, bf16[256,1536]{1,0:T(8,128)(2,1)}, bf16[256,1536]{1,0:T(8,128)(2,1)}) custom-call(s32[16,3]{1,0:T(8,128)} %copy.37.lengths_ref, s32[48]{0:T(128)} %dealing_ref.5, s32[1]{0:T(128)} %bitcast.me_ref, f32[512,1536]{1,0:T(8,128)} %get-tuple-element.133.hidden_ref, ...), custom_call_target="tpu_custom_call" | custom-call | tf_op jit(solution)/shard_map/rows_dealt/pallas_call | solution.py:543
  284.2 1.6 added.4.a_ref
  287.2 5.6 %collective-permute-done.15.refs_2_ = bf16[384,2048]{1,0:T(8,128)(2,1)S(1)} collective-permute-done((bf16[384,2048]{1,0:T(8,128)(2,1)S(1)}, bf16[384,2048]{1,0:T(8,128)(2,1)S(1)}, u32[]{:S(2)}, u32[]{:S(2)}) %collective-permute-start.15) | collective-permute-done | bytes 1572896 | tf_op jit(solution)/shard_map/ppermute | solution.py:1002
  293.9 2.5 fold.17
  296.4 8.7 %collective-permute-done.21.refs_1_ = bf16[768,768]{1,0:T(8,128)(2,1)} collective-permute-done((bf16[768,768]{1,0:T(8,128)(2,1)}, bf16[768,768]{1,0:T(8,128)(2,1)}, u32[]{:S(2)}, u32[]{:S(2)}) %collective-permute-start.21) | collective-permute-done | bytes 1179680 | tf_op jit(solution)/shard_map/ppermute | solution.py:1002
  305.1 3.4 fold.18
  308.5 2.2 fold.19
  311.4 1.6 added.5.a_ref
  313.0 2.1 fold.20
  315.1 1.7 collective-permute-start.17
  316.8 4.6 %collective-permute-start.13 = (bf16[256,1536]{1,0:T(8,128)(2,1)}, bf16[256,1536]{1,0:T(8,128)(2,1)}, u32[]{:S(2)}, u32[]{:S(2)}) collective-permute-start(bf16[256,1536]{1,0:T(8,128)(2,1)} %get-tuple-element.183), channel_id=1, source_target_pairs={{0,2},{2,4},{4,6},{6,8},{8,10},{10,12},{12,14},{14,16},{16,18},{18... | collective-permute-start | bytes 2359304 | tf_op jit(solution)/shard_map/ppermute | solution.py:1249
  322.9 4.1 collective-permute-start.23
  327.0 14.2 %collective-permute-done.17.refs_3_ = bf16[192,2048]{1,0:T(8,128)(2,1)S(1)} collective-permute-done((bf16[192,2048]{1,0:T(8,128)(2,1)S(1)}, bf16[192,2048]{1,0:T(8,128)(2,1)S(1)}, u32[]{:S(2)}, u32[]{:S(2)}) %collective-permute-start.17) | collective-permute-done | bytes 786464 | tf_op jit(solution)/shard_map/ppermute | solution.py:1002
  342.0 2.3 fold.21
  344.4 23.4 %collective-permute-done.24.refs_2_ = bf16[384,768]{1,0:T(8,128)(2,1)S(1)} collective-permute-done((bf16[384,768]{1,0:T(8,128)(2,1)S(1)}, bf16[384,768]{1,0:T(8,128)(2,1)S(1)}, u32[]{:S(2)}, u32[]{:S(2)}) %collective-permute-start.24) | collective-permute-done | bytes 589856 | tf_op jit(solution)/shard_map/ppermute | solution.py:1002
  368.6 3.5 fold.22
  372.1 11.1 %collective-permute-done.23.refs_3_ = bf16[192,768]{1,0:T(8,128)(2,1)} collective-permute-done((bf16[192,768]{1,0:T(8,128)(2,1)}, bf16[192,768]{1,0:T(8,128)(2,1)}, u32[]{:S(2)}, u32[]{:S(2)}) %collective-permute-start.23) | collective-permute-done | bytes 294944 | tf_op jit(solution)/shard_map/ppermute | solution.py:1002
  383.2 3.5 all-to-all-start.1
  386.7 1.9 fold.23
  388.5 1.9 convert_element_type.18
  391.2 2.7 fold.24
  394.6 1.6 added.6.a_ref
  396.2 2.9 collective-permute-start.26
  399.1 3.2 select_select_fusion
  406.7 2.0 fold.25
  (137 shorter events, 30.4 us)
Async XLA Ops:
  7.2 129.7 %all-gather.3.cloned.1.call-start = ((), (), s32[]{:S(2)}) async-start(), calls=%async_computation.8 | async-start | bytes 7864320 | tf_op jit(solution)/shard_map/all_gather | solution.py:1101
  12.6 10.7 %copy-start.24 = (s32[16,3]{0,1:T(4,128)S(1)}, s32[16,3]{0,1:T(4,128)}, u32[]{:S(2)}) copy-start(s32[16,3]{0,1:T(4,128)} %param.21) | copy-start | bytes 580
  12.6 11.4 %copy-start.21 = (bf16[1536,6]{0,1:T(8,128)(2,1)S(1)}, bf16[1536,6]{0,1:T(8,128)(2,1)}, u32[]{:S(2)}) copy-start(bf16[1536,6]{0,1:T(8,128)(2,1)} %param.28) | copy-start | bytes 55300
  12.6 13.9 %copy-start.6 = (bf16[1536,768]{1,0:T(8,128)(2,1)S(1)}, bf16[1536,768]{1,0:T(8,128)(2,1)}, u32[]{:S(2)}) copy-start(bf16[1536,768]{1,0:T(8,128)(2,1)} %refs_6_.1) | copy-start | bytes 7077892
  17.1 198.6 %reduce-scatter.4.cloned.1.call-start = ((), (), s32[]{:S(2)}) async-start(), calls=%async_computation.5 | async-start | bytes 7864320 | tf_op jit(solution)/shard_map/reduce_scatter | solution.py:1163
  17.1 53.2 %collective-permute-start.2 = (bf16[264,1536]{1,0:T(8,128)(2,1)}, bf16[264,1536]{1,0:T(8,128)(2,1)S(1)}, u32[]{:S(2)}, u32[]{:S(2)}) collective-permute-start(bf16[264,1536]{1,0:T(8,128)(2,1)} %get-tuple-element.121), channel_id=1, source_target_pairs={{0,2},{2,4},{4,6},{6,8},{8,10},{10,12},{12,14},{14,16},{16,18},{18... | collective-permute-start | bytes 2433032 | tf_op jit(solution)/shard_map/ppermute | solution.py:1097
  22.0 53.8 %collective-permute-start.3 = (bf16[264,1536]{1,0:T(8,128)(2,1)}, bf16[264,1536]{1,0:T(8,128)(2,1)}, u32[]{:S(2)}, u32[]{:S(2)}) collective-permute-start(bf16[264,1536]{1,0:T(8,128)(2,1)} %get-tuple-element.122), channel_id=1, source_target_pairs={{2,0},{4,2},{6,4},{8,6},{10,8},{12,10},{14,12},{16,14},{18,16},{20... | collective-permute-start | bytes 2433032 | tf_op jit(solution)/shard_map/ppermute | solution.py:1098
  26.5 4.1 copy-start.5
  26.5 4.1 copy-start.8
  30.6 2.3 copy-start.4
  32.9 2.3 copy-start.3
  55.4 5.2 %copy-start.27 = (s32[4]{0:T(128)S(1)}, s32[4]{0:T(128)}, u32[]{:S(2)}) copy-start(s32[4]{0:T(128)} %constant.37.clone) | copy-start | bytes 52
  55.4 5.3 %copy-start.22 = (f32[1536]{0:T(1024)S(1)}, f32[1536]{0:T(1024)}, u32[]{:S(2)}) copy-start(f32[1536]{0:T(1024)} %param.31) | copy-start | bytes 18436
  60.0 2.5 collective-permute-start
  60.0 3.6 collective-permute-start.1
  62.5 1.1 copy-start.12
  63.6 0.9 copy-start.13
  70.3 5.5 %copy-start.10 = (bf16[264,1536]{1,0:T(8,128)(2,1)}, bf16[264,1536]{1,0:T(8,128)(2,1)S(1)}, u32[]{:S(2)}) copy-start(bf16[264,1536]{1,0:T(8,128)(2,1)S(1)} %collective-permute-done.2.low_ref) | copy-start | bytes 2433028
  107.4 207.7 %reduce-scatter.6.cloned.1.call-start = ((), (), s32[]{:S(2)}) async-start(), calls=%async_computation.6 | async-start | bytes 7864320 | tf_op jit(solution)/shard_map/reduce_scatter | solution.py:1163
  107.5 0.7 copy-start.25
  107.5 0.7 copy-start.26
  115.8 69.6 %collective-permute-start.6 = (bf16[768,2048]{1,0:T(8,128)(2,1)}, bf16[768,2048]{1,0:T(8,128)(2,1)S(1)}, u32[]{:S(2)}, u32[]{:S(2)}) collective-permute-start(bf16[768,2048]{1,0:T(8,128)(2,1)} %wgrad.4), channel_id=1, source_target_pairs={{0,8},{2,10},{4,12},{6,14},{8,0},{10,2},{12,4},{14,6},{16,24},{18,... | collective-permute-start | bytes 9437192 | tf_op jit(solution)/shard_map/ppermute | solution.py:1002
  128.8 8.1 %collective-permute-start.4 = (bf16[256,1536]{1,0:T(8,128)(2,1)}, bf16[256,1536]{1,0:T(8,128)(2,1)}, u32[]{:S(2)}, u32[]{:S(2)}) collective-permute-start(bf16[256,1536]{1,0:T(8,128)(2,1)} %get-tuple-element.145.upper_ref), channel_id=1, source_target_pairs={{0,1},{1,0},{2,3},{3,2},{4,5},{5,4},{6,7},{7,6},{8,9},{9,8},{10,11... | collective-permute-start | bytes 2359304 | tf_op jit(solution)/shard_map/ppermute | solution.py:1002
  128.8 8.1 %collective-permute-start.5 = (bf16[256,1536]{1,0:T(8,128)(2,1)}, bf16[256,1536]{1,0:T(8,128)(2,1)}, u32[]{:S(2)}, u32[]{:S(2)}) collective-permute-start(bf16[256,1536]{1,0:T(8,128)(2,1)} %get-tuple-element.146.lower_ref), channel_id=1, source_target_pairs={{0,1},{1,0},{2,3},{3,2},{4,5},{5,4},{6,7},{7,6},{8,9},{9,8},{10,11... | collective-permute-start | bytes 2359304 | tf_op jit(solution)/shard_map/ppermute | solution.py:1002
  172.6 57.6 %all-to-all-start = ((bf16[4,512,768]{2,1,0:T(8,128)(2,1)}), bf16[4,512,768]{2,1,0:T(8,128)(2,1)}, u32[]{:S(2)}, u32[]{:S(2)}) async-start(bf16[4,512,768]{2,1,0:T(8,128)(2,1)} %get-tuple-element.164.refs_0_.refs_1_.refs_2_.refs_3_), calls=%async_computation.1 | async-start | bytes 6291456 | tf_op jit(solution)/shard_map/all_to_all | solution.py:1191
  177.3 211.3 %reduce-scatter.8.cloned.1.call-start = ((), (), s32[]{:S(2)}) async-start(), calls=%async_computation.7 | async-start | bytes 1966080 | tf_op jit(solution)/shard_map/reduce_scatter | solution.py:1246
  185.4 1.6 copy-start
  201.0 22.5 %collective-permute-start.11 = (bf16[256,1536]{1,0:T(8,128)(2,1)}, bf16[256,1536]{1,0:T(8,128)(2,1)}, u32[]{:S(2)}, u32[]{:S(2)}) collective-permute-start(bf16[256,1536]{1,0:T(8,128)(2,1)} %get-tuple-element.165.upper_ref), channel_id=1, source_target_pairs={{0,1},{1,0},{2,3},{3,2},{4,5},{5,4},{6,7},{7,6},{8,9},{9,8},{10,11... | collective-permute-start | bytes 2359304 | tf_op jit(solution)/shard_map/ppermute | solution.py:1002
  201.0 22.5 %collective-permute-start.12 = (bf16[256,1536]{1,0:T(8,128)(2,1)}, bf16[256,1536]{1,0:T(8,128)(2,1)}, u32[]{:S(2)}, u32[]{:S(2)}) collective-permute-start(bf16[256,1536]{1,0:T(8,128)(2,1)} %get-tuple-element.166.lower_ref), channel_id=1, source_target_pairs={{0,1},{1,0},{2,3},{3,2},{4,5},{5,4},{6,7},{7,6},{8,9},{9,8},{10,11... | collective-permute-start | bytes 2359304 | tf_op jit(solution)/shard_map/ppermute | solution.py:1002
  208.7 12.1 %copy-start.9 = (bf16[384,2048]{1,0:T(8,128)(2,1)S(1)}, bf16[384,2048]{1,0:T(8,128)(2,1)}, u32[]{:S(2)}) copy-start(bf16[384,2048]{1,0:T(8,128)(2,1)} %fold.13) | copy-start | bytes 4718596
  217.6 38.3 %collective-permute-start.10 = (bf16[192,2048]{1,0:T(8,128)(2,1)}, bf16[192,2048]{1,0:T(8,128)(2,1)}, u32[]{:S(2)}, u32[]{:S(2)}) collective-permute-start(bf16[192,2048]{1,0:T(8,128)(2,1)} %fold.14), channel_id=1, source_target_pairs={{0,8},{2,10},{4,12},{6,14},{8,0},{10,2},{12,4},{14,6},{16,24},{18,... | collective-permute-start | bytes 2359304 | tf_op jit(solution)/shard_map/ppermute | solution.py:1002
  220.8 48.9 %collective-permute-start.9 = (bf16[768,768]{1,0:T(8,128)(2,1)}, bf16[768,768]{1,0:T(8,128)(2,1)}, u32[]{:S(2)}, u32[]{:S(2)}) collective-permute-start(bf16[768,768]{1,0:T(8,128)(2,1)} %wgrad.6), channel_id=1, source_target_pairs={{0,2},{2,0},{4,6},{6,4},{8,10},{10,8},{12,14},{14,12},{16,18},{18,... | collective-permute-start | bytes 3538952 | tf_op jit(solution)/shard_map/ppermute | solution.py:1002
  220.8 72.0 %collective-permute-start.15 = (bf16[384,2048]{1,0:T(8,128)(2,1)S(1)}, bf16[384,2048]{1,0:T(8,128)(2,1)S(1)}, u32[]{:S(2)}, u32[]{:S(2)}) collective-permute-start(bf16[384,2048]{1,0:T(8,128)(2,1)S(1)} %copy-done.9), channel_id=1, source_target_pairs={{0,16},{2,18},{4,20},{6,22},{8,24},{10,26},{12,28},{14,30},{16,0},... | collective-permute-start | bytes 4718600 | tf_op jit(solution)/shard_map/ppermute | solution.py:1002
  236.9 68.2 %collective-permute-start.21 = (bf16[768,768]{1,0:T(8,128)(2,1)}, bf16[768,768]{1,0:T(8,128)(2,1)}, u32[]{:S(2)}, u32[]{:S(2)}) collective-permute-start(bf16[768,768]{1,0:T(8,128)(2,1)} %wgrad_plane.2), channel_id=1, source_target_pairs={{0,8},{2,10},{4,12},{6,14},{8,0},{10,2},{12,4},{14,6},{16,24},{18,... | collective-permute-start | bytes 3538952 | tf_op jit(solution)/shard_map/ppermute | solution.py:1002
  237.6 35.9 %collective-permute-start.7 = (bf16[256,1536]{1,0:T(8,128)(2,1)}, bf16[256,1536]{1,0:T(8,128)(2,1)}, u32[]{:S(2)}, u32[]{:S(2)}) collective-permute-start(bf16[256,1536]{1,0:T(8,128)(2,1)} %get-tuple-element.168.upper_ref), channel_id=1, source_target_pairs={{0,1},{1,0},{2,3},{3,2},{4,5},{5,4},{6,7},{7,6},{8,9},{9,8},{10,11... | collective-permute-start | bytes 2359304 | tf_op jit(solution)/shard_map/ppermute | solution.py:1002
  255.9 19.8 %collective-permute-start.8 = (bf16[256,1536]{1,0:T(8,128)(2,1)}, bf16[256,1536]{1,0:T(8,128)(2,1)}, u32[]{:S(2)}, u32[]{:S(2)}) collective-permute-start(bf16[256,1536]{1,0:T(8,128)(2,1)} %get-tuple-element.169.lower_ref), channel_id=1, source_target_pairs={{0,1},{1,0},{2,3},{3,2},{4,5},{5,4},{6,7},{7,6},{8,9},{9,8},{10,11... | collective-permute-start | bytes 2359304 | tf_op jit(solution)/shard_map/ppermute | solution.py:1002
  264.6 8.9 %copy-start.30 = (bf16[96,2048]{1,0:T(8,128)(2,1)S(1)}, bf16[96,2048]{1,0:T(8,128)(2,1)}, u32[]{:S(2)}) copy-start(bf16[96,2048]{1,0:T(8,128)(2,1)} %fold.15) | copy-start | bytes 1179652
  264.6 11.1 %copy-start.16 = (f32[16,1536]{1,0:T(8,128)S(1)}, f32[16,1536]{1,0:T(8,128)}, u32[]{:S(2)}) copy-start(f32[16,1536]{1,0:T(8,128)} %get-tuple-element.174.a_ref) | copy-start | bytes 294916
  273.1 39.9 %collective-permute-start.18 = (bf16[384,768]{1,0:T(8,128)(2,1)}, bf16[384,768]{1,0:T(8,128)(2,1)}, u32[]{:S(2)}, u32[]{:S(2)}) collective-permute-start(bf16[384,768]{1,0:T(8,128)(2,1)} %fold.16), channel_id=1, source_target_pairs={{0,4},{2,6},{4,0},{6,2},{8,12},{10,14},{12,8},{14,10},{16,20},{18,... | collective-permute-start | bytes 1769480 | tf_op jit(solution)/shard_map/ppermute | solution.py:1002
  273.5 35.0 %collective-permute-start.20 = (bf16[96,2048]{1,0:T(8,128)(2,1)S(1)}, bf16[96,2048]{1,0:T(8,128)(2,1)}, u32[]{:S(2)}, u32[]{:S(2)}) collective-permute-start(bf16[96,2048]{1,0:T(8,128)(2,1)S(1)} %copy-done.30), channel_id=1, source_target_pairs={{0,16},{2,18},{4,20},{6,22},{8,24},{10,26},{12,28},{14,30},{16,0},... | collective-permute-start | bytes 1179656 | tf_op jit(solution)/shard_map/ppermute | solution.py:1002
  275.7 7.9 %collective-permute-start.16 = (f32[16,1536]{1,0:T(8,128)S(1)}, f32[16,1536]{1,0:T(8,128)S(1)}, u32[]{:S(2)}, u32[]{:S(2)}) collective-permute-start(f32[16,1536]{1,0:T(8,128)S(1)} %copy-done.16), channel_id=1, source_target_pairs={{0,2},{2,0},{4,6},{6,4},{8,10},{10,8},{12,14},{14,12},{16,18},{18,... | collective-permute-start | bytes 294920 | tf_op jit(solution)/shard_map/ppermute | solution.py:1002
  283.6 0.6 copy-start.19
  285.8 24.9 %collective-permute-start.19 = (f32[16,1536]{1,0:T(8,128)}, f32[16,1536]{1,0:T(8,128)S(1)}, u32[]{:S(2)}, u32[]{:S(2)}) collective-permute-start(f32[16,1536]{1,0:T(8,128)} %added.4.a_ref), channel_id=1, source_target_pairs={{0,4},{2,6},{4,0},{6,2},{8,12},{10,14},{12,8},{14,10},{16,20},{18,... | collective-permute-start | bytes 294920 | tf_op jit(solution)/shard_map/ppermute | solution.py:1002
  292.8 1.1 copy-start.1
  310.8 0.6 copy-start.18
  313.0 2.1 copy-start.11
  313.0 3.8 copy-start.28
  313.0 9.8 %copy-start.23 = (s32[48]{0:T(128)S(1)}, s32[48]{0:T(128)}, u32[]{:S(2)}) copy-start(s32[48]{0:T(128)} %dealing_ref.5) | copy-start | bytes 580
  315.1 26.1 %collective-permute-start.17 = (bf16[192,2048]{1,0:T(8,128)(2,1)S(1)}, bf16[192,2048]{1,0:T(8,128)(2,1)S(1)}, u32[]{:S(2)}, u32[]{:S(2)}) collective-permute-start(bf16[192,2048]{1,0:T(8,128)(2,1)S(1)} %copy-done.11), channel_id=1, source_target_pairs={{0,2},{2,0},{4,6},{6,4},{8,10},{10,8},{12,14},{14,12},{16,18},{18,... | collective-permute-start | bytes 2359304 | tf_op jit(solution)/shard_map/ppermute | solution.py:1002
  316.8 50.9 %collective-permute-start.24 = (bf16[384,768]{1,0:T(8,128)(2,1)S(1)}, bf16[384,768]{1,0:T(8,128)(2,1)S(1)}, u32[]{:S(2)}, u32[]{:S(2)}) collective-permute-start(bf16[384,768]{1,0:T(8,128)(2,1)S(1)} %copy-done.28), channel_id=1, source_target_pairs={{0,16},{2,18},{4,20},{6,22},{8,24},{10,26},{12,28},{14,30},{16,0},... | collective-permute-start | bytes 1769480 | tf_op jit(solution)/shard_map/ppermute | solution.py:1002
  316.8 77.1 %collective-permute-start.13 = (bf16[256,1536]{1,0:T(8,128)(2,1)}, bf16[256,1536]{1,0:T(8,128)(2,1)}, u32[]{:S(2)}, u32[]{:S(2)}) collective-permute-start(bf16[256,1536]{1,0:T(8,128)(2,1)} %get-tuple-element.183), channel_id=1, source_target_pairs={{0,2},{2,4},{4,6},{6,8},{8,10},{10,12},{12,14},{14,16},{16,18},{18... | collective-permute-start | bytes 2359304 | tf_op jit(solution)/shard_map/ppermute | solution.py:1249
  321.5 72.4 %collective-permute-start.14 = (bf16[256,1536]{1,0:T(8,128)(2,1)}, bf16[256,1536]{1,0:T(8,128)(2,1)}, u32[]{:S(2)}, u32[]{:S(2)}) collective-permute-start(bf16[256,1536]{1,0:T(8,128)(2,1)} %get-tuple-element.184), channel_id=1, source_target_pairs={{2,0},{4,2},{6,4},{8,6},{10,8},{12,10},{14,12},{16,14},{18,16},{20... | collective-permute-start | bytes 2359304 | tf_op jit(solution)/shard_map/ppermute | solution.py:1250
  322.9 44.9 %copy-start.15 = (f32[16,1536]{1,0:T(8,128)S(1)}, f32[16,1536]{1,0:T(8,128)}, u32[]{:S(2)}) copy-start(f32[16,1536]{1,0:T(8,128)} %added.5.a_ref) | copy-start | bytes 294916
  322.9 60.3 %collective-permute-start.23 = (bf16[192,768]{1,0:T(8,128)(2,1)}, bf16[192,768]{1,0:T(8,128)(2,1)}, u32[]{:S(2)}, u32[]{:S(2)}) collective-permute-start(bf16[192,768]{1,0:T(8,128)(2,1)} %fold.20), channel_id=1, source_target_pairs={{0,8},{2,10},{4,12},{6,14},{8,0},{10,2},{12,4},{14,6},{16,24},{18,... | collective-permute-start | bytes 884744 | tf_op jit(solution)/shard_map/ppermute | solution.py:1002
  341.2 0.9 copy-start.2
  344.4 46.1 %collective-permute-start.22 = (bf16[96,2048]{1,0:T(8,128)(2,1)}, bf16[96,2048]{1,0:T(8,128)(2,1)S(1)}, u32[]{:S(2)}, u32[]{:S(2)}) collective-permute-start(bf16[96,2048]{1,0:T(8,128)(2,1)} %fold.21), channel_id=1, source_target_pairs={{0,4},{2,6},{4,0},{6,2},{8,12},{10,14},{12,8},{14,10},{16,20},{18,... | collective-permute-start | bytes 1179656 | tf_op jit(solution)/shard_map/ppermute | solution.py:1002
  367.7 0.8 copy-start.29
  367.7 26.2 %collective-permute-start.25 = (f32[16,1536]{1,0:T(8,128)S(1)}, f32[16,1536]{1,0:T(8,128)S(1)}, u32[]{:S(2)}, u32[]{:S(2)}) collective-permute-start(f32[16,1536]{1,0:T(8,128)S(1)} %copy-done.15), channel_id=1, source_target_pairs={{0,8},{2,10},{4,12},{6,14},{8,0},{10,2},{12,4},{14,6},{16,24},{18,... | collective-permute-start | bytes 294920 | tf_op jit(solution)/shard_map/ppermute | solution.py:1002
  383.2 25.6 %all-to-all-start.1 = ((bf16[4,96,768]{2,1,0:T(8,128)(2,1)}), bf16[4,96,768]{2,1,0:T(8,128)(2,1)S(1)}, u32[]{:S(2)}, u32[]{:S(2)}) async-start(bf16[4,96,768]{2,1,0:T(8,128)(2,1)} %bitcast.38), calls=%async_computation.4 | async-start | bytes 1179648 | tf_op jit(solution)/shard_map/all_to_all | solution.py:1254
  388.5 18.2 %collective-permute-start.27 = (bf16[96,768]{1,0:T(8,128)(2,1)}, bf16[96,768]{1,0:T(8,128)(2,1)}, u32[]{:S(2)}, u32[]{:S(2)}) collective-permute-start(bf16[96,768]{1,0:T(8,128)(2,1)} %fold.23), channel_id=1, source_target_pairs={{0,16},{2,18},{4,20},{6,22},{8,24},{10,26},{12,28},{14,30},{16,0},... | collective-permute-start | bytes 442376 | tf_op jit(solution)/shard_map/ppermute | solution.py:1002
  390.5 8.6 %copy-start.7 = (bf16[768,1536]{1,0:T(8,128)(2,1)S(1)}, bf16[768,1536]{1,0:T(8,128)(2,1)}, u32[]{:S(2)}) copy-start(bf16[768,1536]{1,0:T(8,128)(2,1)} %get-tuple-element.185) | copy-start | bytes 7077892
  390.5 0.8 copy-start.14
  393.9 0.6 copy-start.17
  396.2 6.1 %collective-permute-start.26 = (f32[16,1536]{1,0:T(8,128)}, f32[16,1536]{1,0:T(8,128)S(1)}, u32[]{:S(2)}, u32[]{:S(2)}) collective-permute-start(f32[16,1536]{1,0:T(8,128)} %added.6.a_ref), channel_id=1, source_target_pairs={{0,16},{2,18},{4,20},{6,22},{8,24},{10,26},{12,28},{14,30},{16,0},... | collective-permute-start | bytes 294920 | tf_op jit(solution)/shard_map/ppermute | solution.py:1002
  (1 other events, 0.6 us)
Sparse Core Ops, SparseCore 0:
  17.2 99.9 all-gather.2
  120.1 95.5 reduce-scatter.3
  218.7 92.3 reduce-scatter.5
  315.2 59.0 reduce-scatter.7
